TPU v7x, 128 devices: a whole 4x4x4 slice. The times are simulated.
128 devices in a mesh: atom: 8 (over x, core), aux: 16 (over z, y).
Axes of the slice: x: 4, y: 4, z: 4, core: 2. Of those that a mesh axis runs over, the one named last changes fastest.
Arguments:
- three_index: bfloat16 [256, 16, 4, 128, 128], P('aux', 'atom'), may hold values from -0.09375 to 0.09375
- density: bfloat16 [2048, 2048], P(('atom', 'aux')), may hold values from -6 to 6
- pair_blocks: int32 [16, 4], replicated, may hold values from 0 to 15, as said below
- basis_counts: int32 [16], replicated, may hold values from 1 to 128, 1536 in all
Outputs:
- exchange_matrix: float32 [2048, 2048], P(('atom', 'aux'))
Inputs may be any that keep to these rules, and one draw needn't show every extreme that they name: `pair_blocks`: each row names 4 different basis blocks, the first being the row's own block.
All inputs are finite; a program needn't handle non-finite values.
Results may differ from a plain program's by a relative error of at most 0.0029.
Values may be sent and summed in bfloat16 or wider, within the bound.
No kernel may reach another device: no remote copies, remote signals or barrier semaphores. Data moves between devices by JAX's collectives and lax.ppermute only.
A program may use at most 192 MiB of HBM per device.

v0:
```python
import math

import jax
import jax.numpy as jnp
from jax import lax
from jax.sharding import PartitionSpec as P


def split_up(value, dim, size):
    lengths = value.shape
    parts = value.reshape(*lengths[:dim], size, lengths[dim] // size, *lengths[dim + 1 :])
    return jnp.moveaxis(parts, dim, 0)


def sent_and_summed(value, axis, dim):
    size = lax.axis_size(axis)
    parts = lax.all_to_all(split_up(value, dim, size), axis, 0, 0, tiled=True)
    return jnp.sum(parts, axis=0)


def per_device(three_index, density, pair_blocks, basis_counts):
    whole_density = lax.all_gather(density, ("atom", "aux"), axis=0, tiled=True)
    block_size = three_index.shape[-1]
    total_basis = whole_density.shape[1]
    total_blocks = total_basis // block_size
    own_blocks = three_index.shape[1]
    aux_here = three_index.shape[0]
    first_block = lax.axis_index("atom") * own_blocks
    live_slots = (jnp.arange(block_size)[None, :] < basis_counts[:, None]).astype(jnp.bfloat16)

    def masked(portion, offset):
        block_count = portion.shape[1]
        row_live = lax.dynamic_slice_in_dim(live_slots, offset, block_count, 0)
        partners = lax.dynamic_slice_in_dim(pair_blocks, offset, block_count, 0)
        col_live = live_slots[partners]
        cleaned = portion * row_live[None, :, None, :, None] * col_live[None, :, :, None, :]
        return (cleaned, partners)

    own_tensor, own_partners = masked(three_index, first_block)
    near_density = whole_density.reshape(total_blocks, block_size, total_basis)[own_partners]
    group_size = math.gcd(aux_here, 8)
    grouped = own_tensor.reshape((aux_here // group_size, group_size) + own_tensor.shape[1:])

    def contract(portion):
        product = jnp.einsum(
            "pmjab,mjbs->pmas", portion, near_density, preferred_element_type=jnp.float32
        )
        return product.astype(jnp.bfloat16)

    halfway = lax.map(contract, grouped).reshape(aux_here, own_blocks * block_size, total_basis)
    halfway_cols = halfway.reshape(aux_here, own_blocks * block_size, total_blocks, block_size)
    portion = lax.all_gather(three_index, "atom", axis=1, tiled=True)
    block_count = portion.shape[1]
    cleaned, partners = masked(portion, jnp.int32(0))
    contrib = jnp.einsum(
        "pmbc,pbjcn->mbjn", halfway_cols, cleaned, preferred_element_type=jnp.float32
    )
    placement = (partners.reshape(-1)[:, None] == jnp.arange(total_blocks)[None, :]).astype(
        jnp.float32
    )
    spread_out = jnp.einsum(
        "mqn,qk->mkn",
        contrib.reshape(contrib.shape[0], -1, block_size),
        placement,
        precision=lax.Precision.HIGHEST,
    )
    row_sums = spread_out.reshape(contrib.shape[0], total_basis)
    return sent_and_summed(row_sums, "aux", 0)


def solution(mesh):
    in_specs = (P("aux", "atom", None, None, None), P(("atom", "aux"), None), P(), P())
    out_specs = P(("atom", "aux"), None)
    return jax.shard_map(
        per_device, mesh=mesh, in_specs=in_specs, out_specs=out_specs, check_vma=False
    )
```

profile of v0, /device:TPU:0, one launch (start us, length us, event | category | flops | bytes accessed | tf_op | source)
XLA Modules:
  0.0 328.8 jit_solution(8203879094852832548)
XLA Ops:
  6.5 0.0 all-gather.5.cloned.1.call-start
  6.5 0.7 all-gather.5.cloned.1.call-update
  7.3 0.0 all-gather.3.cloned.1.call-start
  7.3 0.7 all-gather.3.cloned.1.call-update
  8.0 0.8 copy.10
  8.8 0.8 compare_select_fusion
  9.5 0.1 copy.12
  9.6 0.1 reshape.48
  9.7 0.7 compare_select_fusion.1
  10.4 0.1 copy.11
  10.5 0.1 reshape.40
  10.6 0.7 fusion.7
  11.3 0.6 gather_fusion.1
  11.9 0.6 gather_fusion
  12.5 0.1 eq.15
  12.6 4.5 %multiply_multiply_fusion.1 = bf16[16,2,4,128,128]{4,3,2,1,0:T(8,128)(2,1)} fusion(bf16[16,2,4,128,128]{4,3,2,1,0:T(8,128)(2,1)} %param.6, bf16[2,4,128]{2,1,0:T(4,128)(2,1)S(1)} %bitcast.57, bf16[2,128]{1,0:T(2,128)(2,1)S(1)} %constant_dynamic-slice_fusion.1), kind=kLoop, calls=%fused_computation.14 | loop fusion | flops 4194304 | bytes 8391168 | tf_op jit(solution)/shard_map/mul | solution.py:36
  17.2 66.0 %all-gather.5.cloned.1.call-done = bf16[2048,2048]{1,0:T(8,128)(2,1)} async-done(((bf16[16,2048]{1,0:T(8,128)(2,1)}), bf16[2048,2048]{1,0:T(8,128)(2,1)}) %all-gather.5.cloned.1.call-update) | async-done | bytes 8388624 | tf_op jit(solution)/shard_map/all_gather | solution.py:22
  83.2 6.1 %gather_fusion.2 = bf16[8,128,2048]{2,1,0:T(8,128)(2,1)} fusion(bf16[16,128,2048]{2,1,0:T(8,128)(2,1)} %bitcast.55, s32[1024]{0:T(1024)S(1)} %pad_clamp_fusion), kind=kCustom, calls=%fused_computation.2 | custom fusion | bytes 8388640 | tf_op jit(solution)/shard_map/gather | solution.py:40
  89.3 37.6 %while.10 = (s32[]{:T(128)}, bf16[2,8,2,128,2048]{4,3,2,1,0:T(8,128)(2,1)}, bf16[2,8,2,4,128,128]{5,4,3,2,1,0:T(8,128)(2,1)}, bf16[2,4,128,2048]{3,2,1,0:T(8,128)(2,1)}, s32[]{:T(128)}) while((s32[]{:T(128)}, bf16[2,8,2,128,2048]{4,3,2,1,0:T(8,128)(2,1)}, bf16[2,8,2,4,128,128]{5,4,3,2,1,0:T(8,128)(2,1)}, bf16[2,4,128,2048]{3,2,1,0:T(8,128)(2,1)}, ...), condition=%wide.region_1.2_spmd, body=%wide.region_0.1_spmd.sunk | while | flops 4299161600 | bytes 31458364 | solution.py:50
  89.3 9.7 %fusion.13 = bf16[1,8,2,128,2048]{4,3,1,2,0:T(8,128)(2,1)} fusion(bf16[2,4,128,2048]{3,2,1,0:T(8,128)(2,1)} %get-tuple-element.78, bf16[2,8,2,4,128,128]{5,4,3,2,1,0:T(8,128)(2,1)} %get-tuple-element.77, s32[]{:T(128)} %get-tuple-element.70), kind=kOutput, calls=%fused_computation.4.clone.1 | convolution fusion | flops 4299161600 | bytes 14680576 | tf_op jit(solution)/shard_map/while/body/eval_jaxpr/pmjab,mjbs->pmas/dot_general | solution.py:45
  99.0 10.4 %copy_dynamic-update-slice_fusion.2 = bf16[2,8,2,128,2048]{4,3,2,1,0:T(8,128)(2,1)} fusion(bf16[2,8,2,128,2048]{4,3,2,1,0:T(8,128)(2,1)} %get-tuple-element.71, s32[]{:T(128)} %get-tuple-element.70, bf16[1,8,2,128,2048]{4,3,1,2,0:T(8,128)(2,1)} %fusion.13), kind=kLoop, calls=%fused_computation.5.clone.1 | loop fusion | bytes 16777728 | tf_op jit(solution)/shard_map/while/body/jit(dynamic_update_index_in_dim)/dynamic_update_slice | solution.py:50
  109.4 9.2 %fusion.13 = bf16[1,8,2,128,2048]{4,3,1,2,0:T(8,128)(2,1)} fusion(bf16[2,4,128,2048]{3,2,1,0:T(8,128)(2,1)} %get-tuple-element.78, bf16[2,8,2,4,128,128]{5,4,3,2,1,0:T(8,128)(2,1)} %get-tuple-element.77, s32[]{:T(128)} %get-tuple-element.70), kind=kOutput, calls=%fused_computation.4.clone.1 | convolution fusion | flops 4299161600 | bytes 14680576 | tf_op jit(solution)/shard_map/while/body/eval_jaxpr/pmjab,mjbs->pmas/dot_general | solution.py:45
  118.7 8.2 %copy_dynamic-update-slice_fusion.2 = bf16[2,8,2,128,2048]{4,3,2,1,0:T(8,128)(2,1)} fusion(bf16[2,8,2,128,2048]{4,3,2,1,0:T(8,128)(2,1)} %get-tuple-element.71, s32[]{:T(128)} %get-tuple-element.70, bf16[1,8,2,128,2048]{4,3,1,2,0:T(8,128)(2,1)} %fusion.13), kind=kLoop, calls=%fused_computation.5.clone.1 | loop fusion | bytes 16777728 | tf_op jit(solution)/shard_map/while/body/jit(dynamic_update_index_in_dim)/dynamic_update_slice | solution.py:50
  126.9 9.9 %copy.29 = bf16[512,8,16,128]{3,2,1,0:T(8,128)(2,1)S(1)} copy(bf16[512,8,16,128]{3,1,2,0:T(8,128)(2,1)} %bitcast.52) | data formatting | bytes 33554432
  136.8 7.4 %bitcast_bitcast_fusion = bf16[16,256,16,128,1]{3,2,1,0,4:T(8,128)(2,1)} fusion(bf16[16,256,16,128]{3,2,1,0:T(8,128)(2,1)S(1)} %bitcast.50), kind=kLoop, calls=%fused_computation.12 | loop fusion | bytes 33554432 | tf_op jit(solution)/shard_map/reshape;reshape | solution.py:51
  144.3 94.0 %all-gather.3.cloned.1.call-done = bf16[16,16,4,128,128]{4,3,2,1,0:T(8,128)(2,1)} async-done(((bf16[16,2,4,128,128]{4,3,2,1,0:T(8,128)(2,1)}), bf16[16,16,4,128,128]{4,3,2,1,0:T(8,128)(2,1)}) %all-gather.3.cloned.1.call-update) | async-done | bytes 33554448 | tf_op jit(solution)/shard_map/all_gather | solution.py:52
  238.2 24.2 %fusion.2 = f32[16,4,128,256,1]{3,2,0,1,4:T(8,128)} fusion(bf16[16,256,16,128,1]{3,2,1,0,4:T(8,128)(2,1)} %bitcast_bitcast_fusion, bf16[16,16,4,128,128]{4,3,2,1,0:T(8,128)(2,1)} %all-gather.3.cloned.1.call-done, bf16[16,4,128]{2,1,0:T(4,128)(2,1)S(1)} %bitcast.56, bf16[16,128]{1,0:T(8,128)(2,1)S(1)} %fusion.7), kind=kOutput, calls=%fused_computation.9 | convolution fusion | flops 8623489024 | bytes 58740736 | tf_op jit(solution)/shard_map/pmbc,pbjcn->mbjn/dot_general | solution.py:55
  262.4 7.6 %copy.22 = f32[16,4,128,256,1]{3,2,1,0,4:T(8,128)} copy(f32[16,4,128,256,1]{3,2,0,1,4:T(8,128)} %fusion.2) | data formatting | bytes 16777216 | tf_op jit(solution)/shard_map/pmbc,pbjcn->mbjn/dot_general | solution.py:55
  270.0 8.7 %copy.17 = f32[256,64,128]{2,1,0:T(8,128)} copy(f32[256,64,128]{0,2,1:T(8,128)} %bitcast.51) | data formatting | bytes 16777216 | tf_op jit(solution)/shard_map/reshape | solution.py:63
  278.8 5.1 %convolution_bitcast_fusion = f32[256,16,128]{2,1,0:T(8,128)S(1)} fusion(f32[256,64,128]{2,1,0:T(8,128)} %copy.17, s32[64]{0:T(128)S(1)} %eq.15), kind=kOutput, calls=%fused_computation.15 | convolution fusion | flops 402654208 | bytes 10486016 | tf_op jit(solution)/shard_map/mqn,qk->mkn/dot_general | solution.py:61
  283.9 1.5 reshape_reshape.7
  285.4 35.8 %all_to_all.5 = f32[16,16,2048]{2,1,0:T(8,128)S(1)} all-to-all(f32[16,16,2048]{2,1,0:T(8,128)} %reshape_reshape.7), channel_id=1, replica_groups=mesh['atom'=8,'aux'=16] {'aux'}, dimensions={0} | all-to-all | bytes 4194304 | tf_op jit(solution)/shard_map/all_to_all | solution.py:17
  321.2 0.8 reduce_sum.9
  (4 shorter events, 0.0 us)
Async XLA Ops:
  6.5 76.6 %all-gather.5.cloned.1.call-start = ((), (), s32[]{:S(2)}) async-start(), calls=%async_computation.2 | async-start | bytes 8454144 | tf_op jit(solution)/shard_map/all_gather | solution.py:22
  7.3 231.0 %all-gather.3.cloned.1.call-start = ((), (), s32[]{:S(2)}) async-start(), calls=%async_computation.1 | async-start | bytes 37748736 | tf_op jit(solution)/shard_map/all_gather | solution.py:52
Sparse Core Ops, SparseCore 0:
  10.5 72.6 all-gather.4
  84.8 153.3 all-gather.2
where the time goes:
time: 329 us
  waiting for transfers between devices  161 us (49%)
  local copies, waits for them, and re-layouts  62.4 us (19%)
  matrix products  48.3 us (15%)
  blocking collectives  35.8 us (11%)
  between operations  13.5 us (4%)
  other arithmetic  7.45 us (2%)
    all_gather x1, waiting for transfers between devices, per_device(): portion = lax.all_gather(three_index, 'atom', axis=1, tiled=True)  94 us
    all_gather x1, waiting for transfers between devices, per_device(): whole_density = lax.all_gather(density, ('atom', 'aux'), axis=0, tiled=True)  66 us
    all_to_all x1, blocking collectives, sent_and_summed(): parts = lax.all_to_all(split_up(value, dim, size), axis, 0, 0, tiled=True)  35.8 us
    dot_general x1, matrix products, per_device(): jnp.einsum('pmbc,pbjcn->mbjn', halfway_cols, cleaned, preferred_element_t...  24.2 us
    dot_general x2, matrix products, contract(): jnp.einsum('pmjab,mjbs->pmas', portion, near_density, preferred_element_t...  18.9 us
    dynamic_update_slice x2, local copies, waits for them, and re-layouts, per_device(): lax.map(contract, grouped)  18.7 us
    unnamed x2, local copies, waits for them, and re-layouts  10.7 us
    reshape x1, local copies, waits for them, and re-layouts, per_device(): contrib.reshape(contrib.shape[0], -1, block_size)  8.72 us
  transfers between devices with their start and end apart: 2, of which 2 were waited for; matrix products, arithmetic and copies ran while one was open for 21% of the time, Pallas kernels for 0%

commit v1 on v0

v1 whole, which is shorter than its diff:
```python
import functools

import jax
import jax.numpy as jnp
from jax import lax
from jax.experimental import pallas as pl
from jax.experimental.pallas import tpu as pltpu
from jax.sharding import Mesh, PartitionSpec as P

CORES = 2
SIDE = 4


def exchange_kernel(groups, place, pairs, own_hbm, other_hbm, density_hbm, out_ref,
                    own, other, density, halfway, total, sems):
    sources, aux, per_source, neigh, size, _ = own.shape
    tiles, basis, width = density.shape
    step = pl.program_id(0)
    core = place[0]

    copies = [pltpu.make_async_copy(own_hbm, own, sems.at[0])]
    for t in range(tiles):
        copies.append(
            pltpu.make_async_copy(
                density_hbm.at[:, pl.ds(t * width, width)], density.at[t], sems.at[1 + t]
            )
        )
    copies.append(pltpu.make_async_copy(other_hbm, other, sems.at[1 + tiles]))

    @pl.when(step == 0)
    def _():
        for copy in copies:
            copy.start()
        copies[0].wait()

    blocks_here = halfway.shape[1] // size
    per_group = blocks_here // per_source

    for t in range(tiles):
        @pl.when(step == 0)
        def _():
            copies[1 + t].wait()

        @pl.loop(0, blocks_here)
        def _(b):
            source = step * per_group + b // per_source
            mi = b % per_source
            block = (source * CORES + core) * per_source + mi
            rows = jnp.concatenate(
                [
                    jnp.concatenate([own[source, p, mi, j] for j in range(neigh)], axis=1)
                    for p in range(aux)
                ],
                axis=0,
            )
            near = jnp.concatenate(
                [
                    density[t, pl.ds(pl.multiple_of(pairs[block * neigh + j] * size, size), size), :]
                    for j in range(neigh)
                ],
                axis=0,
            )
            product = jnp.dot(rows, near, preferred_element_type=jnp.float32).astype(jnp.bfloat16)
            at = pl.ds(pl.multiple_of(b * size, size), size)
            for k in range(width // size):
                for p in range(aux):
                    halfway[t * (width // size) + k, at, p * size : (p + 1) * size] = product[
                        p * size : (p + 1) * size, k * size : (k + 1) * size
                    ]

    @pl.when(step == 0)
    def _():
        copies[-1].wait()

    total[...] = jnp.zeros_like(total)

    def add_in(tensor, which):
        @pl.loop(0, sources * per_source)
        def _(b):
            source = b // per_source
            mi = b % per_source
            block = (source * CORES + which) * per_source + mi
            rows = jnp.concatenate(
                [
                    jnp.concatenate([tensor[source, p, mi, j] for j in range(neigh)], axis=1)
                    for p in range(aux)
                ],
                axis=0,
            )
            product = jnp.dot(halfway[block], rows, preferred_element_type=jnp.float32)
            for j in range(neigh):
                total[pairs[block * neigh + j]] += product[:, j * size : (j + 1) * size]

    add_in(own, core)
    add_in(other, 1 - core)
    for n in range(basis // size):
        out_ref[:, n * size : (n + 1) * size] = total[n].astype(out_ref.dtype)


def exchange_rows(place, pairs, own, other, density, groups=2, tiles=4):
    sources, aux, per_source, neigh, size, _ = own.shape
    basis = density.shape[0]
    rows = sources * per_source * size
    return pl.pallas_call(
        functools.partial(exchange_kernel, groups),
        out_shape=jax.ShapeDtypeStruct((rows, basis), jnp.bfloat16),
        grid_spec=pltpu.PrefetchScalarGridSpec(
            num_scalar_prefetch=2,
            grid=(groups,),
            in_specs=[pl.BlockSpec(memory_space=pl.ANY)] * 3,
            out_specs=pl.BlockSpec((rows // groups, basis), lambda g, *_: (g, 0)),
            scratch_shapes=[
                pltpu.VMEM(own.shape, jnp.bfloat16),
                pltpu.VMEM(own.shape, jnp.bfloat16),
                pltpu.VMEM((tiles, basis, basis // tiles), jnp.bfloat16),
                pltpu.VMEM((basis // size, rows // groups, aux * size), jnp.bfloat16),
                pltpu.VMEM((basis // size, rows // groups, size), jnp.float32),
                pltpu.SemaphoreType.DMA((tiles + 2,)),
            ],
        ),
        compiler_params=pltpu.CompilerParams(
            vmem_limit_bytes=56 << 20, dimension_semantics=("arbitrary",)
        ),
        cost_estimate=pl.CostEstimate(
            flops=4 * rows * aux * neigh * size * basis,
            bytes_accessed=4 * own.size + 2 * density.size + 2 * rows * basis,
            transcendentals=0,
        ),
    )(place, pairs, own, other, density)


def per_device(three_index, density, pair_blocks, basis_counts):
    aux_here, own_blocks, neigh, size, _ = three_index.shape
    rows_here, basis = density.shape
    blocks = basis // size
    x, core = lax.axis_index("x"), lax.axis_index("core")
    zy = lax.axis_index("z") * lax.axis_size("y") + lax.axis_index("y")
    first_row = (x * CORES + core) * own_blocks * size + zy * rows_here

    column_live = (jnp.arange(size)[None, :] < basis_counts[:, None]).reshape(basis)
    row_numbers = first_row % size + jnp.arange(rows_here)
    row_live = row_numbers < basis_counts[first_row // size]
    live = row_live[:, None] & column_live[None, :]

    kept = jnp.where(live, density, 0)
    whole = lax.all_gather(kept, ("x", "core", "z", "y"), axis=0, tiled=True)

    parted = three_index.reshape(SIDE, aux_here // SIDE, own_blocks, neigh, size, size)
    own = lax.all_to_all(parted, "x", 0, 0, tiled=True)
    other = lax.ppermute(own, "core", [(0, 1), (1, 0)])

    place = core.astype(jnp.int32).reshape(1)
    partial = exchange_rows(place, pair_blocks.reshape(-1), own, other, whole)
    pieces = lax.all_to_all(partial.reshape(-1, rows_here, basis), ("x", "z", "y"), 0, 0, tiled=True)
    summed = jnp.sum(pieces.astype(jnp.float32), axis=0)
    return jnp.where(live, summed, 0)


def solution(mesh):
    devices = mesh.devices.reshape(SIDE, CORES, SIDE, SIDE)
    fine = Mesh(devices, ("x", "core", "z", "y"))
    in_specs = (P(("z", "y"), ("x", "core")), P(("x", "core", "z", "y"), None), P(), P())
    out_specs = P(("x", "core", "z", "y"), None)
    return jax.shard_map(
        per_device, mesh=fine, in_specs=in_specs, out_specs=out_specs, check_vma=False
    )
```

time: 329 us -> 193 us (0.59)
  waiting for transfers between devices: 161 us -> 17.3 us
  blocking collectives: 35.8 us -> 117 us
  local copies, waits for them, and re-layouts: 62.4 us -> 2 us
  matrix products: 48.3 us -> 0 us
  Pallas kernels: 0 us -> 37.5 us
    all_gather x2 -> x1, waiting for transfers between devices: 160 us -> 10.6 us  [per_device(): whole = lax.all_gather(kept, ('x', 'core', 'z', 'y'), axis=0, tiled=True)]
    all_to_all x1 -> x2, blocking collectives: 35.8 us -> 117 us  [the longest x1 59 us: per_device(): lax.all_to_all(partial.reshape(-1, rows_here, basis), ('x', 'z', 'y'), 0,...]
    dot_general x4 -> x0, matrix products: 48.3 us -> none  [the longest x1 24.2 us: per_device(): jnp.einsum('pmbc,pbjcn->mbjn', halfway_cols, cleaned, preferred_element_t...]
    pallas_call x0 -> x1, Pallas kernels: none -> 37.5 us  [exchange_rows(): pl.pallas_call(functools.partial(exchange_kernel, groups), out_shape=jax....]
    dynamic_update_slice x2 -> x0, local copies, waits for them, and re-layouts: 18.7 us -> none  [per_device(): lax.map(contract, grouped)]
    unnamed x2 -> x3, local copies, waits for them, and re-layouts: 10.7 us -> 0.09 us
    another operation x2 -> x0, local copies, waits for them, and re-layouts: 8.93 us -> none  [the longest x1 7.43 us: per_device(): halfway.reshape(aux_here, own_blocks * block_size, total_blocks, block_size)]
    reshape x1, local copies, waits for them, and re-layouts: 8.72 us -> 0.67 us  [per_device(): partial = exchange_rows(place, pair_blocks.reshape(-1), own, other, whole)]
  transfers between devices with their start and end apart: 2 -> 2, of which waited for: 2 -> 2; matrix products, arithmetic and copies ran while one was open for 21% -> 0% of each run, Pallas kernels for 0% -> 0%
where the time goes in v1:
time: 193 us; the launch traced here: 192 us
  blocking collectives  117 us (61%)
  Pallas kernels  37.5 us (19%)
  waiting for transfers between devices  17.3 us (9%)
  between operations  13.4 us (7%)
  other arithmetic  4.34 us (2%)
  local copies, waits for them, and re-layouts  2 us (1%)
    all_to_all x1, blocking collectives, per_device(): lax.all_to_all(partial.reshape(-1, rows_here, basis), ('x', 'z', 'y'), 0,...  59 us
    all_to_all x1, blocking collectives, per_device(): own = lax.all_to_all(parted, 'x', 0, 0, tiled=True)  58.2 us
    pallas_call x1, Pallas kernels, exchange_rows(): pl.pallas_call(functools.partial(exchange_kernel, groups), out_shape=jax....  37.5 us
    all_gather x1, waiting for transfers between devices, per_device(): whole = lax.all_gather(kept, ('x', 'core', 'z', 'y'), axis=0, tiled=True)  10.6 us
    ppermute x1, waiting for transfers between devices, per_device(): other = lax.ppermute(own, 'core', [(0, 1), (1, 0)])  6.74 us
  transfers between devices with their start and end apart: 2, of which 2 were waited for; matrix products, arithmetic and copies ran while one was open for 0% of the time, Pallas kernels for 0%

profile of v1, /device:TPU:0, one launch (start us, length us, event | category | flops | bytes accessed | tf_op | source)
XLA Modules:
  0.0 191.8 jit_solution(15491554281778750716)
XLA Ops:
  6.5 0.0 all-gather.2.cloned.1.call-start
  6.5 0.7 fusion
  7.3 1.2 dynamic_slice.3
  8.5 0.7 add_compare_fusion
  9.2 1.6 and_select_fusion.1
  10.7 0.0 all-gather.2.cloned.1.call-update
  10.7 0.0 copy-start
  10.8 58.2 %all_to_all.10.own_hbm = bf16[4,4,2,4,128,128]{5,4,3,2,1,0:T(8,128)(2,1)} all-to-all(bf16[4,4,2,4,128,128]{5,4,3,2,1,0:T(8,128)(2,1)} %bitcast.6), channel_id=1, replica_groups=mesh['x'=4,'core'=2,'z'=4,'y'=4] {'x'}, dimensions={0} | all-to-all | bytes 8388608 | tf_op jit(solution)/shard_map/all_to_all | solution.py:149
  68.9 0.0 collective-permute-start
  68.9 0.0 copy-done
  68.9 0.1 copy.6
  69.0 0.7 reshape.33.pairs
  69.7 6.7 %collective-permute-done.other_hbm = bf16[4,4,2,4,128,128]{5,4,3,2,1,0:T(8,128)(2,1)} collective-permute-done((bf16[4,4,2,4,128,128]{5,4,3,2,1,0:T(8,128)(2,1)}, bf16[4,4,2,4,128,128]{5,4,3,2,1,0:T(8,128)(2,1)}, u32[]{:S(2)}, u32[]{:S(2)}) %collective-permute-start) | collective-permute-done | bytes 4194336 | tf_op jit(solution)/shard_map/ppermute | solution.py:150
  76.4 10.6 %all-gather.2.cloned.1.call-done.density_hbm = bf16[2048,2048]{1,0:T(8,128)(2,1)} async-done(((bf16[16,2048]{1,0:T(8,128)(2,1)}), bf16[2048,2048]{1,0:T(8,128)(2,1)}) %all-gather.2.cloned.1.call-update) | async-done | bytes 8388624 | tf_op jit(solution)/shard_map/all_gather | solution.py:146
  87.0 37.5 %shard_map.46 = bf16[1024,2048]{1,0:T(8,128)(2,1)} custom-call(s32[1]{0:T(128)} %bitcast.2.place, s32[64]{0:T(128)} %reshape.33.pairs, bf16[4,4,2,4,128,128]{5,4,3,2,1,0:T(8,128)(2,1)} %all_to_all.10.own_hbm, bf16[4,4,2,4,128,128]{5,4,3,2,1,0:T(8,128)(2,1)} %collective-permute-done.other_hbm, bf16[2048,2048]{1,0:T(8,128)(2,1)} %all-gather.2.cloned.1.call-done.density_hbm), custom_call_target="tpu_custom_call" | custom-call | flops 17179869184 | bytes 20971520 | tf_op jit(solution)/shard_map/pallas_call | solution.py:104
  124.5 59.0 %all_to_all.11 = bf16[64,16,2048]{2,1,0:T(8,128)(2,1)S(1)} all-to-all(bf16[64,16,2048]{2,1,0:T(8,128)(2,1)} %bitcast.7), channel_id=1, replica_groups=mesh['x'=4,'core'=2,'z'=4,'y'=4] {'x','z','y'}, dimensions={0} | all-to-all | bytes 8388608 | tf_op jit(solution)/shard_map/all_to_all | solution.py:154
  183.5 0.7 convert_reduce_fusion
  184.2 0.7 and_select_fusion
Async XLA Ops:
  6.5 80.4 %all-gather.2.cloned.1.call-start = ((), (), s32[]{:S(2)}) async-start(), calls=%async_computation.2 | async-start | bytes 8454144 | tf_op jit(solution)/shard_map/all_gather | solution.py:146
  10.7 58.2 %copy-start = (s32[16,4]{0,1:T(4,128)S(1)}, s32[16,4]{0,1:T(4,128)}, u32[]{:S(2)}) copy-start(s32[16,4]{0,1:T(4,128)} %param.6) | copy-start | bytes 772
  68.9 7.5 %collective-permute-start = (bf16[4,4,2,4,128,128]{5,4,3,2,1,0:T(8,128)(2,1)}, bf16[4,4,2,4,128,128]{5,4,3,2,1,0:T(8,128)(2,1)}, u32[]{:S(2)}, u32[]{:S(2)}) collective-permute-start(bf16[4,4,2,4,128,128]{5,4,3,2,1,0:T(8,128)(2,1)} %all_to_all.10.own_hbm), channel_id=1, source_target_pairs={{0,16},{16,0},{1,17},{17,1},{2,18},{18,2},{3,19},{19,3},{4,20},{20... | collective-permute-start | bytes 12582920 | tf_op jit(solution)/shard_map/ppermute | solution.py:150
Sparse Core Ops, SparseCore 0:
  10.9 76.0 all-gather.1

commit v2 on v1

v2 whole, which is shorter than its diff:
```python
import jax
import jax.numpy as jnp
from jax import lax
from jax.experimental import pallas as pl
from jax.experimental.pallas import tpu as pltpu
from jax.sharding import Mesh, PartitionSpec as P

CORES = 2
SIDE = 4
LIVE = 1536
LANES = 128
PIECE = 128
WIDTH = 1024


def stacked(tensor, source, mi, aux, neigh):
    return jnp.concatenate(
        [
            jnp.concatenate([tensor[source, p, mi, j] for j in range(neigh)], axis=1)
            for p in range(aux)
        ],
        axis=0,
    )


def exchange_kernel(place, pairs, starts, shifts, counts, own_hbm, other_hbm, density_hbm,
                    out_ref, own, other, density, halfway, total, sems):
    sources, aux, per_source, neigh, size, _ = own.shape
    tiles, basis, width = density.shape
    rows = sources * per_source * size
    core = place[0]

    own_copy = pltpu.make_async_copy(own_hbm, own, sems.at[0])
    other_copy = pltpu.make_async_copy(other_hbm, other, sems.at[1])
    density_copies = [
        pltpu.make_async_copy(
            density_hbm.at[:, t * width : (t + 1) * width], density.at[t], sems.at[2 + t]
        )
        for t in range(tiles)
    ]
    own_copy.start()
    density_copies[0].start()
    own_copy.wait()

    for t in range(tiles):
        density_copies[t].wait()
        if t + 1 < tiles:
            density_copies[t + 1].start()
        if t == 0:
            other_copy.start()

        def first(b, carry):
            block = (b // per_source * CORES + core) * per_source + b % per_source
            at = pl.ds(pl.multiple_of(b * size, size), size)
            lhs = stacked(own, b // per_source, b % per_source, aux, neigh)
            near = jnp.concatenate(
                [
                    density[t, pl.ds(pl.multiple_of(pairs[block * neigh + j] * size, size), size), :]
                    for j in range(neigh)
                ],
                axis=0,
            )
            product = jnp.dot(lhs, near, preferred_element_type=jnp.float32).astype(jnp.bfloat16)
            for k in range(width // size):
                for p in range(aux):
                    halfway[t * (width // size) + k, at, p * size : (p + 1) * size] = product[
                        p * size : (p + 1) * size, k * size : (k + 1) * size
                    ]
            return carry

        lax.fori_loop(0, sources * per_source, first, 0, unroll=2)

    total[...] = jnp.zeros_like(total)
    other_copy.wait()

    def add_in(tensor, which):
        def second(b, carry):
            block = (b // per_source * CORES + which) * per_source + b % per_source
            rhs = stacked(tensor, b // per_source, b % per_source, aux, neigh)
            for r in range(0, rows, PIECE):
                product = jnp.dot(
                    halfway[block, r : r + PIECE], rhs, preferred_element_type=jnp.float32
                )
                for j in range(neigh):
                    total[pairs[block * neigh + j], r : r + PIECE] += product[
                        :, j * size : (j + 1) * size
                    ]
            return carry

        lax.fori_loop(0, sources * per_source, second, 0, unroll=2)

    add_in(own, core)
    add_in(other, 1 - core)

    out_ref[...] = jnp.zeros_like(out_ref)
    row = lax.broadcasted_iota(jnp.int32, (size, 2 * LANES), 0)
    column = lax.broadcasted_iota(jnp.int32, (size, 2 * LANES), 1)

    def pack(n, carry):
        chosen = (column == row + shifts[n]) & (row < counts[n])
        moved = jnp.dot(
            total[n].astype(jnp.bfloat16),
            jnp.where(chosen, 1.0, 0.0).astype(jnp.bfloat16),
            preferred_element_type=jnp.float32,
        ).astype(jnp.bfloat16)
        at = pl.ds(pl.multiple_of(starts[n] * LANES, LANES), 2 * LANES)
        out_ref[:, at] += moved
        return carry

    lax.fori_loop(0, basis // size, pack, 0)


def exchange_rows(place, pairs, starts, shifts, counts, own, other, density):
    sources, aux, per_source, neigh, size, _ = own.shape
    basis = density.shape[0]
    rows = sources * per_source * size
    scalar, vector = pl.BlockSpec(memory_space=pltpu.SMEM), pl.BlockSpec(memory_space=pltpu.VMEM)
    tiles = basis // WIDTH
    return pl.pallas_call(
        exchange_kernel,
        out_shape=jax.ShapeDtypeStruct((rows, LIVE), jnp.bfloat16),
        in_specs=[scalar] * 5 + [pl.BlockSpec(memory_space=pl.ANY)] * 3,
        out_specs=vector,
        scratch_shapes=[
            pltpu.VMEM(own.shape, jnp.bfloat16),
            pltpu.VMEM(own.shape, jnp.bfloat16),
            pltpu.VMEM((tiles, basis, WIDTH), jnp.bfloat16),
            pltpu.VMEM((basis // size, rows, aux * size), jnp.bfloat16),
            pltpu.VMEM((basis // size, rows, size), jnp.float32),
            pltpu.SemaphoreType.DMA((2 + tiles,)),
        ],
        compiler_params=pltpu.CompilerParams(vmem_limit_bytes=52 << 20),
        cost_estimate=pl.CostEstimate(
            flops=4 * rows * aux * neigh * size * basis,
            bytes_accessed=4 * own.size + 2 * density.size + 2 * rows * LIVE,
            transcendentals=0,
        ),
    )(place, pairs, starts, shifts, counts, own, other, density)


def finish_kernel(rows_live, starts, shifts, counts, pieces, out_ref, summed):
    amount, rows, _ = pieces.shape
    summed[...] = jnp.zeros_like(summed)

    def add(i, carry):
        part = pieces[pl.ds(i * 8, 8)].astype(jnp.float32)
        summed[...] += jnp.sum(part, axis=0)
        return carry

    lax.fori_loop(0, amount // 8, add, 0)
    row = lax.broadcasted_iota(jnp.int32, (rows, LANES), 0)
    lane = lax.broadcasted_iota(jnp.int32, (rows, LANES), 1)
    for n in range(out_ref.shape[1] // LANES):
        window = summed[:, pl.ds(pl.multiple_of(starts[n] * LANES, LANES), 2 * LANES)]
        turned = pltpu.roll(window, lax.rem(2 * LANES - shifts[n], 2 * LANES), axis=1)
        live = (lane < counts[n]) & (row < rows_live[0])
        out_ref[:, n * LANES : (n + 1) * LANES] = jnp.where(live, turned[:, :LANES], 0.0)


def finish(rows_live, starts, shifts, counts, pieces, basis):
    rows = pieces.shape[1]
    scalar, vector = pl.BlockSpec(memory_space=pltpu.SMEM), pl.BlockSpec(memory_space=pltpu.VMEM)
    return pl.pallas_call(
        finish_kernel,
        out_shape=jax.ShapeDtypeStruct((rows, basis), jnp.float32),
        in_specs=[scalar] * 4 + [vector],
        out_specs=vector,
        scratch_shapes=[pltpu.VMEM((rows, LIVE), jnp.float32)],
    )(rows_live, starts, shifts, counts, pieces)


def per_device(three_index, density, pair_blocks, basis_counts):
    aux_here, own_blocks, neigh, size, _ = three_index.shape
    rows_here, basis = density.shape
    blocks = basis // size
    x, core = lax.axis_index("x"), lax.axis_index("core")
    zy = lax.axis_index("z") * lax.axis_size("y") + lax.axis_index("y")
    first_row = (x * CORES + core) * own_blocks * size + zy * rows_here

    numbers = jnp.arange(blocks)
    offsets = jnp.sum(jnp.where(numbers[None, :] < numbers[:, None], basis_counts[None, :], 0), axis=1)
    starts = jnp.minimum(offsets // LANES, LIVE // LANES - 2)
    shifts = offsets - starts * LANES

    rows_live = jnp.sum(jnp.where(numbers == first_row // size, basis_counts, 0)) - first_row % size
    column_live = (jnp.arange(size)[None, :] < basis_counts[:, None]).reshape(basis)
    live = (jnp.arange(rows_here) < rows_live)[:, None] & column_live[None, :]

    kept = jnp.where(live, density, 0)
    whole = lax.all_gather(kept, ("x", "core", "z", "y"), axis=0, tiled=True)

    parted = three_index.reshape(SIDE, aux_here // SIDE, own_blocks, neigh, size, size)
    own = lax.all_to_all(parted, "x", 0, 0, tiled=True)
    other = lax.ppermute(own, "core", [(0, 1), (1, 0)])

    partial = exchange_rows(
        core.astype(jnp.int32).reshape(1), pair_blocks.reshape(-1), starts, shifts, basis_counts,
        own, other, whole,
    )
    pieces = lax.all_to_all(partial.reshape(-1, rows_here, LIVE), ("x", "z", "y"), 0, 0, tiled=True)
    return finish(rows_live.astype(jnp.int32).reshape(1), starts, shifts, basis_counts, pieces, basis)


def solution(mesh):
    devices = mesh.devices.reshape(SIDE, CORES, SIDE, SIDE)
    fine = Mesh(devices, ("x", "core", "z", "y"))
    in_specs = (P(("z", "y"), ("x", "core")), P(("x", "core", "z", "y"), None), P(), P())
    out_specs = P(("x", "core", "z", "y"), None)
    return jax.shard_map(
        per_device, mesh=fine, in_specs=in_specs, out_specs=out_specs, check_vma=False
    )
```

time: 193 us -> 177 us (0.917)
  blocking collectives: 117 us -> 106 us
  Pallas kernels: 37.5 us -> 34.9 us
    all_to_all x1, blocking collectives: 59 us -> 48.1 us  [per_device(): lax.all_to_all(partial.reshape(-1, rows_here, LIVE), ('x', 'z', 'y'), 0,...]
    pallas_call x1 -> x2, Pallas kernels: 37.5 us -> 34.9 us  [the longest x1 31.8 us: exchange_rows(): pl.pallas_call(exchange_kernel, out_shape=jax.ShapeDtypeStruct((rows, LIV...]
where the time goes in v2:
time: 177 us
  blocking collectives  106 us (60%)
  Pallas kernels  34.9 us (20%)
  waiting for transfers between devices  17.8 us (10%)
  between operations  14.1 us (8%)
  other arithmetic  3.71 us (2%)
    all_to_all x1, blocking collectives, per_device(): own = lax.all_to_all(parted, 'x', 0, 0, tiled=True)  58.1 us
    all_to_all x1, blocking collectives, per_device(): lax.all_to_all(partial.reshape(-1, rows_here, LIVE), ('x', 'z', 'y'), 0,...  48.1 us
    pallas_call x1, Pallas kernels, exchange_rows(): pl.pallas_call(exchange_kernel, out_shape=jax.ShapeDtypeStruct((rows, LIV...  31.8 us
    all_gather x1, waiting for transfers between devices, per_device(): whole = lax.all_gather(kept, ('x', 'core', 'z', 'y'), axis=0, tiled=True)  10.6 us
    ppermute x1, waiting for transfers between devices, per_device(): other = lax.ppermute(own, 'core', [(0, 1), (1, 0)])  7.16 us
  transfers between devices with their start and end apart: 2, of which 2 were waited for; matrix products, arithmetic and copies ran while one was open for 0% of the time, Pallas kernels for 0%

profile of v2, /device:TPU:0, one launch (start us, length us, event | category | flops | bytes accessed | tf_op | source)
XLA Modules:
  0.0 177.0 jit_solution(13653760411762746249)
XLA Ops:
  6.5 0.0 all-gather.2.cloned.1.call-start
  6.5 0.7 fusion
  7.3 1.3 fusion.1
  9.2 1.6 and_select_fusion
  10.8 0.0 all-gather.2.cloned.1.call-update
  10.8 0.0 copy-start.3
  10.8 0.0 copy-start
  10.8 58.1 %all_to_all.10.own_hbm = bf16[4,4,2,4,128,128]{5,4,3,2,1,0:T(8,128)(2,1)} all-to-all(bf16[4,4,2,4,128,128]{5,4,3,2,1,0:T(8,128)(2,1)} %bitcast.6), channel_id=1, replica_groups=mesh['x'=4,'core'=2,'z'=4,'y'=4] {'x'}, dimensions={0} | all-to-all | bytes 8388608 | tf_op jit(solution)/shard_map/all_to_all | solution.py:193
  69.0 0.0 collective-permute-start
  69.0 0.0 copy-done.3
  69.0 0.1 copy.7
  69.1 0.1 reshape.37.pairs
  69.2 0.0 copy-done
  69.2 0.1 select_reduce_fusion
  69.3 0.0 copy-start.1
  69.3 0.0 copy-start.2
  69.3 7.2 %collective-permute-done.other_hbm = bf16[4,4,2,4,128,128]{5,4,3,2,1,0:T(8,128)(2,1)} collective-permute-done((bf16[4,4,2,4,128,128]{5,4,3,2,1,0:T(8,128)(2,1)}, bf16[4,4,2,4,128,128]{5,4,3,2,1,0:T(8,128)(2,1)}, u32[]{:S(2)}, u32[]{:S(2)}) %collective-permute-start) | collective-permute-done | bytes 4194336 | tf_op jit(solution)/shard_map/ppermute | solution.py:194
  76.5 10.6 %all-gather.2.cloned.1.call-done.density_hbm = bf16[2048,2048]{1,0:T(8,128)(2,1)} async-done(((bf16[16,2048]{1,0:T(8,128)(2,1)}), bf16[2048,2048]{1,0:T(8,128)(2,1)}) %all-gather.2.cloned.1.call-update) | async-done | bytes 8388624 | tf_op jit(solution)/shard_map/all_gather | solution.py:190
  87.1 31.8 %shard_map.46 = bf16[1024,1536]{1,0:T(8,128)(2,1)} custom-call(s32[1]{0:T(128)} %bitcast.1.place, s32[64]{0:T(128)S(1)} %reshape.37.pairs, s32[16]{0:T(128)S(1)} %get-tuple-element.6.starts, s32[16]{0:T(128)S(1)} %get-tuple-element.5.shifts, s32[16]{0:T(128)S(1)} %copy-done, bf16[4,4,2,4,128,128]{5,4,3,2,1,0:T(8,128)(2,1)} %all_to_all.10.own_hbm, ...), custom_call_target="tpu_custom_call" | custom-call | flops 17179869184 | bytes 19922944 | tf_op jit(solution)/shard_map/pallas_call | solution.py:119
  118.9 0.0 copy-done.1
  118.9 0.0 copy-done.2
  118.9 48.1 %all_to_all.11.pieces = bf16[64,16,1536]{2,1,0:T(8,128)(2,1)} all-to-all(bf16[64,16,1536]{2,1,0:T(8,128)(2,1)} %bitcast.7), channel_id=1, replica_groups=mesh['x'=4,'core'=2,'z'=4,'y'=4] {'x','z','y'}, dimensions={0} | all-to-all | bytes 6291456 | tf_op jit(solution)/shard_map/all_to_all | solution.py:200
  167.0 3.2 %shard_map.47 = f32[16,2048]{1,0:T(8,128)} custom-call(s32[1]{0:T(128)} %bitcast.rows_live, s32[16]{0:T(128)} %copy-done.2, s32[16]{0:T(128)} %copy-done.1, s32[16]{0:T(128)} %counts.3, bf16[64,16,1536]{2,1,0:T(8,128)(2,1)} %all_to_all.11.pieces), custom_call_target="tpu_custom_call" | custom-call | tf_op jit(solution)/shard_map/pallas_call | solution.py:163
  (2 shorter events, 0.0 us)
Async XLA Ops:
  6.5 80.6 %all-gather.2.cloned.1.call-start = ((), (), s32[]{:S(2)}) async-start(), calls=%async_computation.2 | async-start | bytes 8454144 | tf_op jit(solution)/shard_map/all_gather | solution.py:190
  10.8 58.2 %copy-start.3 = (s32[16,4]{0,1:T(4,128)S(1)}, s32[16,4]{0,1:T(4,128)}, u32[]{:S(2)}) copy-start(s32[16,4]{0,1:T(4,128)} %param.6) | copy-start | bytes 772
  10.8 58.3 %copy-start = (s32[16]{0:T(128)S(1)}, s32[16]{0:T(128)}, u32[]{:S(2)}) copy-start(s32[16]{0:T(128)} %counts.3) | copy-start | bytes 196
  69.0 7.5 %collective-permute-start = (bf16[4,4,2,4,128,128]{5,4,3,2,1,0:T(8,128)(2,1)}, bf16[4,4,2,4,128,128]{5,4,3,2,1,0:T(8,128)(2,1)}, u32[]{:S(2)}, u32[]{:S(2)}) collective-permute-start(bf16[4,4,2,4,128,128]{5,4,3,2,1,0:T(8,128)(2,1)} %all_to_all.10.own_hbm), channel_id=1, source_target_pairs={{0,16},{16,0},{1,17},{17,1},{2,18},{18,2},{3,19},{19,3},{4,20},{20... | collective-permute-start | bytes 12582920 | tf_op jit(solution)/shard_map/ppermute | solution.py:194
  69.3 49.6 %copy-start.1 = (s32[16]{0:T(128)}, s32[16]{0:T(128)S(1)}, u32[]{:S(2)}) copy-start(s32[16]{0:T(128)S(1)} %get-tuple-element.5.shifts) | copy-start | bytes 196
  69.3 49.6 %copy-start.2 = (s32[16]{0:T(128)}, s32[16]{0:T(128)S(1)}, u32[]{:S(2)}) copy-start(s32[16]{0:T(128)S(1)} %get-tuple-element.6.starts) | copy-start | bytes 196
Sparse Core Ops, SparseCore 0:
  10.9 76.1 all-gather.1

commit v3 on v2

v3 whole, which is shorter than its diff:
```python
import jax
import jax.numpy as jnp
from jax import lax
from jax.experimental import pallas as pl
from jax.experimental.pallas import tpu as pltpu
from jax.sharding import Mesh, PartitionSpec as P

CORES = 2
SIDE = 4
LIVE = 1536
LANES = 128
PIECE = 128


def stacked(tensor, source, mi, aux, neigh):
    return jnp.concatenate(
        [
            jnp.concatenate([tensor[source, p, mi, j] for j in range(neigh)], axis=1)
            for p in range(aux)
        ],
        axis=0,
    )


def halfway_kernel(place, pairs, own, here_a, there_a, here_b, there_b, out_ref, density, sems):
    _, aux, per_source, neigh, size, _ = own.shape
    piece = density.shape[-2]
    half, source = pl.program_id(0), pl.program_id(1)
    x, core, z, y = place[0], place[1], place[2], place[3]

    def copies(here, there, first):
        return [
            pltpu.make_async_copy(here, density.at[first // 2, 0], sems.at[first]),
            pltpu.make_async_copy(there, density.at[first // 2, 1], sems.at[first + 1]),
        ]

    copies_a, copies_b = copies(here_a, there_a, 0), copies(here_b, there_b, 2)

    @pl.when((half == 0) & (source == 0))
    def _():
        for copy in copies_a + copies_b:
            copy.start()
        for copy in copies_a:
            copy.wait()

    @pl.when((half == 1) & (source == 0))
    def _():
        for copy in copies_b:
            copy.wait()

    for mi in range(per_source):
        block = (source * CORES + core) * per_source + mi
        lhs = stacked(own, 0, mi, aux, neigh)
        near = []
        for j in range(neigh):
            partner = pairs[block * neigh + j]
            back_x = lax.rem(x - partner // (CORES * per_source) + SIDE, SIDE)
            swap = jnp.where(partner // per_source % CORES == core, 0, 1)
            for zy in range(size // piece):
                from_z = partner % per_source * (SIDE // per_source) + zy // SIDE
                back_z = lax.rem(z - from_z + SIDE, SIDE)
                back_y = lax.rem(y - zy % SIDE + SIDE, SIDE)
                outer = jnp.where(half == 0, back_y, back_z)
                inner = jnp.where(half == 0, back_z, back_y)
                near.append(density[half, swap, outer, inner, back_x])
        product = jnp.dot(
            lhs, jnp.concatenate(near, axis=0), preferred_element_type=jnp.float32
        ).astype(jnp.bfloat16)
        for k in range(out_ref.shape[0]):
            for p in range(aux):
                out_ref[k, mi * size : (mi + 1) * size, p * size : (p + 1) * size] = product[
                    p * size : (p + 1) * size, k * size : (k + 1) * size
                ]


def halfway_rows(place, pairs, own, here_a, there_a, here_b, there_b):
    sources, aux, per_source, neigh, size, _ = own.shape
    width = here_a.shape[-1]
    blocks = 2 * width // size
    rows = sources * per_source * size
    anywhere = pl.BlockSpec(memory_space=pl.ANY)
    return pl.pallas_call(
        halfway_kernel,
        out_shape=jax.ShapeDtypeStruct((blocks, rows, aux * size), jnp.bfloat16),
        grid_spec=pltpu.PrefetchScalarGridSpec(
            num_scalar_prefetch=2,
            grid=(2, sources),
            in_specs=[
                pl.BlockSpec((1,) + own.shape[1:], lambda h, s, *_: (s, 0, 0, 0, 0, 0)),
            ] + [anywhere] * 4,
            out_specs=pl.BlockSpec(
                (blocks // 2, per_source * size, aux * size), lambda h, s, *_: (h, s, 0)
            ),
            scratch_shapes=[
                pltpu.VMEM((2, CORES) + here_a.shape, jnp.bfloat16),
                pltpu.SemaphoreType.DMA((4,)),
            ],
        ),
        compiler_params=pltpu.CompilerParams(vmem_limit_bytes=36 << 20),
        cost_estimate=pl.CostEstimate(
            flops=2 * rows * aux * neigh * size * 2 * width,
            bytes_accessed=4 * own.size + 8 * here_a.size + 2 * blocks * rows * aux * size,
            transcendentals=0,
        ),
    )(place, pairs, own, here_a, there_a, here_b, there_b)


def exchange_kernel(place, pairs, starts, shifts, counts, own, other, from_own, from_other,
                    out_ref, total):
    _, aux, _, neigh, size, _ = own.shape
    _, rows, _ = from_own.shape
    step = pl.program_id(0)
    per_source = pl.num_programs(0) // SIDE

    @pl.when(step == 0)
    def _():
        total[...] = jnp.zeros_like(total)

    for which, tensor, halfway in ((place[1], own, from_own), (1 - place[1], other, from_other)):
        block = (step // per_source * CORES + which) * per_source + step % per_source
        rhs = stacked(tensor, 0, 0, aux, neigh)
        for r in range(0, rows, PIECE):
            product = jnp.dot(halfway[0, r : r + PIECE], rhs, preferred_element_type=jnp.float32)
            for j in range(neigh):
                total[pairs[block * neigh + j], r : r + PIECE] += product[
                    :, j * size : (j + 1) * size
                ]

    @pl.when(step == pl.num_programs(0) - 1)
    def _():
        out_ref[...] = jnp.zeros_like(out_ref)
        row = lax.broadcasted_iota(jnp.int32, (size, 2 * LANES), 0)
        column = lax.broadcasted_iota(jnp.int32, (size, 2 * LANES), 1)

        def pack(n, carry):
            chosen = (column == row + shifts[n]) & (row < counts[n])
            moved = jnp.dot(
                total[n].astype(jnp.bfloat16),
                jnp.where(chosen, 1.0, 0.0).astype(jnp.bfloat16),
                preferred_element_type=jnp.float32,
            ).astype(jnp.bfloat16)
            at = pl.ds(pl.multiple_of(starts[n] * LANES, LANES), 2 * LANES)
            out_ref[:, at] += moved
            return carry

        lax.fori_loop(0, total.shape[0], pack, 0)


def exchange_rows(place, pairs, starts, shifts, counts, own, other, halfway):
    sources, aux, per_source, neigh, size, _ = own.shape
    blocks, rows, _ = halfway.shape

    def tensor_map(i, *_):
        return (i // per_source, 0, i % per_source, 0, 0, 0)

    def halfway_map(swap):
        def at(i, place, *_):
            which = place[1] if swap == 0 else 1 - place[1]
            return ((i // per_source * CORES + which) * per_source + i % per_source, 0, 0)

        return at

    tensor = pl.BlockSpec((1, aux, 1, neigh, size, size), tensor_map)
    return pl.pallas_call(
        exchange_kernel,
        out_shape=jax.ShapeDtypeStruct((rows, LIVE), jnp.bfloat16),
        grid_spec=pltpu.PrefetchScalarGridSpec(
            num_scalar_prefetch=5,
            grid=(sources * per_source,),
            in_specs=[tensor, tensor] + [
                pl.BlockSpec((1, rows, aux * size), halfway_map(swap)) for swap in range(CORES)
            ],
            out_specs=pl.BlockSpec((rows, LIVE), lambda i, *_: (0, 0)),
            scratch_shapes=[pltpu.VMEM((blocks, rows, size), jnp.float32)],
        ),
        compiler_params=pltpu.CompilerParams(vmem_limit_bytes=36 << 20),
        cost_estimate=pl.CostEstimate(
            flops=2 * rows * aux * neigh * size * blocks * size,
            bytes_accessed=4 * own.size + 2 * halfway.size + 2 * rows * LIVE,
            transcendentals=0,
        ),
    )(place, pairs, starts, shifts, counts, own, other, halfway, halfway)


def finish_kernel(rows_live, starts, shifts, counts, pieces, out_ref, summed):
    amount, rows, _ = pieces.shape
    summed[...] = jnp.zeros_like(summed)

    def add(i, carry):
        part = pieces[pl.ds(i * 8, 8)].astype(jnp.float32)
        summed[...] += jnp.sum(part, axis=0)
        return carry

    lax.fori_loop(0, amount // 8, add, 0)
    row = lax.broadcasted_iota(jnp.int32, (rows, LANES), 0)
    lane = lax.broadcasted_iota(jnp.int32, (rows, LANES), 1)
    for n in range(out_ref.shape[1] // LANES):
        window = summed[:, pl.ds(pl.multiple_of(starts[n] * LANES, LANES), 2 * LANES)]
        turned = pltpu.roll(window, lax.rem(2 * LANES - shifts[n], 2 * LANES), axis=1)
        live = (lane < counts[n]) & (row < rows_live[0])
        out_ref[:, n * LANES : (n + 1) * LANES] = jnp.where(live, turned[:, :LANES], 0.0)


def finish(rows_live, starts, shifts, counts, pieces, basis):
    rows = pieces.shape[1]
    scalar, vector = pl.BlockSpec(memory_space=pltpu.SMEM), pl.BlockSpec(memory_space=pltpu.VMEM)
    return pl.pallas_call(
        finish_kernel,
        out_shape=jax.ShapeDtypeStruct((rows, basis), jnp.float32),
        in_specs=[scalar] * 4 + [vector],
        out_specs=vector,
        scratch_shapes=[pltpu.VMEM((rows, LIVE), jnp.float32)],
    )(rows_live, starts, shifts, counts, pieces)


def moved(value, axis, shift):
    return lax.ppermute(value, axis, [(k, (k + shift) % SIDE) for k in range(SIDE)])


def swapped(value):
    return lax.ppermute(value, "core", [(0, 1), (1, 0)])


def ring(value, axis):
    up, down = moved(value, axis, 1), moved(value, axis, SIDE - 1)
    cut = value.shape[0] // 2
    far = [moved(up[:cut], axis, 1), moved(down[cut:], axis, SIDE - 1)]
    return jnp.stack([value, up, jnp.concatenate(far), down])


def per_device(three_index, density, pair_blocks, basis_counts):
    aux_here, own_blocks, neigh, size, _ = three_index.shape
    rows_here, basis = density.shape
    blocks = basis // size
    x, core, z, y = (lax.axis_index(name) for name in ("x", "core", "z", "y"))
    first_row = (x * CORES + core) * own_blocks * size + (z * SIDE + y) * rows_here

    numbers = jnp.arange(blocks)
    offsets = jnp.sum(jnp.where(numbers[None, :] < numbers[:, None], basis_counts[None, :], 0), axis=1)
    starts = jnp.minimum(offsets // LANES, LIVE // LANES - 2)
    shifts = offsets - starts * LANES

    rows_live = jnp.sum(jnp.where(numbers == first_row // size, basis_counts, 0)) - first_row % size
    column_live = (jnp.arange(size)[None, :] < basis_counts[:, None]).reshape(basis)
    live = (jnp.arange(rows_here) < rows_live)[:, None] & column_live[None, :]

    kept = jnp.where(live, density, 0)
    lines = jnp.stack([kept] + [moved(kept, "x", s) for s in range(1, SIDE)])
    here_a = ring(ring(lines[..., : basis // 2], "z"), "y")
    here_b = ring(ring(lines[..., basis // 2 :], "y"), "z")
    there_a, there_b = swapped(here_a), swapped(here_b)

    parted = three_index.reshape(SIDE, aux_here // SIDE, own_blocks, neigh, size, size)
    own = lax.all_to_all(parted, "x", 0, 0, tiled=True)
    own, there_a, there_b = lax.optimization_barrier((own, there_a, there_b))
    other = swapped(own)

    place = jnp.stack([x, core, z, y]).astype(jnp.int32)
    pairs = pair_blocks.reshape(-1)
    halfway = halfway_rows(place, pairs, own, here_a, there_a, here_b, there_b)
    partial = exchange_rows(place, pairs, starts, shifts, basis_counts, own, other, halfway)
    pieces = lax.all_to_all(partial.reshape(-1, rows_here, LIVE), ("x", "z", "y"), 0, 0, tiled=True)
    return finish(rows_live.astype(jnp.int32).reshape(1), starts, shifts, basis_counts, pieces, basis)


def solution(mesh):
    devices = mesh.devices.reshape(SIDE, CORES, SIDE, SIDE)
    fine = Mesh(devices, ("x", "core", "z", "y"))
    in_specs = (P(("z", "y"), ("x", "core")), P(("x", "core", "z", "y"), None), P(), P())
    out_specs = P(("x", "core", "z", "y"), None)
    return jax.shard_map(
        per_device, mesh=fine, in_specs=in_specs, out_specs=out_specs, check_vma=False
    )
```

time: 177 us -> 179 us (1.011)
  blocking collectives: 106 us -> 48.4 us
  starting transfers between devices: 0.01 us -> 35.2 us
  waiting for transfers between devices: 17.8 us -> 35.8 us
  between operations: 14.1 us -> 1.01 us
  local copies, waits for them, and re-layouts: 0.19 us -> 9.18 us
  Pallas kernels: 34.9 us -> 40.2 us
  other arithmetic: 3.71 us -> 7.9 us
    all_to_all x1 -> x0, blocking collectives: 58.1 us -> none  [per_device(): own = lax.all_to_all(parted, 'x', 0, 0, tiled=True)]
    ppermute x1 -> x22, starting transfers between devices: 0.01 us -> 30.4 us  [the longest x19 30.2 us: moved(): lax.ppermute(value, axis, [(k, (k + shift) % SIDE) for k in range(SIDE)])]
    all_to_all x0 -> x1, waiting for transfers between devices: none -> 24.1 us  [per_device(): own = lax.all_to_all(parted, 'x', 0, 0, tiled=True)]
    pallas_call x0 -> x1, Pallas kernels: none -> 16.6 us  [halfway_rows(): pl.pallas_call(halfway_kernel, out_shape=jax.ShapeDtypeStruct((blocks, ro...]
    pallas_call x1, Pallas kernels: 31.8 us -> 20.4 us  [exchange_rows(): pl.pallas_call(exchange_kernel, out_shape=jax.ShapeDtypeStruct((rows, LIV...]
    all_gather x1 -> x0, waiting for transfers between devices: 10.6 us -> none  [per_device(): whole = lax.all_gather(kept, ('x', 'core', 'z', 'y'), axis=0, tiled=True)]
    unnamed x9 -> x33, local copies, waits for them, and re-layouts: 0.1 us -> 8.96 us
    all_to_all x0 -> x1, starting transfers between devices: none -> 4.84 us  [per_device(): own = lax.all_to_all(parted, 'x', 0, 0, tiled=True)]
  transfers between devices with their start and end apart: 2 -> 23, of which waited for: 2 -> 7; matrix products, arithmetic and copies ran while one was open for 0% -> 3% of each run, Pallas kernels for 0% -> 9%
where the time goes in v3:
time: 179 us; the launch traced here: 178 us
  blocking collectives  48.4 us (27%)
  Pallas kernels  40.2 us (22%)
  waiting for transfers between devices  35.8 us (20%)
  starting transfers between devices  35.2 us (20%)
  local copies, waits for them, and re-layouts  9.18 us (5%)
  other arithmetic  7.9 us (4%)
    all_to_all x1, blocking collectives, per_device(): lax.all_to_all(partial.reshape(-1, rows_here, LIVE), ('x', 'z', 'y'), 0,...  48.4 us
    ppermute x19, starting transfers between devices, moved(): lax.ppermute(value, axis, [(k, (k + shift) % SIDE) for k in range(SIDE)])  30.2 us
    all_to_all x1, waiting for transfers between devices, per_device(): own = lax.all_to_all(parted, 'x', 0, 0, tiled=True)  24.1 us
    pallas_call x1, Pallas kernels, exchange_rows(): pl.pallas_call(exchange_kernel, out_shape=jax.ShapeDtypeStruct((rows, LIV...  20.4 us
    pallas_call x1, Pallas kernels, halfway_rows(): pl.pallas_call(halfway_kernel, out_shape=jax.ShapeDtypeStruct((blocks, ro...  16.6 us
    ppermute x19, waiting for transfers between devices, moved(): lax.ppermute(value, axis, [(k, (k + shift) % SIDE) for k in range(SIDE)])  10.3 us
    unnamed x33, local copies, waits for them, and re-layouts  8.96 us
    all_to_all x1, starting transfers between devices, per_device(): own = lax.all_to_all(parted, 'x', 0, 0, tiled=True)  4.84 us
  transfers between devices with their start and end apart: 23, of which 7 were waited for; matrix products, arithmetic and copies ran while one was open for 3% of the time, Pallas kernels for 9%

profile of v3, /device:TPU:0, one launch (start us, length us, event | category | flops | bytes accessed | tf_op | source)
XLA Modules:
  0.0 177.7 jit_solution(6718245295323979663)
XLA Ops:
  0.0 0.7 fusion
  0.7 1.4 fusion.1
  2.8 0.9 and_select_fusion
  3.7 2.9 %collective-permute-start.2 = (bf16[16,2048]{1,0:T(8,128)(2,1)S(1)}, bf16[16,2048]{1,0:T(8,128)(2,1)S(1)}, u32[]{:S(2)}, u32[]{:S(2)}) collective-permute-start(bf16[16,2048]{1,0:T(8,128)(2,1)S(1)} %and_select_fusion), channel_id=1, source_target_pairs={{0,96},{32,0},{64,32},{96,64},{1,97},{33,1},{65,33},{97,65},{2,98}... | collective-permute-start | bytes 196616 | tf_op jit(solution)/shard_map/ppermute | solution.py:217
  6.6 2.3 %collective-permute-start.1 = (bf16[16,2048]{1,0:T(8,128)(2,1)S(1)}, bf16[16,2048]{1,0:T(8,128)(2,1)S(1)}, u32[]{:S(2)}, u32[]{:S(2)}) collective-permute-start(bf16[16,2048]{1,0:T(8,128)(2,1)S(1)} %and_select_fusion), channel_id=1, source_target_pairs={{0,64},{32,96},{64,0},{96,32},{1,65},{33,97},{65,1},{97,33},{2,66}... | collective-permute-start | bytes 196616 | tf_op jit(solution)/shard_map/ppermute | solution.py:217
  8.9 0.9 fusion.6
  9.9 3.0 %collective-permute-done = bf16[16,2048]{1,0:T(8,128)(2,1)S(1)} collective-permute-done((bf16[16,2048]{1,0:T(8,128)(2,1)S(1)}, bf16[16,2048]{1,0:T(8,128)(2,1)S(1)}, u32[]{:S(2)}, u32[]{:S(2)}) %collective-permute-start) | collective-permute-done | bytes 65568 | tf_op jit(solution)/shard_map/ppermute | solution.py:217
  12.9 1.6 collective-permute-start.12
  14.6 1.7 collective-permute-start.14
  16.3 1.9 %collective-permute-start.3 = (bf16[4,16,1024]{2,1,0:T(8,128)(2,1)S(1)}, bf16[4,16,1024]{2,1,0:T(8,128)(2,1)S(1)}, u32[]{:S(2)}, u32[]{:S(2)}) collective-permute-start(bf16[4,16,1024]{2,1,0:T(8,128)(2,1)S(1)} %get-tuple-element.20), channel_id=1, source_target_pairs={{0,4},{4,8},{8,12},{12,0},{1,5},{5,9},{9,13},{13,1},{2,6},{6,10},{... | collective-permute-start | bytes 393224 | tf_op jit(solution)/shard_map/ppermute | solution.py:217
  18.2 2.1 %collective-permute-start.5 = (bf16[4,16,1024]{2,1,0:T(8,128)(2,1)S(1)}, bf16[4,16,1024]{2,1,0:T(8,128)(2,1)S(1)}, u32[]{:S(2)}, u32[]{:S(2)}) collective-permute-start(bf16[4,16,1024]{2,1,0:T(8,128)(2,1)S(1)} %get-tuple-element.20), channel_id=1, source_target_pairs={{0,12},{4,0},{8,4},{12,8},{1,13},{5,1},{9,5},{13,9},{2,14},{6,2},{... | collective-permute-start | bytes 393224 | tf_op jit(solution)/shard_map/ppermute | solution.py:217
  20.3 0.4 collective-permute-start.13
  20.8 2.9 %collective-permute-start.15 = (bf16[2,16,1024]{2,1,0:T(8,128)(2,1)S(1)}, bf16[2,16,1024]{2,1,0:T(8,128)(2,1)S(1)}, u32[]{:S(2)}, u32[]{:S(2)}) collective-permute-start(bf16[2,16,1024]{2,1,0:T(8,128)(2,1)S(1)} %slice.47), channel_id=1, source_target_pairs={{0,3},{1,0},{2,1},{3,2},{4,7},{5,4},{6,5},{7,6},{8,11},{9,8},{10,9... | collective-permute-start | bytes 196616 | tf_op jit(solution)/shard_map/ppermute | solution.py:217
  23.7 0.8 collective-permute-start.4
  24.5 2.6 %collective-permute-start.6 = (bf16[2,16,1024]{2,1,0:T(8,128)(2,1)S(1)}, bf16[2,16,1024]{2,1,0:T(8,128)(2,1)S(1)}, u32[]{:S(2)}, u32[]{:S(2)}) collective-permute-start(bf16[2,16,1024]{2,1,0:T(8,128)(2,1)S(1)} %slice.42), channel_id=1, source_target_pairs={{0,12},{4,0},{8,4},{12,8},{1,13},{5,1},{9,5},{13,9},{2,14},{6,2},{... | collective-permute-start | bytes 196616 | tf_op jit(solution)/shard_map/ppermute | solution.py:217
  27.1 0.9 fusion.3
  28.0 3.2 %collective-permute-start.18 = (bf16[4,4,16,1024]{3,2,1,0:T(8,128)(2,1)}, bf16[4,4,16,1024]{3,2,1,0:T(8,128)(2,1)S(1)}, u32[]{:S(2)}, u32[]{:S(2)}) collective-permute-start(bf16[4,4,16,1024]{3,2,1,0:T(8,128)(2,1)} %get-tuple-element.14), channel_id=1, source_target_pairs={{0,12},{4,0},{8,4},{12,8},{1,13},{5,1},{9,5},{13,9},{2,14},{6,2},{... | collective-permute-start | bytes 1572872 | tf_op jit(solution)/shard_map/ppermute | solution.py:217
  31.3 0.9 fusion.4
  32.2 2.1 %collective-permute-start.9 = (bf16[4,4,16,1024]{3,2,1,0:T(8,128)(2,1)}, bf16[4,4,16,1024]{3,2,1,0:T(8,128)(2,1)S(1)}, u32[]{:S(2)}, u32[]{:S(2)}) collective-permute-start(bf16[4,4,16,1024]{3,2,1,0:T(8,128)(2,1)} %get-tuple-element.16), channel_id=1, source_target_pairs={{0,3},{1,0},{2,1},{3,2},{4,7},{5,4},{6,5},{7,6},{8,11},{9,8},{10,9... | collective-permute-start | bytes 1572872 | tf_op jit(solution)/shard_map/ppermute | solution.py:217
  34.2 4.8 %all-to-all-start = ((bf16[4,4,2,4,128,128]{5,4,3,2,1,0:T(8,128)(2,1)}), bf16[4,4,2,4,128,128]{5,4,3,2,1,0:T(8,128)(2,1)}, u32[]{:S(2)}, u32[]{:S(2)}) async-start(bf16[4,4,2,4,128,128]{5,4,3,2,1,0:T(8,128)(2,1)} %bitcast.39), calls=%async_computation | async-start | bytes 8388608 | tf_op jit(solution)/shard_map/all_to_all | solution.py:254
  39.1 1.4 collective-permute-done.16
  40.5 0.1 collective-permute-start.17
  40.6 3.3 %collective-permute-start.19 = (bf16[2,4,16,1024]{3,2,1,0:T(8,128)(2,1)S(1)}, bf16[2,4,16,1024]{3,2,1,0:T(8,128)(2,1)S(1)}, u32[]{:S(2)}, u32[]{:S(2)}) collective-permute-start(bf16[2,4,16,1024]{3,2,1,0:T(8,128)(2,1)S(1)} %slice.49), channel_id=1, source_target_pairs={{0,12},{4,0},{8,4},{12,8},{1,13},{5,1},{9,5},{13,9},{2,14},{6,2},{... | collective-permute-start | bytes 786440 | tf_op jit(solution)/shard_map/ppermute | solution.py:217
  43.9 2.2 %collective-permute-start.10 = (bf16[2,4,16,1024]{3,2,1,0:T(8,128)(2,1)S(1)}, bf16[2,4,16,1024]{3,2,1,0:T(8,128)(2,1)S(1)}, u32[]{:S(2)}, u32[]{:S(2)}) collective-permute-start(bf16[2,4,16,1024]{3,2,1,0:T(8,128)(2,1)S(1)} %slice.44), channel_id=1, source_target_pairs={{0,3},{1,0},{2,1},{3,2},{4,7},{5,4},{6,5},{7,6},{8,11},{9,8},{10,9... | collective-permute-start | bytes 786440 | tf_op jit(solution)/shard_map/ppermute | solution.py:217
  46.2 0.1 collective-permute-start.8
  46.3 1.9 %collective-permute-done.17 = bf16[2,4,16,1024]{3,2,1,0:T(8,128)(2,1)S(1)} collective-permute-done((bf16[2,4,16,1024]{3,2,1,0:T(8,128)(2,1)S(1)}, bf16[2,4,16,1024]{3,2,1,0:T(8,128)(2,1)S(1)}, u32[]{:S(2)}, u32[]{:S(2)}) %collective-permute-start.17) | collective-permute-done | bytes 262176 | tf_op jit(solution)/shard_map/ppermute | solution.py:217
  48.3 1.5 pad_maximum_fusion.1.here_b
  49.8 0.1 collective-permute-start.20
  49.9 0.5 collective-permute-done.10
  50.4 3.4 %collective-permute-done.8 = bf16[2,4,16,1024]{3,2,1,0:T(8,128)(2,1)S(1)} collective-permute-done((bf16[2,4,16,1024]{3,2,1,0:T(8,128)(2,1)S(1)}, bf16[2,4,16,1024]{3,2,1,0:T(8,128)(2,1)S(1)}, u32[]{:S(2)}, u32[]{:S(2)}) %collective-permute-start.8) | collective-permute-done | bytes 262176 | tf_op jit(solution)/shard_map/ppermute | solution.py:217
  53.9 0.3 pad_maximum_fusion.here_a
  54.2 0.1 collective-permute-start.11
  54.3 1.4 copy-done
  55.7 1.4 copy-done.5
  57.0 1.4 collective-permute-done.11.there_a
  58.4 1.3 copy-done.7
  59.8 24.1 %all-to-all-done.own = bf16[4,4,2,4,128,128]{5,4,3,2,1,0:T(8,128)(2,1)} async-done(((bf16[4,4,2,4,128,128]{5,4,3,2,1,0:T(8,128)(2,1)}), bf16[4,4,2,4,128,128]{5,4,3,2,1,0:T(8,128)(2,1)}, u32[]{:S(2)}, u32[]{:S(2)}) %all-to-all-start) | async-done | bytes 4194336 | tf_op jit(solution)/shard_map/all_to_all | solution.py:254
  83.9 0.1 copy.7
  84.0 0.1 reshape.33.pairs
  84.1 0.1 pad_add_fusion.place
  84.1 0.1 select_reduce_fusion
  84.3 1.6 copy-done.1
  85.9 1.6 copy-done.6
  87.5 1.6 copy-done.8
  89.1 16.6 %shard_map.46.from_own.from_other = bf16[16,1024,512]{2,1,0:T(8,128)(2,1)} custom-call(s32[4]{0:T(128)S(1)} %pad_add_fusion.place, s32[64]{0:T(128)S(1)} %reshape.33.pairs, bf16[4,4,2,4,128,128]{5,4,3,2,1,0:T(8,128)(2,1)} %all-to-all-done.own, bf16[4,4,4,16,1024]{4,3,2,1,0:T(8,128)(2,1)S(1)} %copy-done.1, bf16[4,4,4,16,1024]{4,3,2,1,0:T(8,128)(2,1)S(1)} %copy-done.8, ...), custom_call_target="tpu_custom_call" | custom-call | flops 8589934592 | bytes 33554432 | tf_op jit(solution)/shard_map/pallas_call | solution.py:82
  105.7 20.4 %shard_map.47 = bf16[1024,1536]{1,0:T(8,128)(2,1)S(1)} custom-call(s32[4]{0:T(128)S(1)} %pad_add_fusion.place, s32[64]{0:T(128)S(1)} %reshape.33.pairs, s32[16]{0:T(128)S(1)} %get-tuple-element.12.starts, s32[16]{0:T(128)S(1)} %get-tuple-element.11.shifts, s32[16]{0:T(128)S(1)} %copy-done.2, bf16[4,4,2,4,128,128]{5,4,3,2,1,0:T(8,128)(2,1)} %all-to-all-done.own, ...), custom_call_target="tpu_custom_call" | custom-call | flops 8589934592 | bytes 28311552 | tf_op jit(solution)/shard_map/pallas_call | solution.py:164
  126.1 48.4 %all_to_all.10.pieces = bf16[64,16,1536]{2,1,0:T(8,128)(2,1)} all-to-all(bf16[64,16,1536]{2,1,0:T(8,128)(2,1)S(1)} %bitcast.38), channel_id=1, replica_groups=mesh['x'=4,'core'=2,'z'=4,'y'=4] {'x','z','y'}, dimensions={0} | all-to-all | bytes 6291456 | tf_op jit(solution)/shard_map/all_to_all | solution.py:262
  174.6 3.2 %shard_map.48 = f32[16,2048]{1,0:T(8,128)} custom-call(s32[1]{0:T(128)} %bitcast.rows_live, s32[16]{0:T(128)} %copy-done.4, s32[16]{0:T(128)} %copy-done.3, s32[16]{0:T(128)} %counts.3, bf16[64,16,1536]{2,1,0:T(8,128)(2,1)} %all_to_all.10.pieces), custom_call_target="tpu_custom_call" | custom-call | tf_op jit(solution)/shard_map/pallas_call | solution.py:207
  (62 shorter events, 0.4 us)
Async XLA Ops:
  3.7 6.1 %collective-permute-start.2 = (bf16[16,2048]{1,0:T(8,128)(2,1)S(1)}, bf16[16,2048]{1,0:T(8,128)(2,1)S(1)}, u32[]{:S(2)}, u32[]{:S(2)}) collective-permute-start(bf16[16,2048]{1,0:T(8,128)(2,1)S(1)} %and_select_fusion), channel_id=1, source_target_pairs={{0,96},{32,0},{64,32},{96,64},{1,97},{33,1},{65,33},{97,65},{2,98}... | collective-permute-start | bytes 196616 | tf_op jit(solution)/shard_map/ppermute | solution.py:217
  6.6 6.2 %collective-permute-start = (bf16[16,2048]{1,0:T(8,128)(2,1)S(1)}, bf16[16,2048]{1,0:T(8,128)(2,1)S(1)}, u32[]{:S(2)}, u32[]{:S(2)}) collective-permute-start(bf16[16,2048]{1,0:T(8,128)(2,1)S(1)} %and_select_fusion), channel_id=1, source_target_pairs={{0,32},{32,64},{64,96},{96,0},{1,33},{33,65},{65,97},{97,1},{2,34}... | collective-permute-start | bytes 196616 | tf_op jit(solution)/shard_map/ppermute | solution.py:217
  6.6 6.2 %collective-permute-start.1 = (bf16[16,2048]{1,0:T(8,128)(2,1)S(1)}, bf16[16,2048]{1,0:T(8,128)(2,1)S(1)}, u32[]{:S(2)}, u32[]{:S(2)}) collective-permute-start(bf16[16,2048]{1,0:T(8,128)(2,1)S(1)} %and_select_fusion), channel_id=1, source_target_pairs={{0,64},{32,96},{64,0},{96,32},{1,65},{33,97},{65,1},{97,33},{2,66}... | collective-permute-start | bytes 196616 | tf_op jit(solution)/shard_map/ppermute | solution.py:217
  12.9 7.3 %collective-permute-start.12 = (bf16[4,16,1024]{2,1,0:T(8,128)(2,1)S(1)}, bf16[4,16,1024]{2,1,0:T(8,128)(2,1)S(1)}, u32[]{:S(2)}, u32[]{:S(2)}) collective-permute-start(bf16[4,16,1024]{2,1,0:T(8,128)(2,1)S(1)} %get-tuple-element.19), channel_id=1, source_target_pairs={{0,1},{1,2},{2,3},{3,0},{4,5},{5,6},{6,7},{7,4},{8,9},{9,10},{10,1... | collective-permute-start | bytes 393224 | tf_op jit(solution)/shard_map/ppermute | solution.py:217
  14.6 6.2 %collective-permute-start.14 = (bf16[4,16,1024]{2,1,0:T(8,128)(2,1)S(1)}, bf16[4,16,1024]{2,1,0:T(8,128)(2,1)S(1)}, u32[]{:S(2)}, u32[]{:S(2)}) collective-permute-start(bf16[4,16,1024]{2,1,0:T(8,128)(2,1)S(1)} %get-tuple-element.19), channel_id=1, source_target_pairs={{0,3},{1,0},{2,1},{3,2},{4,7},{5,4},{6,5},{7,6},{8,11},{9,8},{10,9... | collective-permute-start | bytes 393224 | tf_op jit(solution)/shard_map/ppermute | solution.py:217
  16.3 7.4 %collective-permute-start.3 = (bf16[4,16,1024]{2,1,0:T(8,128)(2,1)S(1)}, bf16[4,16,1024]{2,1,0:T(8,128)(2,1)S(1)}, u32[]{:S(2)}, u32[]{:S(2)}) collective-permute-start(bf16[4,16,1024]{2,1,0:T(8,128)(2,1)S(1)} %get-tuple-element.20), channel_id=1, source_target_pairs={{0,4},{4,8},{8,12},{12,0},{1,5},{5,9},{9,13},{13,1},{2,6},{6,10},{... | collective-permute-start | bytes 393224 | tf_op jit(solution)/shard_map/ppermute | solution.py:217
  18.2 6.3 %collective-permute-start.5 = (bf16[4,16,1024]{2,1,0:T(8,128)(2,1)S(1)}, bf16[4,16,1024]{2,1,0:T(8,128)(2,1)S(1)}, u32[]{:S(2)}, u32[]{:S(2)}) collective-permute-start(bf16[4,16,1024]{2,1,0:T(8,128)(2,1)S(1)} %get-tuple-element.20), channel_id=1, source_target_pairs={{0,12},{4,0},{8,4},{12,8},{1,13},{5,1},{9,5},{13,9},{2,14},{6,2},{... | collective-permute-start | bytes 393224 | tf_op jit(solution)/shard_map/ppermute | solution.py:217
  20.3 6.8 %collective-permute-start.13 = (bf16[2,16,1024]{2,1,0:T(8,128)(2,1)S(1)}, bf16[2,16,1024]{2,1,0:T(8,128)(2,1)S(1)}, u32[]{:S(2)}, u32[]{:S(2)}) collective-permute-start(bf16[2,16,1024]{2,1,0:T(8,128)(2,1)S(1)} %slice.46), channel_id=1, source_target_pairs={{0,1},{1,2},{2,3},{3,0},{4,5},{5,6},{6,7},{7,4},{8,9},{9,10},{10,1... | collective-permute-start | bytes 196616 | tf_op jit(solution)/shard_map/ppermute | solution.py:217
  20.8 6.3 %collective-permute-start.15 = (bf16[2,16,1024]{2,1,0:T(8,128)(2,1)S(1)}, bf16[2,16,1024]{2,1,0:T(8,128)(2,1)S(1)}, u32[]{:S(2)}, u32[]{:S(2)}) collective-permute-start(bf16[2,16,1024]{2,1,0:T(8,128)(2,1)S(1)} %slice.47), channel_id=1, source_target_pairs={{0,3},{1,0},{2,1},{3,2},{4,7},{5,4},{6,5},{7,6},{8,11},{9,8},{10,9... | collective-permute-start | bytes 196616 | tf_op jit(solution)/shard_map/ppermute | solution.py:217
  23.7 7.5 %collective-permute-start.4 = (bf16[2,16,1024]{2,1,0:T(8,128)(2,1)S(1)}, bf16[2,16,1024]{2,1,0:T(8,128)(2,1)S(1)}, u32[]{:S(2)}, u32[]{:S(2)}) collective-permute-start(bf16[2,16,1024]{2,1,0:T(8,128)(2,1)S(1)} %slice.41), channel_id=1, source_target_pairs={{0,4},{4,8},{8,12},{12,0},{1,5},{5,9},{9,13},{13,1},{2,6},{6,10},{... | collective-permute-start | bytes 196616 | tf_op jit(solution)/shard_map/ppermute | solution.py:217
  24.5 6.7 %collective-permute-start.6 = (bf16[2,16,1024]{2,1,0:T(8,128)(2,1)S(1)}, bf16[2,16,1024]{2,1,0:T(8,128)(2,1)S(1)}, u32[]{:S(2)}, u32[]{:S(2)}) collective-permute-start(bf16[2,16,1024]{2,1,0:T(8,128)(2,1)S(1)} %slice.42), channel_id=1, source_target_pairs={{0,12},{4,0},{8,4},{12,8},{1,13},{5,1},{9,5},{13,9},{2,14},{6,2},{... | collective-permute-start | bytes 196616 | tf_op jit(solution)/shard_map/ppermute | solution.py:217
  28.0 12.5 %collective-permute-start.16 = (bf16[4,4,16,1024]{3,2,1,0:T(8,128)(2,1)}, bf16[4,4,16,1024]{3,2,1,0:T(8,128)(2,1)S(1)}, u32[]{:S(2)}, u32[]{:S(2)}) collective-permute-start(bf16[4,4,16,1024]{3,2,1,0:T(8,128)(2,1)} %get-tuple-element.14), channel_id=1, source_target_pairs={{0,4},{4,8},{8,12},{12,0},{1,5},{5,9},{9,13},{13,1},{2,6},{6,10},{... | collective-permute-start | bytes 1572872 | tf_op jit(solution)/shard_map/ppermute | solution.py:217
  28.0 12.6 %collective-permute-start.18 = (bf16[4,4,16,1024]{3,2,1,0:T(8,128)(2,1)}, bf16[4,4,16,1024]{3,2,1,0:T(8,128)(2,1)S(1)}, u32[]{:S(2)}, u32[]{:S(2)}) collective-permute-start(bf16[4,4,16,1024]{3,2,1,0:T(8,128)(2,1)} %get-tuple-element.14), channel_id=1, source_target_pairs={{0,12},{4,0},{8,4},{12,8},{1,13},{5,1},{9,5},{13,9},{2,14},{6,2},{... | collective-permute-start | bytes 1572872 | tf_op jit(solution)/shard_map/ppermute | solution.py:217
  32.2 11.8 %collective-permute-start.9 = (bf16[4,4,16,1024]{3,2,1,0:T(8,128)(2,1)}, bf16[4,4,16,1024]{3,2,1,0:T(8,128)(2,1)S(1)}, u32[]{:S(2)}, u32[]{:S(2)}) collective-permute-start(bf16[4,4,16,1024]{3,2,1,0:T(8,128)(2,1)} %get-tuple-element.16), channel_id=1, source_target_pairs={{0,3},{1,0},{2,1},{3,2},{4,7},{5,4},{6,5},{7,6},{8,11},{9,8},{10,9... | collective-permute-start | bytes 1572872 | tf_op jit(solution)/shard_map/ppermute | solution.py:217
  34.2 11.9 %collective-permute-start.7 = (bf16[4,4,16,1024]{3,2,1,0:T(8,128)(2,1)}, bf16[4,4,16,1024]{3,2,1,0:T(8,128)(2,1)S(1)}, u32[]{:S(2)}, u32[]{:S(2)}) collective-permute-start(bf16[4,4,16,1024]{3,2,1,0:T(8,128)(2,1)} %get-tuple-element.16), channel_id=1, source_target_pairs={{0,1},{1,2},{2,3},{3,0},{4,5},{5,6},{6,7},{7,4},{8,9},{9,10},{10,1... | collective-permute-start | bytes 1572872 | tf_op jit(solution)/shard_map/ppermute | solution.py:217
  34.2 49.6 %all-to-all-start = ((bf16[4,4,2,4,128,128]{5,4,3,2,1,0:T(8,128)(2,1)}), bf16[4,4,2,4,128,128]{5,4,3,2,1,0:T(8,128)(2,1)}, u32[]{:S(2)}, u32[]{:S(2)}) async-start(bf16[4,4,2,4,128,128]{5,4,3,2,1,0:T(8,128)(2,1)} %bitcast.39), calls=%async_computation | async-start | bytes 8388608 | tf_op jit(solution)/shard_map/all_to_all | solution.py:254
  40.5 7.7 %copy-start.9 = (bf16[4,4,16,1024]{3,2,1,0:T(8,128)(2,1)}, bf16[4,4,16,1024]{3,2,1,0:T(8,128)(2,1)S(1)}, u32[]{:S(2)}) copy-start(bf16[4,4,16,1024]{3,2,1,0:T(8,128)(2,1)S(1)} %collective-permute-done.16) | copy-start | bytes 1572868
  40.5 7.7 %collective-permute-start.17 = (bf16[2,4,16,1024]{3,2,1,0:T(8,128)(2,1)S(1)}, bf16[2,4,16,1024]{3,2,1,0:T(8,128)(2,1)S(1)}, u32[]{:S(2)}, u32[]{:S(2)}) collective-permute-start(bf16[2,4,16,1024]{3,2,1,0:T(8,128)(2,1)S(1)} %slice.48), channel_id=1, source_target_pairs={{0,4},{4,8},{8,12},{12,0},{1,5},{5,9},{9,13},{13,1},{2,6},{6,10},{... | collective-permute-start | bytes 786440 | tf_op jit(solution)/shard_map/ppermute | solution.py:217
  40.6 7.6 %copy-start.10 = (bf16[4,4,16,1024]{3,2,1,0:T(8,128)(2,1)}, bf16[4,4,16,1024]{3,2,1,0:T(8,128)(2,1)S(1)}, u32[]{:S(2)}) copy-start(bf16[4,4,16,1024]{3,2,1,0:T(8,128)(2,1)S(1)} %collective-permute-done.18) | copy-start | bytes 1572868
  40.6 7.5 %collective-permute-start.19 = (bf16[2,4,16,1024]{3,2,1,0:T(8,128)(2,1)S(1)}, bf16[2,4,16,1024]{3,2,1,0:T(8,128)(2,1)S(1)}, u32[]{:S(2)}, u32[]{:S(2)}) collective-permute-start(bf16[2,4,16,1024]{3,2,1,0:T(8,128)(2,1)S(1)} %slice.49), channel_id=1, source_target_pairs={{0,12},{4,0},{8,4},{12,8},{1,13},{5,1},{9,5},{13,9},{2,14},{6,2},{... | collective-permute-start | bytes 786440 | tf_op jit(solution)/shard_map/ppermute | solution.py:217
  43.9 4.3 %copy-start.11 = (bf16[4,4,16,1024]{3,2,1,0:T(8,128)(2,1)}, bf16[4,4,16,1024]{3,2,1,0:T(8,128)(2,1)S(1)}, u32[]{:S(2)}) copy-start(bf16[4,4,16,1024]{3,2,1,0:T(8,128)(2,1)S(1)} %collective-permute-done.9) | copy-start | bytes 1572868
  43.9 6.4 %collective-permute-start.10 = (bf16[2,4,16,1024]{3,2,1,0:T(8,128)(2,1)S(1)}, bf16[2,4,16,1024]{3,2,1,0:T(8,128)(2,1)S(1)}, u32[]{:S(2)}, u32[]{:S(2)}) collective-permute-start(bf16[2,4,16,1024]{3,2,1,0:T(8,128)(2,1)S(1)} %slice.44), channel_id=1, source_target_pairs={{0,3},{1,0},{2,1},{3,2},{4,7},{5,4},{6,5},{7,6},{8,11},{9,8},{10,9... | collective-permute-start | bytes 786440 | tf_op jit(solution)/shard_map/ppermute | solution.py:217
  46.2 2.1 %copy-start.13 = (bf16[4,4,16,1024]{3,2,1,0:T(8,128)(2,1)}, bf16[4,4,16,1024]{3,2,1,0:T(8,128)(2,1)S(1)}, u32[]{:S(2)}) copy-start(bf16[4,4,16,1024]{3,2,1,0:T(8,128)(2,1)S(1)} %collective-permute-done.7) | copy-start | bytes 1572868
  46.2 7.7 %collective-permute-start.8 = (bf16[2,4,16,1024]{3,2,1,0:T(8,128)(2,1)S(1)}, bf16[2,4,16,1024]{3,2,1,0:T(8,128)(2,1)S(1)}, u32[]{:S(2)}, u32[]{:S(2)}) collective-permute-start(bf16[2,4,16,1024]{3,2,1,0:T(8,128)(2,1)S(1)} %slice.43), channel_id=1, source_target_pairs={{0,1},{1,2},{2,3},{3,0},{4,5},{5,6},{6,7},{7,4},{8,9},{9,10},{10,1... | collective-permute-start | bytes 786440 | tf_op jit(solution)/shard_map/ppermute | solution.py:217
  48.3 5.6 %copy-start.12 = (bf16[4,4,16,1024]{3,2,1,0:T(8,128)(2,1)S(1)}, bf16[4,4,16,1024]{3,2,1,0:T(8,128)(2,1)}, u32[]{:S(2)}) copy-start(bf16[4,4,16,1024]{3,2,1,0:T(8,128)(2,1)} %copy-done.11) | copy-start | bytes 1572868
  48.3 5.6 %copy-start.14 = (bf16[4,4,16,1024]{3,2,1,0:T(8,128)(2,1)S(1)}, bf16[4,4,16,1024]{3,2,1,0:T(8,128)(2,1)}, u32[]{:S(2)}) copy-start(bf16[4,4,16,1024]{3,2,1,0:T(8,128)(2,1)} %copy-done.13) | copy-start | bytes 1572868
  49.8 5.8 %collective-permute-start.20 = (bf16[4,4,4,16,1024]{4,3,2,1,0:T(8,128)(2,1)S(1)}, bf16[4,4,4,16,1024]{4,3,2,1,0:T(8,128)(2,1)S(1)}, u32[]{:S(2)}, u32[]{:S(2)}) collective-permute-start(bf16[4,4,4,16,1024]{4,3,2,1,0:T(8,128)(2,1)S(1)} %pad_maximum_fusion.1.here_b), channel_id=1, source_target_pairs={{0,16},{16,0},{1,17},{17,1},{2,18},{18,2},{3,19},{19,3},{4,20},{20... | collective-permute-start | bytes 6291464 | tf_op jit(solution)/shard_map/ppermute | solution.py:221
  53.9 30.0 %copy-start.15 = (s32[16,4]{0,1:T(4,128)S(1)}, s32[16,4]{0,1:T(4,128)}, u32[]{:S(2)}) copy-start(s32[16,4]{0,1:T(4,128)} %param.6) | copy-start | bytes 772
  53.9 30.2 %copy-start.2 = (s32[16]{0:T(128)S(1)}, s32[16]{0:T(128)}, u32[]{:S(2)}) copy-start(s32[16]{0:T(128)} %counts.3) | copy-start | bytes 196
  54.2 4.2 %collective-permute-start.11 = (bf16[4,4,4,16,1024]{4,3,2,1,0:T(8,128)(2,1)S(1)}, bf16[4,4,4,16,1024]{4,3,2,1,0:T(8,128)(2,1)S(1)}, u32[]{:S(2)}, u32[]{:S(2)}) collective-permute-start(bf16[4,4,4,16,1024]{4,3,2,1,0:T(8,128)(2,1)S(1)} %pad_maximum_fusion.here_a), channel_id=1, source_target_pairs={{0,16},{16,0},{1,17},{17,1},{2,18},{18,2},{3,19},{19,3},{4,20},{20... | collective-permute-start | bytes 6291464 | tf_op jit(solution)/shard_map/ppermute | solution.py:221
  54.3 1.4 copy-start
  55.7 1.4 copy-start.5
  58.4 1.3 copy-start.7
  83.9 21.8 %collective-permute-start.21 = (bf16[4,4,2,4,128,128]{5,4,3,2,1,0:T(8,128)(2,1)}, bf16[4,4,2,4,128,128]{5,4,3,2,1,0:T(8,128)(2,1)}, u32[]{:S(2)}, u32[]{:S(2)}) collective-permute-start(bf16[4,4,2,4,128,128]{5,4,3,2,1,0:T(8,128)(2,1)} %all-to-all-done.own), channel_id=1, source_target_pairs={{0,16},{16,0},{1,17},{17,1},{2,18},{18,2},{3,19},{19,3},{4,20},{20... | collective-permute-start | bytes 12582920 | tf_op jit(solution)/shard_map/ppermute | solution.py:221
  84.3 1.6 copy-start.1
  85.9 1.6 copy-start.6
  87.5 1.6 copy-start.8
  89.1 16.6 %copy-start.3 = (s32[16]{0:T(128)}, s32[16]{0:T(128)S(1)}, u32[]{:S(2)}) copy-start(s32[16]{0:T(128)S(1)} %get-tuple-element.11.shifts) | copy-start | bytes 196
  89.1 16.6 %copy-start.4 = (s32[16]{0:T(128)}, s32[16]{0:T(128)S(1)}, u32[]{:S(2)}) copy-start(s32[16]{0:T(128)S(1)} %get-tuple-element.12.starts) | copy-start | bytes 196

commit v4 on v3

--- a/solution.py
+++ b/solution.py
@@ -1,3 +1,5 @@
+import functools
+
 import jax
 import jax.numpy as jnp
 from jax import lax
@@ -22,30 +24,21 @@
     )
 
 
-def halfway_kernel(place, pairs, own, here_a, there_a, here_b, there_b, out_ref, density, sems):
+def halfway_kernel(y_first, place, pairs, own, here_hbm, there_hbm, out_ref, density, sems):
     _, aux, per_source, neigh, size, _ = own.shape
     piece = density.shape[-2]
-    half, source = pl.program_id(0), pl.program_id(1)
+    source = pl.program_id(0)
     x, core, z, y = place[0], place[1], place[2], place[3]
 
-    def copies(here, there, first):
-        return [
-            pltpu.make_async_copy(here, density.at[first // 2, 0], sems.at[first]),
-            pltpu.make_async_copy(there, density.at[first // 2, 1], sems.at[first + 1]),
+    @pl.when(source == 0)
+    def _():
+        copies = [
+            pltpu.make_async_copy(here_hbm, density.at[0], sems.at[0]),
+            pltpu.make_async_copy(there_hbm, density.at[1], sems.at[1]),
         ]
-
-    copies_a, copies_b = copies(here_a, there_a, 0), copies(here_b, there_b, 2)
-
-    @pl.when((half == 0) & (source == 0))
-    def _():
-        for copy in copies_a + copies_b:
+        for copy in copies:
             copy.start()
-        for copy in copies_a:
-            copy.wait()
-
-    @pl.when((half == 1) & (source == 0))
-    def _():
-        for copy in copies_b:
+        for copy in copies:
             copy.wait()
 
     for mi in range(per_source):
@@ -60,9 +53,8 @@
                 from_z = partner % per_source * (SIDE // per_source) + zy // SIDE
                 back_z = lax.rem(z - from_z + SIDE, SIDE)
                 back_y = lax.rem(y - zy % SIDE + SIDE, SIDE)
-                outer = jnp.where(half == 0, back_y, back_z)
-                inner = jnp.where(half == 0, back_z, back_y)
-                near.append(density[half, swap, outer, inner, back_x])
+                outer, inner = (back_y, back_z) if y_first else (back_z, back_y)
+                near.append(density[swap, outer, inner, back_x])
         product = jnp.dot(
             lhs, jnp.concatenate(near, axis=0), preferred_element_type=jnp.float32
         ).astype(jnp.bfloat16)
@@ -73,42 +65,42 @@
                 ]
 
 
-def halfway_rows(place, pairs, own, here_a, there_a, here_b, there_b):
+def halfway_rows(y_first, place, pairs, own, here, there):
     sources, aux, per_source, neigh, size, _ = own.shape
-    width = here_a.shape[-1]
-    blocks = 2 * width // size
+    width = here.shape[-1]
+    blocks = width // size
     rows = sources * per_source * size
     anywhere = pl.BlockSpec(memory_space=pl.ANY)
     return pl.pallas_call(
-        halfway_kernel,
+        functools.partial(halfway_kernel, y_first),
         out_shape=jax.ShapeDtypeStruct((blocks, rows, aux * size), jnp.bfloat16),
         grid_spec=pltpu.PrefetchScalarGridSpec(
             num_scalar_prefetch=2,
-            grid=(2, sources),
+            grid=(sources,),
             in_specs=[
-                pl.BlockSpec((1,) + own.shape[1:], lambda h, s, *_: (s, 0, 0, 0, 0, 0)),
-            ] + [anywhere] * 4,
-            out_specs=pl.BlockSpec(
-                (blocks // 2, per_source * size, aux * size), lambda h, s, *_: (h, s, 0)
-            ),
+                pl.BlockSpec((1,) + own.shape[1:], lambda s, *_: (s, 0, 0, 0, 0, 0)),
+                anywhere,
+                anywhere,
+            ],
+            out_specs=pl.BlockSpec((blocks, per_source * size, aux * size), lambda s, *_: (0, s, 0)),
             scratch_shapes=[
-                pltpu.VMEM((2, CORES) + here_a.shape, jnp.bfloat16),
-                pltpu.SemaphoreType.DMA((4,)),
+                pltpu.VMEM((CORES,) + here.shape, jnp.bfloat16),
+                pltpu.SemaphoreType.DMA((CORES,)),
             ],
         ),
-        compiler_params=pltpu.CompilerParams(vmem_limit_bytes=36 << 20),
+        compiler_params=pltpu.CompilerParams(vmem_limit_bytes=20 << 20),
         cost_estimate=pl.CostEstimate(
-            flops=2 * rows * aux * neigh * size * 2 * width,
-            bytes_accessed=4 * own.size + 8 * here_a.size + 2 * blocks * rows * aux * size,
+            flops=2 * rows * aux * neigh * size * width,
+            bytes_accessed=2 * own.size + 4 * here.size + 2 * blocks * rows * aux * size,
             transcendentals=0,
         ),
-    )(place, pairs, own, here_a, there_a, here_b, there_b)
-
-
-def exchange_kernel(place, pairs, starts, shifts, counts, own, other, from_own, from_other,
-                    out_ref, total):
+    )(place, pairs, own, here, there)
+
+
+def exchange_kernel(place, pairs, starts, shifts, counts, own, other, own_a, other_a,
+                    own_b, other_b, out_ref, total):
     _, aux, _, neigh, size, _ = own.shape
-    _, rows, _ = from_own.shape
+    _, rows, _ = own_a.shape
     step = pl.program_id(0)
     per_source = pl.num_programs(0) // SIDE
 
@@ -116,7 +108,7 @@
     def _():
         total[...] = jnp.zeros_like(total)
 
-    for which, tensor, halfway in ((place[1], own, from_own), (1 - place[1], other, from_other)):
+    def add_in(which, tensor, halfway):
         block = (step // per_source * CORES + which) * per_source + step % per_source
         rhs = stacked(tensor, 0, 0, aux, neigh)
         for r in range(0, rows, PIECE):
@@ -125,6 +117,16 @@
                 total[pairs[block * neigh + j], r : r + PIECE] += product[
                     :, j * size : (j + 1) * size
                 ]
+
+    @pl.when(step < pl.num_programs(0) // 2)
+    def _():
+        add_in(place[1], own, own_a)
+        add_in(1 - place[1], other, other_a)
+
+    @pl.when(step >= pl.num_programs(0) // 2)
+    def _():
+        add_in(place[1], own, own_b)
+        add_in(1 - place[1], other, other_b)
 
     @pl.when(step == pl.num_programs(0) - 1)
     def _():
@@ -146,17 +148,19 @@
         lax.fori_loop(0, total.shape[0], pack, 0)
 
 
-def exchange_rows(place, pairs, starts, shifts, counts, own, other, halfway):
+def exchange_rows(place, pairs, starts, shifts, counts, own, other, halfway_a, halfway_b):
     sources, aux, per_source, neigh, size, _ = own.shape
-    blocks, rows, _ = halfway.shape
+    half, rows, _ = halfway_a.shape
+    blocks = 2 * half
 
     def tensor_map(i, *_):
         return (i // per_source, 0, i % per_source, 0, 0, 0)
 
-    def halfway_map(swap):
+    def halfway_map(swap, first):
         def at(i, place, *_):
             which = place[1] if swap == 0 else 1 - place[1]
-            return ((i // per_source * CORES + which) * per_source + i % per_source, 0, 0)
+            block = (i // per_source * CORES + which) * per_source + i % per_source - first
+            return (jnp.clip(block, 0, half - 1), 0, 0)
 
         return at
 
@@ -168,18 +172,20 @@
             num_scalar_prefetch=5,
             grid=(sources * per_source,),
             in_specs=[tensor, tensor] + [
-                pl.BlockSpec((1, rows, aux * size), halfway_map(swap)) for swap in range(CORES)
+                pl.BlockSpec((1, rows, aux * size), halfway_map(swap, first))
+                for first in (0, half)
+                for swap in range(CORES)
             ],
             out_specs=pl.BlockSpec((rows, LIVE), lambda i, *_: (0, 0)),
             scratch_shapes=[pltpu.VMEM((blocks, rows, size), jnp.float32)],
         ),
-        compiler_params=pltpu.CompilerParams(vmem_limit_bytes=36 << 20),
+        compiler_params=pltpu.CompilerParams(vmem_limit_bytes=32 << 20),
         cost_estimate=pl.CostEstimate(
             flops=2 * rows * aux * neigh * size * blocks * size,
-            bytes_accessed=4 * own.size + 2 * halfway.size + 2 * rows * LIVE,
+            bytes_accessed=4 * own.size + 4 * halfway_a.size + 2 * rows * LIVE,
             transcendentals=0,
         ),
-    )(place, pairs, starts, shifts, counts, own, other, halfway, halfway)
+    )(place, pairs, starts, shifts, counts, own, other, halfway_a, halfway_a, halfway_b, halfway_b)
 
 
 def finish_kernel(rows_live, starts, shifts, counts, pieces, out_ref, summed):
@@ -246,19 +252,26 @@
 
     kept = jnp.where(live, density, 0)
     lines = jnp.stack([kept] + [moved(kept, "x", s) for s in range(1, SIDE)])
+    lines, three_index = lax.optimization_barrier((lines, three_index))
     here_a = ring(ring(lines[..., : basis // 2], "z"), "y")
     here_b = ring(ring(lines[..., basis // 2 :], "y"), "z")
-    there_a, there_b = swapped(here_a), swapped(here_b)
 
     parted = three_index.reshape(SIDE, aux_here // SIDE, own_blocks, neigh, size, size)
     own = lax.all_to_all(parted, "x", 0, 0, tiled=True)
-    own, there_a, there_b = lax.optimization_barrier((own, there_a, there_b))
-    other = swapped(own)
+    own, here_a, here_b = lax.optimization_barrier((own, here_a, here_b))
+    there_a = swapped(here_a)
+    there_a, here_b = lax.optimization_barrier((there_a, here_b))
+    there_b = swapped(here_b)
 
     place = jnp.stack([x, core, z, y]).astype(jnp.int32)
     pairs = pair_blocks.reshape(-1)
-    halfway = halfway_rows(place, pairs, own, here_a, there_a, here_b, there_b)
-    partial = exchange_rows(place, pairs, starts, shifts, basis_counts, own, other, halfway)
+    halfway_a = halfway_rows(True, place, pairs, own, here_a, there_a)
+    halfway_a, there_b, sent = lax.optimization_barrier((halfway_a, there_b, own))
+    other = swapped(sent)
+    halfway_b = halfway_rows(False, place, pairs, own, here_b, there_b)
+    partial = exchange_rows(
+        place, pairs, starts, shifts, basis_counts, own, other, halfway_a, halfway_b
+    )
     pieces = lax.all_to_all(partial.reshape(-1, rows_here, LIVE), ("x", "z", "y"), 0, 0, tiled=True)
     return finish(rows_live.astype(jnp.int32).reshape(1), starts, shifts, basis_counts, pieces, basis)
 

time: 179 us -> 171 us (0.955)
  waiting for transfers between devices: 35.8 us -> 26.7 us
  blocking collectives: 48.4 us -> 50.9 us
    all_to_all x1, waiting for transfers between devices: 24.1 us -> 5.94 us  [per_device(): own = lax.all_to_all(parted, 'x', 0, 0, tiled=True)]
    ppermute x19, waiting for transfers between devices: 10.3 us -> 16.4 us  [moved(): lax.ppermute(value, axis, [(k, (k + shift) % SIDE) for k in range(SIDE)])]
    ppermute x3, waiting for transfers between devices: 1.4 us -> 4.37 us  [swapped(): return lax.ppermute(value, 'core', [(0, 1), (1, 0)])]
    all_to_all x1, blocking collectives: 48.4 us -> 50.9 us  [per_device(): lax.all_to_all(partial.reshape(-1, rows_here, LIVE), ('x', 'z', 'y'), 0,...]
    unnamed x33 -> x17, local copies, waits for them, and re-layouts: 8.96 us -> 7.91 us
    pallas_call x1 -> x2, Pallas kernels: 16.6 us -> 17.3 us  [halfway_rows(): pl.pallas_call(functools.partial(halfway_kernel, y_first), out_shape=jax....]
  transfers between devices with their start and end apart: 23 -> 23, of which waited for: 7 -> 8; matrix products, arithmetic and copies ran while one was open for 3% -> 2% of each run, Pallas kernels for 9% -> 10%
where the time goes in v4:
time: 171 us; the launch traced here: 170 us
  blocking collectives  50.9 us (30%)
  Pallas kernels  40.6 us (24%)
  starting transfers between devices  36.6 us (21%)
  waiting for transfers between devices  26.7 us (16%)
  local copies, waits for them, and re-layouts  8.13 us (5%)
  other arithmetic  6.26 us (4%)
    all_to_all x1, blocking collectives, per_device(): lax.all_to_all(partial.reshape(-1, rows_here, LIVE), ('x', 'z', 'y'), 0,...  50.9 us
    ppermute x19, starting transfers between devices, moved(): lax.ppermute(value, axis, [(k, (k + shift) % SIDE) for k in range(SIDE)])  30.9 us
    pallas_call x1, Pallas kernels, exchange_rows(): pl.pallas_call(exchange_kernel, out_shape=jax.ShapeDtypeStruct((rows, LIV...  20.2 us
    pallas_call x2, Pallas kernels, halfway_rows(): pl.pallas_call(functools.partial(halfway_kernel, y_first), out_shape=jax....  17.3 us
    ppermute x19, waiting for transfers between devices, moved(): lax.ppermute(value, axis, [(k, (k + shift) % SIDE) for k in range(SIDE)])  16.4 us
    unnamed x17, local copies, waits for them, and re-layouts  7.91 us
    all_to_all x1, waiting for transfers between devices, per_device(): own = lax.all_to_all(parted, 'x', 0, 0, tiled=True)  5.94 us
    all_to_all x1, starting transfers between devices, per_device(): own = lax.all_to_all(parted, 'x', 0, 0, tiled=True)  4.93 us
  transfers between devices with their start and end apart: 23, of which 8 were waited for; matrix products, arithmetic and copies ran while one was open for 2% of the time, Pallas kernels for 10%

profile of v4, /device:TPU:0, one launch (start us, length us, event | category | flops | bytes accessed | tf_op | source)
XLA Modules:
  0.0 169.9 jit_solution(123039683445283348)
XLA Ops:
  0.0 0.7 fusion
  0.7 1.3 fusion.1
  2.6 0.9 and_select_fusion
  3.5 1.6 collective-permute-start
  5.2 2.7 %collective-permute-start.1 = (bf16[16,2048]{1,0:T(8,128)(2,1)S(1)}, bf16[16,2048]{1,0:T(8,128)(2,1)S(1)}, u32[]{:S(2)}, u32[]{:S(2)}) collective-permute-start(bf16[16,2048]{1,0:T(8,128)(2,1)S(1)} %and_select_fusion), channel_id=1, source_target_pairs={{0,64},{32,96},{64,0},{96,32},{1,65},{33,97},{65,1},{97,33},{2,66}... | collective-permute-start | bytes 196616 | tf_op jit(solution)/shard_map/ppermute | solution.py:223
  7.9 1.4 collective-permute-start.2
  9.4 0.9 fusion.6
  10.3 0.8 collective-permute-done.1
  11.1 1.1 collective-permute-done.2
  12.2 4.9 %all-to-all-start = ((bf16[4,4,2,4,128,128]{5,4,3,2,1,0:T(8,128)(2,1)}), bf16[4,4,2,4,128,128]{5,4,3,2,1,0:T(8,128)(2,1)}, u32[]{:S(2)}, u32[]{:S(2)}) async-start(bf16[4,4,2,4,128,128]{5,4,3,2,1,0:T(8,128)(2,1)} %bitcast.39), calls=%async_computation | async-start | bytes 8388608 | tf_op jit(solution)/shard_map/all_to_all | solution.py:260
  17.2 1.6 collective-permute-start.11
  18.9 1.7 collective-permute-start.13
  20.5 1.9 %collective-permute-start.3 = (bf16[4,16,1024]{2,1,0:T(8,128)(2,1)S(1)}, bf16[4,16,1024]{2,1,0:T(8,128)(2,1)S(1)}, u32[]{:S(2)}, u32[]{:S(2)}) collective-permute-start(bf16[4,16,1024]{2,1,0:T(8,128)(2,1)S(1)} %get-tuple-element.34), channel_id=1, source_target_pairs={{0,4},{4,8},{8,12},{12,0},{1,5},{5,9},{9,13},{13,1},{2,6},{6,10},{... | collective-permute-start | bytes 393224 | tf_op jit(solution)/shard_map/ppermute | solution.py:223
  22.4 2.1 %collective-permute-start.5 = (bf16[4,16,1024]{2,1,0:T(8,128)(2,1)S(1)}, bf16[4,16,1024]{2,1,0:T(8,128)(2,1)S(1)}, u32[]{:S(2)}, u32[]{:S(2)}) collective-permute-start(bf16[4,16,1024]{2,1,0:T(8,128)(2,1)S(1)} %get-tuple-element.34), channel_id=1, source_target_pairs={{0,12},{4,0},{8,4},{12,8},{1,13},{5,1},{9,5},{13,9},{2,14},{6,2},{... | collective-permute-start | bytes 393224 | tf_op jit(solution)/shard_map/ppermute | solution.py:223
  24.6 0.4 collective-permute-start.12
  25.0 2.9 %collective-permute-start.14 = (bf16[2,16,1024]{2,1,0:T(8,128)(2,1)S(1)}, bf16[2,16,1024]{2,1,0:T(8,128)(2,1)S(1)}, u32[]{:S(2)}, u32[]{:S(2)}) collective-permute-start(bf16[2,16,1024]{2,1,0:T(8,128)(2,1)S(1)} %slice.45), channel_id=1, source_target_pairs={{0,3},{1,0},{2,1},{3,2},{4,7},{5,4},{6,5},{7,6},{8,11},{9,8},{10,9... | collective-permute-start | bytes 196616 | tf_op jit(solution)/shard_map/ppermute | solution.py:223
  28.0 0.8 collective-permute-start.4
  28.8 2.6 %collective-permute-start.6 = (bf16[2,16,1024]{2,1,0:T(8,128)(2,1)S(1)}, bf16[2,16,1024]{2,1,0:T(8,128)(2,1)S(1)}, u32[]{:S(2)}, u32[]{:S(2)}) collective-permute-start(bf16[2,16,1024]{2,1,0:T(8,128)(2,1)S(1)} %slice.41), channel_id=1, source_target_pairs={{0,12},{4,0},{8,4},{12,8},{1,13},{5,1},{9,5},{13,9},{2,14},{6,2},{... | collective-permute-start | bytes 196616 | tf_op jit(solution)/shard_map/ppermute | solution.py:223
  31.4 0.1 fusion.3
  31.6 3.2 %collective-permute-start.17 = (bf16[4,4,16,1024]{3,2,1,0:T(8,128)(2,1)S(1)}, bf16[4,4,16,1024]{3,2,1,0:T(8,128)(2,1)S(1)}, u32[]{:S(2)}, u32[]{:S(2)}) collective-permute-start(bf16[4,4,16,1024]{3,2,1,0:T(8,128)(2,1)S(1)} %get-tuple-element.28), channel_id=1, source_target_pairs={{0,12},{4,0},{8,4},{12,8},{1,13},{5,1},{9,5},{13,9},{2,14},{6,2},{... | collective-permute-start | bytes 1572872 | tf_op jit(solution)/shard_map/ppermute | solution.py:223
  34.8 0.1 fusion.4
  34.9 2.1 %collective-permute-start.9 = (bf16[4,4,16,1024]{3,2,1,0:T(8,128)(2,1)S(1)}, bf16[4,4,16,1024]{3,2,1,0:T(8,128)(2,1)S(1)}, u32[]{:S(2)}, u32[]{:S(2)}) collective-permute-start(bf16[4,4,16,1024]{3,2,1,0:T(8,128)(2,1)S(1)} %get-tuple-element.30), channel_id=1, source_target_pairs={{0,3},{1,0},{2,1},{3,2},{4,7},{5,4},{6,5},{7,6},{8,11},{9,8},{10,9... | collective-permute-start | bytes 1572872 | tf_op jit(solution)/shard_map/ppermute | solution.py:223
  37.0 7.1 %collective-permute-done.15 = bf16[4,4,16,1024]{3,2,1,0:T(8,128)(2,1)S(1)} collective-permute-done((bf16[4,4,16,1024]{3,2,1,0:T(8,128)(2,1)S(1)}, bf16[4,4,16,1024]{3,2,1,0:T(8,128)(2,1)S(1)}, u32[]{:S(2)}, u32[]{:S(2)}) %collective-permute-start.15) | collective-permute-done | bytes 524320 | tf_op jit(solution)/shard_map/ppermute | solution.py:223
  44.3 3.3 %collective-permute-start.18 = (bf16[2,4,16,1024]{3,2,1,0:T(8,128)(2,1)S(1)}, bf16[2,4,16,1024]{3,2,1,0:T(8,128)(2,1)S(1)}, u32[]{:S(2)}, u32[]{:S(2)}) collective-permute-start(bf16[2,4,16,1024]{3,2,1,0:T(8,128)(2,1)S(1)} %slice.47), channel_id=1, source_target_pairs={{0,12},{4,0},{8,4},{12,8},{1,13},{5,1},{9,5},{13,9},{2,14},{6,2},{... | collective-permute-start | bytes 786440 | tf_op jit(solution)/shard_map/ppermute | solution.py:223
  47.6 2.0 %collective-permute-start.10 = (bf16[2,4,16,1024]{3,2,1,0:T(8,128)(2,1)S(1)}, bf16[2,4,16,1024]{3,2,1,0:T(8,128)(2,1)S(1)}, u32[]{:S(2)}, u32[]{:S(2)}) collective-permute-start(bf16[2,4,16,1024]{3,2,1,0:T(8,128)(2,1)S(1)} %slice.43), channel_id=1, source_target_pairs={{0,3},{1,0},{2,1},{3,2},{4,7},{5,4},{6,5},{7,6},{8,11},{9,8},{10,9... | collective-permute-start | bytes 786440 | tf_op jit(solution)/shard_map/ppermute | solution.py:223
  49.6 0.2 collective-permute-start.8
  49.8 2.0 %collective-permute-done.16 = bf16[2,4,16,1024]{3,2,1,0:T(8,128)(2,1)S(1)} collective-permute-done((bf16[2,4,16,1024]{3,2,1,0:T(8,128)(2,1)S(1)}, bf16[2,4,16,1024]{3,2,1,0:T(8,128)(2,1)S(1)}, u32[]{:S(2)}, u32[]{:S(2)}) %collective-permute-start.16) | collective-permute-done | bytes 262176 | tf_op jit(solution)/shard_map/ppermute | solution.py:223
  51.9 2.2 %collective-permute-done.10 = bf16[2,4,16,1024]{3,2,1,0:T(8,128)(2,1)S(1)} collective-permute-done((bf16[2,4,16,1024]{3,2,1,0:T(8,128)(2,1)S(1)}, bf16[2,4,16,1024]{3,2,1,0:T(8,128)(2,1)S(1)}, u32[]{:S(2)}, u32[]{:S(2)}) %collective-permute-start.10) | collective-permute-done | bytes 262176 | tf_op jit(solution)/shard_map/ppermute | solution.py:223
  54.0 3.2 %collective-permute-done.8 = bf16[2,4,16,1024]{3,2,1,0:T(8,128)(2,1)S(1)} collective-permute-done((bf16[2,4,16,1024]{3,2,1,0:T(8,128)(2,1)S(1)}, bf16[2,4,16,1024]{3,2,1,0:T(8,128)(2,1)S(1)}, u32[]{:S(2)}, u32[]{:S(2)}) %collective-permute-start.8) | collective-permute-done | bytes 262176 | tf_op jit(solution)/shard_map/ppermute | solution.py:223
  57.3 0.3 pad_maximum_fusion.1.here_hbm
  57.5 1.6 pad_maximum_fusion.here_hbm
  59.1 5.9 %all-to-all-done.own = bf16[4,4,2,4,128,128]{5,4,3,2,1,0:T(8,128)(2,1)} async-done(((bf16[4,4,2,4,128,128]{5,4,3,2,1,0:T(8,128)(2,1)}), bf16[4,4,2,4,128,128]{5,4,3,2,1,0:T(8,128)(2,1)}, u32[]{:S(2)}, u32[]{:S(2)}) %all-to-all-start) | async-done | bytes 4194336 | tf_op jit(solution)/shard_map/all_to_all | solution.py:260
  65.1 4.4 %collective-permute-done.19.there_hbm = bf16[4,4,4,16,1024]{4,3,2,1,0:T(8,128)(2,1)S(1)} collective-permute-done((bf16[4,4,4,16,1024]{4,3,2,1,0:T(8,128)(2,1)}, bf16[4,4,4,16,1024]{4,3,2,1,0:T(8,128)(2,1)S(1)}, u32[]{:S(2)}, u32[]{:S(2)}) %collective-permute-start.19) | collective-permute-done | bytes 2097184 | tf_op jit(solution)/shard_map/ppermute | solution.py:227
  69.4 1.4 copy-done.2
  70.8 0.1 collective-permute-start.20
  70.9 0.1 copy.7
  71.0 0.1 reshape.33.pairs
  71.1 0.1 pad_add_fusion.place
  71.2 1.6 copy-done.1
  72.8 1.6 copy-done.3
  74.4 7.9 %shard_map.46.own_a.other_a = bf16[8,1024,512]{2,1,0:T(8,128)(2,1)S(1)} custom-call(s32[4]{0:T(128)S(1)} %pad_add_fusion.place, s32[64]{0:T(128)S(1)} %reshape.33.pairs, bf16[4,4,2,4,128,128]{5,4,3,2,1,0:T(8,128)(2,1)} %all-to-all-done.own, bf16[4,4,4,16,1024]{4,3,2,1,0:T(8,128)(2,1)S(1)} %copy-done.1, bf16[4,4,4,16,1024]{4,3,2,1,0:T(8,128)(2,1)S(1)} %copy-done.3), custom_call_target="tpu_custom_call" | custom-call | flops 4294967296 | bytes 16777216 | tf_op jit(solution)/shard_map/pallas_call | solution.py:74
  82.3 0.6 collective-permute-start.21
  82.9 0.1 select_reduce_fusion
  83.1 9.4 %shard_map.47.own_b.other_b = bf16[8,1024,512]{2,1,0:T(8,128)(2,1)S(1)} custom-call(s32[4]{0:T(128)S(1)} %pad_add_fusion.place, s32[64]{0:T(128)S(1)} %reshape.33.pairs, bf16[4,4,2,4,128,128]{5,4,3,2,1,0:T(8,128)(2,1)} %all-to-all-done.own, bf16[4,4,4,16,1024]{4,3,2,1,0:T(8,128)(2,1)S(1)} %pad_maximum_fusion.1.here_hbm, ...), custom_call_target="tpu_custom_call" | custom-call | flops 4294967296 | bytes 16777216 | tf_op jit(solution)/shard_map/pallas_call | solution.py:74
  92.5 3.3 %copy-done = bf16[8,1024,512]{2,1,0:T(8,128)(2,1)} copy-done((bf16[8,1024,512]{2,1,0:T(8,128)(2,1)}, bf16[8,1024,512]{2,1,0:T(8,128)(2,1)S(1)}, u32[]{:S(2)}) %copy-start) | copy-done | bytes 8388632
  95.8 20.2 %shard_map.48 = bf16[1024,1536]{1,0:T(8,128)(2,1)S(1)} custom-call(s32[4]{0:T(128)S(1)} %pad_add_fusion.place, s32[64]{0:T(128)S(1)} %reshape.33.pairs, s32[16]{0:T(128)S(1)} %get-tuple-element.26.starts, s32[16]{0:T(128)S(1)} %get-tuple-element.25.shifts, s32[16]{0:T(128)S(1)} %copy-done.4, bf16[4,4,2,4,128,128]{5,4,3,2,1,0:T(8,128)(2,1)} %all-to-all-done.own, ...), custom_call_target="tpu_custom_call" | custom-call | flops 8589934592 | bytes 28311552 | tf_op jit(solution)/shard_map/pallas_call | solution.py:168
  115.9 50.9 %all_to_all.10.pieces = bf16[64,16,1536]{2,1,0:T(8,128)(2,1)} all-to-all(bf16[64,16,1536]{2,1,0:T(8,128)(2,1)S(1)} %bitcast.38), channel_id=1, replica_groups=mesh['x'=4,'core'=2,'z'=4,'y'=4] {'x','z','y'}, dimensions={0} | all-to-all | bytes 6291456 | tf_op jit(solution)/shard_map/all_to_all | solution.py:275
  166.8 3.2 %shard_map.49 = f32[16,2048]{1,0:T(8,128)} custom-call(s32[1]{0:T(128)} %bitcast.rows_live, s32[16]{0:T(128)} %copy-done.6, s32[16]{0:T(128)} %copy-done.5, s32[16]{0:T(128)} %counts.3, bf16[64,16,1536]{2,1,0:T(8,128)(2,1)} %all_to_all.10.pieces), custom_call_target="tpu_custom_call" | custom-call | tf_op jit(solution)/shard_map/pallas_call | solution.py:213
  (47 shorter events, 0.5 us)
Async XLA Ops:
  3.5 6.7 %collective-permute-start = (bf16[16,2048]{1,0:T(8,128)(2,1)S(1)}, bf16[16,2048]{1,0:T(8,128)(2,1)S(1)}, u32[]{:S(2)}, u32[]{:S(2)}) collective-permute-start(bf16[16,2048]{1,0:T(8,128)(2,1)S(1)} %and_select_fusion), channel_id=1, source_target_pairs={{0,32},{32,64},{64,96},{96,0},{1,33},{33,65},{65,97},{97,1},{2,34}... | collective-permute-start | bytes 196616 | tf_op jit(solution)/shard_map/ppermute | solution.py:223
  5.2 5.9 %collective-permute-start.1 = (bf16[16,2048]{1,0:T(8,128)(2,1)S(1)}, bf16[16,2048]{1,0:T(8,128)(2,1)S(1)}, u32[]{:S(2)}, u32[]{:S(2)}) collective-permute-start(bf16[16,2048]{1,0:T(8,128)(2,1)S(1)} %and_select_fusion), channel_id=1, source_target_pairs={{0,64},{32,96},{64,0},{96,32},{1,65},{33,97},{65,1},{97,33},{2,66}... | collective-permute-start | bytes 196616 | tf_op jit(solution)/shard_map/ppermute | solution.py:223
  7.9 4.3 %collective-permute-start.2 = (bf16[16,2048]{1,0:T(8,128)(2,1)S(1)}, bf16[16,2048]{1,0:T(8,128)(2,1)S(1)}, u32[]{:S(2)}, u32[]{:S(2)}) collective-permute-start(bf16[16,2048]{1,0:T(8,128)(2,1)S(1)} %and_select_fusion), channel_id=1, source_target_pairs={{0,96},{32,0},{64,32},{96,64},{1,97},{33,1},{65,33},{97,65},{2,98}... | collective-permute-start | bytes 196616 | tf_op jit(solution)/shard_map/ppermute | solution.py:223
  12.2 52.8 %all-to-all-start = ((bf16[4,4,2,4,128,128]{5,4,3,2,1,0:T(8,128)(2,1)}), bf16[4,4,2,4,128,128]{5,4,3,2,1,0:T(8,128)(2,1)}, u32[]{:S(2)}, u32[]{:S(2)}) async-start(bf16[4,4,2,4,128,128]{5,4,3,2,1,0:T(8,128)(2,1)} %bitcast.39), calls=%async_computation | async-start | bytes 8388608 | tf_op jit(solution)/shard_map/all_to_all | solution.py:260
  17.2 7.3 %collective-permute-start.11 = (bf16[4,16,1024]{2,1,0:T(8,128)(2,1)S(1)}, bf16[4,16,1024]{2,1,0:T(8,128)(2,1)S(1)}, u32[]{:S(2)}, u32[]{:S(2)}) collective-permute-start(bf16[4,16,1024]{2,1,0:T(8,128)(2,1)S(1)} %get-tuple-element.33), channel_id=1, source_target_pairs={{0,1},{1,2},{2,3},{3,0},{4,5},{5,6},{6,7},{7,4},{8,9},{9,10},{10,1... | collective-permute-start | bytes 393224 | tf_op jit(solution)/shard_map/ppermute | solution.py:223
  18.9 6.2 %collective-permute-start.13 = (bf16[4,16,1024]{2,1,0:T(8,128)(2,1)S(1)}, bf16[4,16,1024]{2,1,0:T(8,128)(2,1)S(1)}, u32[]{:S(2)}, u32[]{:S(2)}) collective-permute-start(bf16[4,16,1024]{2,1,0:T(8,128)(2,1)S(1)} %get-tuple-element.33), channel_id=1, source_target_pairs={{0,3},{1,0},{2,1},{3,2},{4,7},{5,4},{6,5},{7,6},{8,11},{9,8},{10,9... | collective-permute-start | bytes 393224 | tf_op jit(solution)/shard_map/ppermute | solution.py:223
  20.5 7.4 %collective-permute-start.3 = (bf16[4,16,1024]{2,1,0:T(8,128)(2,1)S(1)}, bf16[4,16,1024]{2,1,0:T(8,128)(2,1)S(1)}, u32[]{:S(2)}, u32[]{:S(2)}) collective-permute-start(bf16[4,16,1024]{2,1,0:T(8,128)(2,1)S(1)} %get-tuple-element.34), channel_id=1, source_target_pairs={{0,4},{4,8},{8,12},{12,0},{1,5},{5,9},{9,13},{13,1},{2,6},{6,10},{... | collective-permute-start | bytes 393224 | tf_op jit(solution)/shard_map/ppermute | solution.py:223
  22.4 6.3 %collective-permute-start.5 = (bf16[4,16,1024]{2,1,0:T(8,128)(2,1)S(1)}, bf16[4,16,1024]{2,1,0:T(8,128)(2,1)S(1)}, u32[]{:S(2)}, u32[]{:S(2)}) collective-permute-start(bf16[4,16,1024]{2,1,0:T(8,128)(2,1)S(1)} %get-tuple-element.34), channel_id=1, source_target_pairs={{0,12},{4,0},{8,4},{12,8},{1,13},{5,1},{9,5},{13,9},{2,14},{6,2},{... | collective-permute-start | bytes 393224 | tf_op jit(solution)/shard_map/ppermute | solution.py:223
  24.6 6.8 %collective-permute-start.12 = (bf16[2,16,1024]{2,1,0:T(8,128)(2,1)S(1)}, bf16[2,16,1024]{2,1,0:T(8,128)(2,1)S(1)}, u32[]{:S(2)}, u32[]{:S(2)}) collective-permute-start(bf16[2,16,1024]{2,1,0:T(8,128)(2,1)S(1)} %slice.44), channel_id=1, source_target_pairs={{0,1},{1,2},{2,3},{3,0},{4,5},{5,6},{6,7},{7,4},{8,9},{9,10},{10,1... | collective-permute-start | bytes 196616 | tf_op jit(solution)/shard_map/ppermute | solution.py:223
  25.0 6.3 %collective-permute-start.14 = (bf16[2,16,1024]{2,1,0:T(8,128)(2,1)S(1)}, bf16[2,16,1024]{2,1,0:T(8,128)(2,1)S(1)}, u32[]{:S(2)}, u32[]{:S(2)}) collective-permute-start(bf16[2,16,1024]{2,1,0:T(8,128)(2,1)S(1)} %slice.45), channel_id=1, source_target_pairs={{0,3},{1,0},{2,1},{3,2},{4,7},{5,4},{6,5},{7,6},{8,11},{9,8},{10,9... | collective-permute-start | bytes 196616 | tf_op jit(solution)/shard_map/ppermute | solution.py:223
  28.0 6.8 %collective-permute-start.4 = (bf16[2,16,1024]{2,1,0:T(8,128)(2,1)S(1)}, bf16[2,16,1024]{2,1,0:T(8,128)(2,1)S(1)}, u32[]{:S(2)}, u32[]{:S(2)}) collective-permute-start(bf16[2,16,1024]{2,1,0:T(8,128)(2,1)S(1)} %slice.40), channel_id=1, source_target_pairs={{0,4},{4,8},{8,12},{12,0},{1,5},{5,9},{9,13},{13,1},{2,6},{6,10},{... | collective-permute-start | bytes 196616 | tf_op jit(solution)/shard_map/ppermute | solution.py:223
  28.8 6.0 %collective-permute-start.6 = (bf16[2,16,1024]{2,1,0:T(8,128)(2,1)S(1)}, bf16[2,16,1024]{2,1,0:T(8,128)(2,1)S(1)}, u32[]{:S(2)}, u32[]{:S(2)}) collective-permute-start(bf16[2,16,1024]{2,1,0:T(8,128)(2,1)S(1)} %slice.41), channel_id=1, source_target_pairs={{0,12},{4,0},{8,4},{12,8},{1,13},{5,1},{9,5},{13,9},{2,14},{6,2},{... | collective-permute-start | bytes 196616 | tf_op jit(solution)/shard_map/ppermute | solution.py:223
  31.5 12.7 %collective-permute-start.15 = (bf16[4,4,16,1024]{3,2,1,0:T(8,128)(2,1)S(1)}, bf16[4,4,16,1024]{3,2,1,0:T(8,128)(2,1)S(1)}, u32[]{:S(2)}, u32[]{:S(2)}) collective-permute-start(bf16[4,4,16,1024]{3,2,1,0:T(8,128)(2,1)S(1)} %get-tuple-element.28), channel_id=1, source_target_pairs={{0,4},{4,8},{8,12},{12,0},{1,5},{5,9},{9,13},{13,1},{2,6},{6,10},{... | collective-permute-start | bytes 1572872 | tf_op jit(solution)/shard_map/ppermute | solution.py:223
  31.6 12.7 %collective-permute-start.17 = (bf16[4,4,16,1024]{3,2,1,0:T(8,128)(2,1)S(1)}, bf16[4,4,16,1024]{3,2,1,0:T(8,128)(2,1)S(1)}, u32[]{:S(2)}, u32[]{:S(2)}) collective-permute-start(bf16[4,4,16,1024]{3,2,1,0:T(8,128)(2,1)S(1)} %get-tuple-element.28), channel_id=1, source_target_pairs={{0,12},{4,0},{8,4},{12,8},{1,13},{5,1},{9,5},{13,9},{2,14},{6,2},{... | collective-permute-start | bytes 1572872 | tf_op jit(solution)/shard_map/ppermute | solution.py:223
  34.9 12.6 %collective-permute-start.9 = (bf16[4,4,16,1024]{3,2,1,0:T(8,128)(2,1)S(1)}, bf16[4,4,16,1024]{3,2,1,0:T(8,128)(2,1)S(1)}, u32[]{:S(2)}, u32[]{:S(2)}) collective-permute-start(bf16[4,4,16,1024]{3,2,1,0:T(8,128)(2,1)S(1)} %get-tuple-element.30), channel_id=1, source_target_pairs={{0,3},{1,0},{2,1},{3,2},{4,7},{5,4},{6,5},{7,6},{8,11},{9,8},{10,9... | collective-permute-start | bytes 1572872 | tf_op jit(solution)/shard_map/ppermute | solution.py:223
  37.0 12.5 %collective-permute-start.7 = (bf16[4,4,16,1024]{3,2,1,0:T(8,128)(2,1)S(1)}, bf16[4,4,16,1024]{3,2,1,0:T(8,128)(2,1)S(1)}, u32[]{:S(2)}, u32[]{:S(2)}) collective-permute-start(bf16[4,4,16,1024]{3,2,1,0:T(8,128)(2,1)S(1)} %get-tuple-element.30), channel_id=1, source_target_pairs={{0,1},{1,2},{2,3},{3,0},{4,5},{5,6},{6,7},{7,4},{8,9},{9,10},{10,1... | collective-permute-start | bytes 1572872 | tf_op jit(solution)/shard_map/ppermute | solution.py:223
  44.1 7.7 %collective-permute-start.16 = (bf16[2,4,16,1024]{3,2,1,0:T(8,128)(2,1)S(1)}, bf16[2,4,16,1024]{3,2,1,0:T(8,128)(2,1)S(1)}, u32[]{:S(2)}, u32[]{:S(2)}) collective-permute-start(bf16[2,4,16,1024]{3,2,1,0:T(8,128)(2,1)S(1)} %slice.46), channel_id=1, source_target_pairs={{0,4},{4,8},{8,12},{12,0},{1,5},{5,9},{9,13},{13,1},{2,6},{6,10},{... | collective-permute-start | bytes 786440 | tf_op jit(solution)/shard_map/ppermute | solution.py:223
  44.3 7.5 %collective-permute-start.18 = (bf16[2,4,16,1024]{3,2,1,0:T(8,128)(2,1)S(1)}, bf16[2,4,16,1024]{3,2,1,0:T(8,128)(2,1)S(1)}, u32[]{:S(2)}, u32[]{:S(2)}) collective-permute-start(bf16[2,4,16,1024]{3,2,1,0:T(8,128)(2,1)S(1)} %slice.47), channel_id=1, source_target_pairs={{0,12},{4,0},{8,4},{12,8},{1,13},{5,1},{9,5},{13,9},{2,14},{6,2},{... | collective-permute-start | bytes 786440 | tf_op jit(solution)/shard_map/ppermute | solution.py:223
  47.6 6.4 %collective-permute-start.10 = (bf16[2,4,16,1024]{3,2,1,0:T(8,128)(2,1)S(1)}, bf16[2,4,16,1024]{3,2,1,0:T(8,128)(2,1)S(1)}, u32[]{:S(2)}, u32[]{:S(2)}) collective-permute-start(bf16[2,4,16,1024]{3,2,1,0:T(8,128)(2,1)S(1)} %slice.43), channel_id=1, source_target_pairs={{0,3},{1,0},{2,1},{3,2},{4,7},{5,4},{6,5},{7,6},{8,11},{9,8},{10,9... | collective-permute-start | bytes 786440 | tf_op jit(solution)/shard_map/ppermute | solution.py:223
  49.6 7.7 %collective-permute-start.8 = (bf16[2,4,16,1024]{3,2,1,0:T(8,128)(2,1)S(1)}, bf16[2,4,16,1024]{3,2,1,0:T(8,128)(2,1)S(1)}, u32[]{:S(2)}, u32[]{:S(2)}) collective-permute-start(bf16[2,4,16,1024]{3,2,1,0:T(8,128)(2,1)S(1)} %slice.42), channel_id=1, source_target_pairs={{0,1},{1,2},{2,3},{3,0},{4,5},{5,6},{6,7},{7,4},{8,9},{9,10},{10,1... | collective-permute-start | bytes 786440 | tf_op jit(solution)/shard_map/ppermute | solution.py:223
  57.5 13.4 %copy-start.7 = (s32[16,4]{0,1:T(4,128)S(1)}, s32[16,4]{0,1:T(4,128)}, u32[]{:S(2)}) copy-start(s32[16,4]{0,1:T(4,128)} %param.6) | copy-start | bytes 772
  65.0 4.4 %collective-permute-start.19 = (bf16[4,4,4,16,1024]{4,3,2,1,0:T(8,128)(2,1)}, bf16[4,4,4,16,1024]{4,3,2,1,0:T(8,128)(2,1)S(1)}, u32[]{:S(2)}, u32[]{:S(2)}) collective-permute-start(bf16[4,4,4,16,1024]{4,3,2,1,0:T(8,128)(2,1)} %pad_maximum_fusion.here_hbm), channel_id=1, source_target_pairs={{0,16},{16,0},{1,17},{17,1},{2,18},{18,2},{3,19},{19,3},{4,20},{20... | collective-permute-start | bytes 6291464 | tf_op jit(solution)/shard_map/ppermute | solution.py:227
  69.4 1.4 copy-start.2
  70.8 11.5 %collective-permute-start.20 = (bf16[4,4,4,16,1024]{4,3,2,1,0:T(8,128)(2,1)S(1)}, bf16[4,4,4,16,1024]{4,3,2,1,0:T(8,128)(2,1)}, u32[]{:S(2)}, u32[]{:S(2)}) collective-permute-start(bf16[4,4,4,16,1024]{4,3,2,1,0:T(8,128)(2,1)S(1)} %pad_maximum_fusion.1.here_hbm), channel_id=1, source_target_pairs={{0,16},{16,0},{1,17},{17,1},{2,18},{18,2},{3,19},{19,3},{4,20},{20... | collective-permute-start | bytes 6291464 | tf_op jit(solution)/shard_map/ppermute | solution.py:227
  71.2 1.6 copy-start.1
  72.8 1.6 copy-start.3
  74.4 8.6 %copy-start.4 = (s32[16]{0:T(128)S(1)}, s32[16]{0:T(128)}, u32[]{:S(2)}) copy-start(s32[16]{0:T(128)} %counts.3) | copy-start | bytes 196
  82.3 13.5 %collective-permute-start.21 = (bf16[4,4,2,4,128,128]{5,4,3,2,1,0:T(8,128)(2,1)}, bf16[4,4,2,4,128,128]{5,4,3,2,1,0:T(8,128)(2,1)S(1)}, u32[]{:S(2)}, u32[]{:S(2)}) collective-permute-start(bf16[4,4,2,4,128,128]{5,4,3,2,1,0:T(8,128)(2,1)} %all-to-all-done.own), channel_id=1, source_target_pairs={{0,16},{16,0},{1,17},{17,1},{2,18},{18,2},{3,19},{19,3},{4,20},{20... | collective-permute-start | bytes 12582920 | tf_op jit(solution)/shard_map/ppermute | solution.py:227
  83.0 12.7 %copy-start.5 = (s32[16]{0:T(128)}, s32[16]{0:T(128)S(1)}, u32[]{:S(2)}) copy-start(s32[16]{0:T(128)S(1)} %get-tuple-element.25.shifts) | copy-start | bytes 196
  83.1 12.7 %copy-start.6 = (s32[16]{0:T(128)}, s32[16]{0:T(128)S(1)}, u32[]{:S(2)}) copy-start(s32[16]{0:T(128)S(1)} %get-tuple-element.26.starts) | copy-start | bytes 196
  92.5 3.3 %copy-start = (bf16[8,1024,512]{2,1,0:T(8,128)(2,1)}, bf16[8,1024,512]{2,1,0:T(8,128)(2,1)S(1)}, u32[]{:S(2)}) copy-start(bf16[8,1024,512]{2,1,0:T(8,128)(2,1)S(1)} %shard_map.47.own_b.other_b) | copy-start | bytes 25165828

commit v5 on v4

--- a/solution.py
+++ b/solution.py
@@ -12,6 +12,7 @@
 LIVE = 1536
 LANES = 128
 PIECE = 128
+PARTS = 2
 
 
 def stacked(tensor, source, mi, aux, neigh):
@@ -57,12 +58,20 @@
                 near.append(density[swap, outer, inner, back_x])
         product = jnp.dot(
             lhs, jnp.concatenate(near, axis=0), preferred_element_type=jnp.float32
-        ).astype(jnp.bfloat16)
-        for k in range(out_ref.shape[0]):
-            for p in range(aux):
-                out_ref[k, mi * size : (mi + 1) * size, p * size : (p + 1) * size] = product[
-                    p * size : (p + 1) * size, k * size : (k + 1) * size
+        )
+        part = piece // PARTS
+        rows = size // PARTS
+        for p in range(aux):
+            for h in range(PARTS):
+                chosen = [
+                    product[at : at + part]
+                    for at in range(p * size + h * part, (p + 1) * size, piece)
                 ]
+                chosen = jnp.concatenate(chosen, axis=0).astype(jnp.bfloat16)
+                for k in range(out_ref.shape[0]):
+                    out_ref[k, h, mi * rows : (mi + 1) * rows, p * size : (p + 1) * size] = chosen[
+                        :, k * size : (k + 1) * size
+                    ]
 
 
 def halfway_rows(y_first, place, pairs, own, here, there):
@@ -73,7 +82,7 @@
     anywhere = pl.BlockSpec(memory_space=pl.ANY)
     return pl.pallas_call(
         functools.partial(halfway_kernel, y_first),
-        out_shape=jax.ShapeDtypeStruct((blocks, rows, aux * size), jnp.bfloat16),
+        out_shape=jax.ShapeDtypeStruct((blocks, PARTS, rows // PARTS, aux * size), jnp.bfloat16),
         grid_spec=pltpu.PrefetchScalarGridSpec(
             num_scalar_prefetch=2,
             grid=(sources,),
@@ -82,13 +91,15 @@
                 anywhere,
                 anywhere,
             ],
-            out_specs=pl.BlockSpec((blocks, per_source * size, aux * size), lambda s, *_: (0, s, 0)),
+            out_specs=pl.BlockSpec(
+                (blocks, PARTS, rows // sources // PARTS, aux * size), lambda s, *_: (0, 0, s, 0)
+            ),
             scratch_shapes=[
                 pltpu.VMEM((CORES,) + here.shape, jnp.bfloat16),
                 pltpu.SemaphoreType.DMA((CORES,)),
             ],
         ),
-        compiler_params=pltpu.CompilerParams(vmem_limit_bytes=20 << 20),
+        compiler_params=pltpu.CompilerParams(vmem_limit_bytes=56 << 20),
         cost_estimate=pl.CostEstimate(
             flops=2 * rows * aux * neigh * size * width,
             bytes_accessed=2 * own.size + 4 * here.size + 2 * blocks * rows * aux * size,
@@ -100,7 +111,7 @@
 def exchange_kernel(place, pairs, starts, shifts, counts, own, other, own_a, other_a,
                     own_b, other_b, out_ref, total):
     _, aux, _, neigh, size, _ = own.shape
-    _, rows, _ = own_a.shape
+    _, _, rows, _ = own_a.shape
     step = pl.program_id(0)
     per_source = pl.num_programs(0) // SIDE
 
@@ -112,7 +123,7 @@
         block = (step // per_source * CORES + which) * per_source + step % per_source
         rhs = stacked(tensor, 0, 0, aux, neigh)
         for r in range(0, rows, PIECE):
-            product = jnp.dot(halfway[0, r : r + PIECE], rhs, preferred_element_type=jnp.float32)
+            product = jnp.dot(halfway[0, 0, r : r + PIECE], rhs, preferred_element_type=jnp.float32)
             for j in range(neigh):
                 total[pairs[block * neigh + j], r : r + PIECE] += product[
                     :, j * size : (j + 1) * size
@@ -148,9 +159,9 @@
         lax.fori_loop(0, total.shape[0], pack, 0)
 
 
-def exchange_rows(place, pairs, starts, shifts, counts, own, other, halfway_a, halfway_b):
+def exchange_rows(part, place, pairs, starts, shifts, counts, own, other, halfway_a, halfway_b):
     sources, aux, per_source, neigh, size, _ = own.shape
-    half, rows, _ = halfway_a.shape
+    half, _, rows, _ = halfway_a.shape
     blocks = 2 * half
 
     def tensor_map(i, *_):
@@ -160,7 +171,7 @@
         def at(i, place, *_):
             which = place[1] if swap == 0 else 1 - place[1]
             block = (i // per_source * CORES + which) * per_source + i % per_source - first
-            return (jnp.clip(block, 0, half - 1), 0, 0)
+            return (jnp.clip(block, 0, half - 1), part, 0, 0)
 
         return at
 
@@ -172,17 +183,17 @@
             num_scalar_prefetch=5,
             grid=(sources * per_source,),
             in_specs=[tensor, tensor] + [
-                pl.BlockSpec((1, rows, aux * size), halfway_map(swap, first))
+                pl.BlockSpec((1, 1, rows, aux * size), halfway_map(swap, first))
                 for first in (0, half)
                 for swap in range(CORES)
             ],
             out_specs=pl.BlockSpec((rows, LIVE), lambda i, *_: (0, 0)),
             scratch_shapes=[pltpu.VMEM((blocks, rows, size), jnp.float32)],
         ),
-        compiler_params=pltpu.CompilerParams(vmem_limit_bytes=32 << 20),
+        compiler_params=pltpu.CompilerParams(vmem_limit_bytes=56 << 20),
         cost_estimate=pl.CostEstimate(
             flops=2 * rows * aux * neigh * size * blocks * size,
-            bytes_accessed=4 * own.size + 4 * halfway_a.size + 2 * rows * LIVE,
+            bytes_accessed=4 * own.size + 2 * halfway_a.size + 2 * rows * LIVE,
             transcendentals=0,
         ),
     )(place, pairs, starts, shifts, counts, own, other, halfway_a, halfway_a, halfway_b, halfway_b)
@@ -239,19 +250,21 @@
     rows_here, basis = density.shape
     blocks = basis // size
     x, core, z, y = (lax.axis_index(name) for name in ("x", "core", "z", "y"))
-    first_row = (x * CORES + core) * own_blocks * size + (z * SIDE + y) * rows_here
 
     numbers = jnp.arange(blocks)
     offsets = jnp.sum(jnp.where(numbers[None, :] < numbers[:, None], basis_counts[None, :], 0), axis=1)
     starts = jnp.minimum(offsets // LANES, LIVE // LANES - 2)
     shifts = offsets - starts * LANES
 
-    rows_live = jnp.sum(jnp.where(numbers == first_row // size, basis_counts, 0)) - first_row % size
+    from_x = lax.rem(x - jnp.arange(SIDE) + SIDE, SIDE)
+    first_row = (from_x * CORES + core) * own_blocks * size + (z * SIDE + y) * rows_here
+    chosen = numbers[None, :] == (first_row // size)[:, None]
+    rows_live = jnp.sum(jnp.where(chosen, basis_counts[None, :], 0), axis=1) - first_row % size
     column_live = (jnp.arange(size)[None, :] < basis_counts[:, None]).reshape(basis)
-    live = (jnp.arange(rows_here) < rows_live)[:, None] & column_live[None, :]
-
-    kept = jnp.where(live, density, 0)
-    lines = jnp.stack([kept] + [moved(kept, "x", s) for s in range(1, SIDE)])
+    live = (jnp.arange(rows_here)[None, :] < rows_live[:, None])[:, :, None] & column_live
+
+    lines = jnp.stack([density] + [moved(density, "x", s) for s in range(1, SIDE)])
+    lines = jnp.where(live, lines, 0)
     lines, three_index = lax.optimization_barrier((lines, three_index))
     here_a = ring(ring(lines[..., : basis // 2], "z"), "y")
     here_b = ring(ring(lines[..., basis // 2 :], "y"), "z")
@@ -269,11 +282,17 @@
     halfway_a, there_b, sent = lax.optimization_barrier((halfway_a, there_b, own))
     other = swapped(sent)
     halfway_b = halfway_rows(False, place, pairs, own, here_b, there_b)
-    partial = exchange_rows(
-        place, pairs, starts, shifts, basis_counts, own, other, halfway_a, halfway_b
-    )
-    pieces = lax.all_to_all(partial.reshape(-1, rows_here, LIVE), ("x", "z", "y"), 0, 0, tiled=True)
-    return finish(rows_live.astype(jnp.int32).reshape(1), starts, shifts, basis_counts, pieces, basis)
+    part_rows = rows_here // PARTS
+    outputs = []
+    for part in range(PARTS):
+        partial = exchange_rows(
+            part, place, pairs, starts, shifts, basis_counts, own, other, halfway_a, halfway_b
+        )
+        partial = partial.reshape(-1, part_rows, LIVE)
+        pieces = lax.all_to_all(partial, ("x", "z", "y"), 0, 0, tiled=True)
+        still = (rows_live[0] - part * part_rows).astype(jnp.int32).reshape(1)
+        outputs.append(finish(still, starts, shifts, basis_counts, pieces, basis))
+    return jnp.concatenate(outputs, axis=0)
 
 
 def solution(mesh):

time: 171 us -> 181 us (1.058)
  blocking collectives: 50.9 us -> 0 us
  waiting for transfers between devices: 26.7 us -> 53.5 us
  Pallas kernels: 40.6 us -> 62.8 us
  starting transfers between devices: 36.6 us -> 51 us
  local copies, waits for them, and re-layouts: 8.13 us -> 4.04 us
    all_to_all x1 -> x0, blocking collectives: 50.9 us -> none  [per_device(): lax.all_to_all(partial.reshape(-1, rows_here, LIVE), ('x', 'z', 'y'), 0,...]
    all_to_all x0 -> x2, waiting for transfers between devices: none -> 27.5 us  [per_device(): pieces = lax.all_to_all(partial, ('x', 'z', 'y'), 0, 0, tiled=True)]
    all_to_all x0 -> x2, starting transfers between devices: none -> 14.6 us  [per_device(): pieces = lax.all_to_all(partial, ('x', 'z', 'y'), 0, 0, tiled=True)]
    pallas_call x1 -> x2, Pallas kernels: 20.2 us -> 34.1 us  [exchange_rows(): pl.pallas_call(exchange_kernel, out_shape=jax.ShapeDtypeStruct((rows, LIV...]
    pallas_call x2, Pallas kernels: 17.3 us -> 23.2 us  [halfway_rows(): pl.pallas_call(functools.partial(halfway_kernel, y_first), out_shape=jax....]
    unnamed x17 -> x15, local copies, waits for them, and re-layouts: 7.91 us -> 3.31 us
    pallas_call x1 -> x2, Pallas kernels: 3.17 us -> 5.48 us  [finish(): pl.pallas_call(finish_kernel, out_shape=jax.ShapeDtypeStruct((rows, basis...]
  transfers between devices with their start and end apart: 23 -> 25, of which waited for: 8 -> 10; matrix products, arithmetic and copies ran while one was open for 2% -> 3% of each run, Pallas kernels for 10% -> 24%
where the time goes in v5:
time: 181 us; the launch traced here: 180 us
  Pallas kernels  62.8 us (35%)
  waiting for transfers between devices  53.5 us (30%)
  starting transfers between devices  51 us (28%)
  other arithmetic  7.97 us (4%)
  local copies, waits for them, and re-layouts  4.04 us (2%)
    pallas_call x2, Pallas kernels, exchange_rows(): pl.pallas_call(exchange_kernel, out_shape=jax.ShapeDtypeStruct((rows, LIV...  34.1 us
    ppermute x19, starting transfers between devices, moved(): lax.ppermute(value, axis, [(k, (k + shift) % SIDE) for k in range(SIDE)])  30.8 us
    all_to_all x2, waiting for transfers between devices, per_device(): pieces = lax.all_to_all(partial, ('x', 'z', 'y'), 0, 0, tiled=True)  27.5 us
    pallas_call x2, Pallas kernels, halfway_rows(): pl.pallas_call(functools.partial(halfway_kernel, y_first), out_shape=jax....  23.2 us
    ppermute x19, waiting for transfers between devices, moved(): lax.ppermute(value, axis, [(k, (k + shift) % SIDE) for k in range(SIDE)])  15.9 us
    all_to_all x2, starting transfers between devices, per_device(): pieces = lax.all_to_all(partial, ('x', 'z', 'y'), 0, 0, tiled=True)  14.6 us
    all_to_all x1, waiting for transfers between devices, per_device(): own = lax.all_to_all(parted, 'x', 0, 0, tiled=True)  5.63 us
    pallas_call x2, Pallas kernels, finish(): pl.pallas_call(finish_kernel, out_shape=jax.ShapeDtypeStruct((rows, basis...  5.48 us
  transfers between devices with their start and end apart: 25, of which 10 were waited for; matrix products, arithmetic and copies ran while one was open for 3% of the time, Pallas kernels for 24%

profile of v5, /device:TPU:0, one launch (start us, length us, event | category | flops | bytes accessed | tf_op | source)
XLA Modules:
  0.0 179.5 jit_solution(4439801115317549612)
XLA Ops:
  0.0 1.6 collective-permute-start
  1.6 2.7 %collective-permute-start.1 = (bf16[16,2048]{1,0:T(8,128)(2,1)}, bf16[16,2048]{1,0:T(8,128)(2,1)S(1)}, u32[]{:S(2)}, u32[]{:S(2)}) collective-permute-start(bf16[16,2048]{1,0:T(8,128)(2,1)} %param.5), channel_id=1, source_target_pairs={{0,64},{32,96},{64,0},{96,32},{1,65},{33,97},{65,1},{97,33},{2,66}... | collective-permute-start | bytes 196616 | tf_op jit(solution)/shard_map/ppermute | solution.py:234
  4.3 1.4 collective-permute-start.2
  5.7 0.7 fusion
  6.5 0.8 select_reduce_fusion.1
  7.4 0.3 collective-permute-done.1
  7.7 1.1 collective-permute-done.2
  8.8 1.0 and_select_fusion
  9.8 4.9 %all-to-all-start = ((bf16[4,4,2,4,128,128]{5,4,3,2,1,0:T(8,128)(2,1)}), bf16[4,4,2,4,128,128]{5,4,3,2,1,0:T(8,128)(2,1)}, u32[]{:S(2)}, u32[]{:S(2)}) async-start(bf16[4,4,2,4,128,128]{5,4,3,2,1,0:T(8,128)(2,1)} %bitcast.40), calls=%async_computation | async-start | bytes 8388608 | tf_op jit(solution)/shard_map/all_to_all | solution.py:273
  14.7 1.6 collective-permute-start.11
  16.3 1.7 collective-permute-start.13
  18.0 1.9 %collective-permute-start.3 = (bf16[4,16,1024]{2,1,0:T(8,128)(2,1)S(1)}, bf16[4,16,1024]{2,1,0:T(8,128)(2,1)S(1)}, u32[]{:S(2)}, u32[]{:S(2)}) collective-permute-start(bf16[4,16,1024]{2,1,0:T(8,128)(2,1)S(1)} %get-tuple-element.34), channel_id=1, source_target_pairs={{0,4},{4,8},{8,12},{12,0},{1,5},{5,9},{9,13},{13,1},{2,6},{6,10},{... | collective-permute-start | bytes 393224 | tf_op jit(solution)/shard_map/ppermute | solution.py:234
  19.9 2.1 %collective-permute-start.5 = (bf16[4,16,1024]{2,1,0:T(8,128)(2,1)S(1)}, bf16[4,16,1024]{2,1,0:T(8,128)(2,1)S(1)}, u32[]{:S(2)}, u32[]{:S(2)}) collective-permute-start(bf16[4,16,1024]{2,1,0:T(8,128)(2,1)S(1)} %get-tuple-element.34), channel_id=1, source_target_pairs={{0,12},{4,0},{8,4},{12,8},{1,13},{5,1},{9,5},{13,9},{2,14},{6,2},{... | collective-permute-start | bytes 393224 | tf_op jit(solution)/shard_map/ppermute | solution.py:234
  22.0 0.4 collective-permute-start.12
  22.5 2.9 %collective-permute-start.14 = (bf16[2,16,1024]{2,1,0:T(8,128)(2,1)S(1)}, bf16[2,16,1024]{2,1,0:T(8,128)(2,1)S(1)}, u32[]{:S(2)}, u32[]{:S(2)}) collective-permute-start(bf16[2,16,1024]{2,1,0:T(8,128)(2,1)S(1)} %slice.50), channel_id=1, source_target_pairs={{0,3},{1,0},{2,1},{3,2},{4,7},{5,4},{6,5},{7,6},{8,11},{9,8},{10,9... | collective-permute-start | bytes 196616 | tf_op jit(solution)/shard_map/ppermute | solution.py:234
  25.4 0.8 collective-permute-start.4
  26.3 2.6 %collective-permute-start.6 = (bf16[2,16,1024]{2,1,0:T(8,128)(2,1)S(1)}, bf16[2,16,1024]{2,1,0:T(8,128)(2,1)S(1)}, u32[]{:S(2)}, u32[]{:S(2)}) collective-permute-start(bf16[2,16,1024]{2,1,0:T(8,128)(2,1)S(1)} %slice.46), channel_id=1, source_target_pairs={{0,12},{4,0},{8,4},{12,8},{1,13},{5,1},{9,5},{13,9},{2,14},{6,2},{... | collective-permute-start | bytes 196616 | tf_op jit(solution)/shard_map/ppermute | solution.py:234
  29.0 3.2 %collective-permute-start.17 = (bf16[4,4,16,1024]{3,2,1,0:T(8,128)(2,1)S(1)}, bf16[4,4,16,1024]{3,2,1,0:T(8,128)(2,1)S(1)}, u32[]{:S(2)}, u32[]{:S(2)}) collective-permute-start(bf16[4,4,16,1024]{3,2,1,0:T(8,128)(2,1)S(1)} %get-tuple-element.28), channel_id=1, source_target_pairs={{0,12},{4,0},{8,4},{12,8},{1,13},{5,1},{9,5},{13,9},{2,14},{6,2},{... | collective-permute-start | bytes 1572872 | tf_op jit(solution)/shard_map/ppermute | solution.py:234
  32.4 2.1 %collective-permute-start.9 = (bf16[4,4,16,1024]{3,2,1,0:T(8,128)(2,1)S(1)}, bf16[4,4,16,1024]{3,2,1,0:T(8,128)(2,1)S(1)}, u32[]{:S(2)}, u32[]{:S(2)}) collective-permute-start(bf16[4,4,16,1024]{3,2,1,0:T(8,128)(2,1)S(1)} %get-tuple-element.30), channel_id=1, source_target_pairs={{0,3},{1,0},{2,1},{3,2},{4,7},{5,4},{6,5},{7,6},{8,11},{9,8},{10,9... | collective-permute-start | bytes 1572872 | tf_op jit(solution)/shard_map/ppermute | solution.py:234
  34.5 7.1 %collective-permute-done.15 = bf16[4,4,16,1024]{3,2,1,0:T(8,128)(2,1)S(1)} collective-permute-done((bf16[4,4,16,1024]{3,2,1,0:T(8,128)(2,1)S(1)}, bf16[4,4,16,1024]{3,2,1,0:T(8,128)(2,1)S(1)}, u32[]{:S(2)}, u32[]{:S(2)}) %collective-permute-start.15) | collective-permute-done | bytes 524320 | tf_op jit(solution)/shard_map/ppermute | solution.py:234
  41.7 3.3 %collective-permute-start.18 = (bf16[2,4,16,1024]{3,2,1,0:T(8,128)(2,1)S(1)}, bf16[2,4,16,1024]{3,2,1,0:T(8,128)(2,1)S(1)}, u32[]{:S(2)}, u32[]{:S(2)}) collective-permute-start(bf16[2,4,16,1024]{3,2,1,0:T(8,128)(2,1)S(1)} %slice.52), channel_id=1, source_target_pairs={{0,12},{4,0},{8,4},{12,8},{1,13},{5,1},{9,5},{13,9},{2,14},{6,2},{... | collective-permute-start | bytes 786440 | tf_op jit(solution)/shard_map/ppermute | solution.py:234
  45.0 2.0 %collective-permute-start.10 = (bf16[2,4,16,1024]{3,2,1,0:T(8,128)(2,1)S(1)}, bf16[2,4,16,1024]{3,2,1,0:T(8,128)(2,1)S(1)}, u32[]{:S(2)}, u32[]{:S(2)}) collective-permute-start(bf16[2,4,16,1024]{3,2,1,0:T(8,128)(2,1)S(1)} %slice.48), channel_id=1, source_target_pairs={{0,3},{1,0},{2,1},{3,2},{4,7},{5,4},{6,5},{7,6},{8,11},{9,8},{10,9... | collective-permute-start | bytes 786440 | tf_op jit(solution)/shard_map/ppermute | solution.py:234
  47.0 0.2 collective-permute-start.8
  47.2 2.0 %collective-permute-done.16 = bf16[2,4,16,1024]{3,2,1,0:T(8,128)(2,1)S(1)} collective-permute-done((bf16[2,4,16,1024]{3,2,1,0:T(8,128)(2,1)S(1)}, bf16[2,4,16,1024]{3,2,1,0:T(8,128)(2,1)S(1)}, u32[]{:S(2)}, u32[]{:S(2)}) %collective-permute-start.16) | collective-permute-done | bytes 262176 | tf_op jit(solution)/shard_map/ppermute | solution.py:234
  49.3 2.2 %collective-permute-done.10 = bf16[2,4,16,1024]{3,2,1,0:T(8,128)(2,1)S(1)} collective-permute-done((bf16[2,4,16,1024]{3,2,1,0:T(8,128)(2,1)S(1)}, bf16[2,4,16,1024]{3,2,1,0:T(8,128)(2,1)S(1)}, u32[]{:S(2)}, u32[]{:S(2)}) %collective-permute-start.10) | collective-permute-done | bytes 262176 | tf_op jit(solution)/shard_map/ppermute | solution.py:234
  51.5 3.2 %collective-permute-done.8 = bf16[2,4,16,1024]{3,2,1,0:T(8,128)(2,1)S(1)} collective-permute-done((bf16[2,4,16,1024]{3,2,1,0:T(8,128)(2,1)S(1)}, bf16[2,4,16,1024]{3,2,1,0:T(8,128)(2,1)S(1)}, u32[]{:S(2)}, u32[]{:S(2)}) %collective-permute-start.8) | collective-permute-done | bytes 262176 | tf_op jit(solution)/shard_map/ppermute | solution.py:234
  54.7 0.3 pad_maximum_fusion.1.here_hbm
  55.0 1.9 %pad_maximum_fusion.here_hbm = bf16[4,4,4,16,1024]{4,3,2,1,0:T(8,128)(2,1)} fusion(bf16[1,4,4,16,1024]{4,3,2,1,0:T(8,128)(2,1)S(1)} %bitcast.43, bf16[1,4,4,16,1024]{4,3,2,1,0:T(8,128)(2,1)S(1)} %maximum_bitcast_fusion, bf16[1,4,4,16,1024]{4,3,2,1,0:T(8,128)(2,1)S(1)} %bitcast.44, bf16[1,4,4,16,1024]{4,3,2,1,0:T(8,128)(2,1)S(1)} %get-tuple-element.29), kind=kLoop, calls=%fused_computation | loop fusion | flops 3145728 | bytes 4194304 | tf_op jit(solution)/shard_map/stack | solution.py:245
  56.9 5.6 %all-to-all-done.own = bf16[4,4,2,4,128,128]{5,4,3,2,1,0:T(8,128)(2,1)} async-done(((bf16[4,4,2,4,128,128]{5,4,3,2,1,0:T(8,128)(2,1)}), bf16[4,4,2,4,128,128]{5,4,3,2,1,0:T(8,128)(2,1)}, u32[]{:S(2)}, u32[]{:S(2)}) %all-to-all-start) | async-done | bytes 4194336 | tf_op jit(solution)/shard_map/all_to_all | solution.py:273
  62.5 4.5 %collective-permute-done.19.there_hbm = bf16[4,4,4,16,1024]{4,3,2,1,0:T(8,128)(2,1)} collective-permute-done((bf16[4,4,4,16,1024]{4,3,2,1,0:T(8,128)(2,1)}, bf16[4,4,4,16,1024]{4,3,2,1,0:T(8,128)(2,1)}, u32[]{:S(2)}, u32[]{:S(2)}) %collective-permute-start.19) | collective-permute-done | bytes 2097184 | tf_op jit(solution)/shard_map/ppermute | solution.py:238
  67.0 0.1 collective-permute-start.20
  67.2 0.6 reshape.98.pairs
  67.9 0.6 pad_add_fusion.place
  68.5 11.6 %shard_map.46.own_a.other_a = bf16[8,2,512,512]{3,2,1,0:T(8,128)(2,1)} custom-call(s32[4]{0:T(128)} %pad_add_fusion.place, s32[64]{0:T(128)} %reshape.98.pairs, bf16[4,4,2,4,128,128]{5,4,3,2,1,0:T(8,128)(2,1)} %all-to-all-done.own, bf16[4,4,4,16,1024]{4,3,2,1,0:T(8,128)(2,1)} %pad_maximum_fusion.here_hbm, ...), custom_call_target="tpu_custom_call" | custom-call | flops 4294967296 | bytes 16777216 | tf_op jit(solution)/shard_map/pallas_call | solution.py:83
  80.1 0.6 collective-permute-start.21
  80.9 0.6 multiply_subtract_fusion
  81.5 11.6 %shard_map.47.own_b.other_b = bf16[8,2,512,512]{3,2,1,0:T(8,128)(2,1)} custom-call(s32[4]{0:T(128)} %pad_add_fusion.place, s32[64]{0:T(128)} %reshape.98.pairs, bf16[4,4,2,4,128,128]{5,4,3,2,1,0:T(8,128)(2,1)} %all-to-all-done.own, bf16[4,4,4,16,1024]{4,3,2,1,0:T(8,128)(2,1)} %copy-done.1, bf16[4,4,4,16,1024]{4,3,2,1,0:T(8,128)(2,1)} %collective-permute-done.20.there_hbm), custom_call_target="tpu_custom_call" | custom-call | flops 4294967296 | bytes 16777216 | tf_op jit(solution)/shard_map/pallas_call | solution.py:83
  93.1 2.0 %copy-done = bf16[4,4,2,4,128,128]{5,4,3,2,1,0:T(8,128)(2,1)} copy-done((bf16[4,4,2,4,128,128]{5,4,3,2,1,0:T(8,128)(2,1)}, bf16[4,4,2,4,128,128]{5,4,3,2,1,0:T(8,128)(2,1)S(1)}, u32[]{:S(2)}) %copy-start) | copy-done | bytes 4194328
  95.1 17.0 %shard_map.48 = bf16[512,1536]{1,0:T(8,128)(2,1)} custom-call(s32[4]{0:T(128)} %pad_add_fusion.place, s32[64]{0:T(128)} %reshape.98.pairs, s32[16]{0:T(128)} %get-tuple-element.26.starts, s32[16]{0:T(128)} %get-tuple-element.25.shifts, s32[16]{0:T(128)} %counts.7, bf16[4,4,2,4,128,128]{5,4,3,2,1,0:T(8,128)(2,1)} %all-to-all-done.own, ...), custom_call_target="tpu_custom_call" | custom-call | flops 4294967296 | bytes 18350080 | tf_op jit(solution)/shard_map/pallas_call | solution.py:179
  112.1 9.7 %all-to-all-start.1 = ((bf16[64,8,1536]{2,1,0:T(8,128)(2,1)}), bf16[64,8,1536]{2,1,0:T(8,128)(2,1)S(1)}, u32[]{:S(2)}, u32[]{:S(2)}) async-start(bf16[64,8,1536]{2,1,0:T(8,128)(2,1)} %bitcast.39), calls=%async_computation.1 | async-start | bytes 3145728 | tf_op jit(solution)/shard_map/all_to_all | solution.py:292
  121.8 17.1 %shard_map.50 = bf16[512,1536]{1,0:T(8,128)(2,1)} custom-call(s32[4]{0:T(128)} %pad_add_fusion.place, s32[64]{0:T(128)} %reshape.98.pairs, s32[16]{0:T(128)} %get-tuple-element.26.starts, s32[16]{0:T(128)} %get-tuple-element.25.shifts, s32[16]{0:T(128)} %counts.7, bf16[4,4,2,4,128,128]{5,4,3,2,1,0:T(8,128)(2,1)} %all-to-all-done.own, ...), custom_call_target="tpu_custom_call" | custom-call | flops 4294967296 | bytes 18350080 | tf_op jit(solution)/shard_map/pallas_call | solution.py:179
  138.9 7.3 %all-to-all-done.1.pieces = bf16[64,8,1536]{2,1,0:T(8,128)(2,1)S(1)} async-done(((bf16[64,8,1536]{2,1,0:T(8,128)(2,1)}), bf16[64,8,1536]{2,1,0:T(8,128)(2,1)S(1)}, u32[]{:S(2)}, u32[]{:S(2)}) %all-to-all-start.1) | async-done | bytes 1572896 | tf_op jit(solution)/shard_map/all_to_all | solution.py:292
  146.2 4.8 %all-to-all-start.2 = ((bf16[64,8,1536]{2,1,0:T(8,128)(2,1)}), bf16[64,8,1536]{2,1,0:T(8,128)(2,1)S(1)}, u32[]{:S(2)}, u32[]{:S(2)}) async-start(bf16[64,8,1536]{2,1,0:T(8,128)(2,1)} %bitcast.38), calls=%async_computation.2 | async-start | bytes 3145728 | tf_op jit(solution)/shard_map/all_to_all | solution.py:292
  151.1 3.0 %shard_map.49 = f32[8,2048]{1,0:T(8,128)} custom-call(s32[1]{0:T(128)} %bitcast.54, s32[16]{0:T(128)} %get-tuple-element.26.starts, s32[16]{0:T(128)} %get-tuple-element.25.shifts, s32[16]{0:T(128)} %counts.7, bf16[64,8,1536]{2,1,0:T(8,128)(2,1)} %copy-done.2), custom_call_target="tpu_custom_call" | custom-call | tf_op jit(solution)/shard_map/pallas_call | solution.py:224
  154.2 20.2 %all-to-all-done.2.pieces = bf16[64,8,1536]{2,1,0:T(8,128)(2,1)S(1)} async-done(((bf16[64,8,1536]{2,1,0:T(8,128)(2,1)}), bf16[64,8,1536]{2,1,0:T(8,128)(2,1)S(1)}, u32[]{:S(2)}, u32[]{:S(2)}) %all-to-all-start.2) | async-done | bytes 1572896 | tf_op jit(solution)/shard_map/all_to_all | solution.py:292
  174.4 1.2 copy-done.3
  175.6 2.4 %shard_map.51 = f32[8,2048]{1,0:T(8,128)} custom-call(s32[1]{0:T(128)S(6)} %sub.40.rows_live, s32[16]{0:T(128)} %get-tuple-element.26.starts, s32[16]{0:T(128)} %get-tuple-element.25.shifts, s32[16]{0:T(128)} %counts.7, bf16[64,8,1536]{2,1,0:T(8,128)(2,1)} %copy-done.3), custom_call_target="tpu_custom_call" | custom-call | tf_op jit(solution)/shard_map/pallas_call | solution.py:224
  178.0 1.5 pad_maximum_fusion.4
  (51 shorter events, 1.0 us)
Async XLA Ops:
  0.0 7.4 %collective-permute-start = (bf16[16,2048]{1,0:T(8,128)(2,1)}, bf16[16,2048]{1,0:T(8,128)(2,1)S(1)}, u32[]{:S(2)}, u32[]{:S(2)}) collective-permute-start(bf16[16,2048]{1,0:T(8,128)(2,1)} %param.5), channel_id=1, source_target_pairs={{0,32},{32,64},{64,96},{96,0},{1,33},{33,65},{65,97},{97,1},{2,34}... | collective-permute-start | bytes 196616 | tf_op jit(solution)/shard_map/ppermute | solution.py:234
  1.6 6.2 %collective-permute-start.1 = (bf16[16,2048]{1,0:T(8,128)(2,1)}, bf16[16,2048]{1,0:T(8,128)(2,1)S(1)}, u32[]{:S(2)}, u32[]{:S(2)}) collective-permute-start(bf16[16,2048]{1,0:T(8,128)(2,1)} %param.5), channel_id=1, source_target_pairs={{0,64},{32,96},{64,0},{96,32},{1,65},{33,97},{65,1},{97,33},{2,66}... | collective-permute-start | bytes 196616 | tf_op jit(solution)/shard_map/ppermute | solution.py:234
  4.3 4.5 %collective-permute-start.2 = (bf16[16,2048]{1,0:T(8,128)(2,1)}, bf16[16,2048]{1,0:T(8,128)(2,1)S(1)}, u32[]{:S(2)}, u32[]{:S(2)}) collective-permute-start(bf16[16,2048]{1,0:T(8,128)(2,1)} %param.5), channel_id=1, source_target_pairs={{0,96},{32,0},{64,32},{96,64},{1,97},{33,1},{65,33},{97,65},{2,98}... | collective-permute-start | bytes 196616 | tf_op jit(solution)/shard_map/ppermute | solution.py:234
  7.4 143.7 %copy-start.5 = (s32[4]{0:T(128)}, s32[4]{0:T(128)S(1)}, u32[]{:S(2)}) copy-start(s32[4]{0:T(128)S(1)} %fusion.1) | copy-start | bytes 52
  9.8 52.7 %all-to-all-start = ((bf16[4,4,2,4,128,128]{5,4,3,2,1,0:T(8,128)(2,1)}), bf16[4,4,2,4,128,128]{5,4,3,2,1,0:T(8,128)(2,1)}, u32[]{:S(2)}, u32[]{:S(2)}) async-start(bf16[4,4,2,4,128,128]{5,4,3,2,1,0:T(8,128)(2,1)} %bitcast.40), calls=%async_computation | async-start | bytes 8388608 | tf_op jit(solution)/shard_map/all_to_all | solution.py:273
  14.7 7.3 %collective-permute-start.11 = (bf16[4,16,1024]{2,1,0:T(8,128)(2,1)S(1)}, bf16[4,16,1024]{2,1,0:T(8,128)(2,1)S(1)}, u32[]{:S(2)}, u32[]{:S(2)}) collective-permute-start(bf16[4,16,1024]{2,1,0:T(8,128)(2,1)S(1)} %get-tuple-element.33), channel_id=1, source_target_pairs={{0,1},{1,2},{2,3},{3,0},{4,5},{5,6},{6,7},{7,4},{8,9},{9,10},{10,1... | collective-permute-start | bytes 393224 | tf_op jit(solution)/shard_map/ppermute | solution.py:234
  16.3 6.2 %collective-permute-start.13 = (bf16[4,16,1024]{2,1,0:T(8,128)(2,1)S(1)}, bf16[4,16,1024]{2,1,0:T(8,128)(2,1)S(1)}, u32[]{:S(2)}, u32[]{:S(2)}) collective-permute-start(bf16[4,16,1024]{2,1,0:T(8,128)(2,1)S(1)} %get-tuple-element.33), channel_id=1, source_target_pairs={{0,3},{1,0},{2,1},{3,2},{4,7},{5,4},{6,5},{7,6},{8,11},{9,8},{10,9... | collective-permute-start | bytes 393224 | tf_op jit(solution)/shard_map/ppermute | solution.py:234
  18.0 7.4 %collective-permute-start.3 = (bf16[4,16,1024]{2,1,0:T(8,128)(2,1)S(1)}, bf16[4,16,1024]{2,1,0:T(8,128)(2,1)S(1)}, u32[]{:S(2)}, u32[]{:S(2)}) collective-permute-start(bf16[4,16,1024]{2,1,0:T(8,128)(2,1)S(1)} %get-tuple-element.34), channel_id=1, source_target_pairs={{0,4},{4,8},{8,12},{12,0},{1,5},{5,9},{9,13},{13,1},{2,6},{6,10},{... | collective-permute-start | bytes 393224 | tf_op jit(solution)/shard_map/ppermute | solution.py:234
  19.9 6.3 %collective-permute-start.5 = (bf16[4,16,1024]{2,1,0:T(8,128)(2,1)S(1)}, bf16[4,16,1024]{2,1,0:T(8,128)(2,1)S(1)}, u32[]{:S(2)}, u32[]{:S(2)}) collective-permute-start(bf16[4,16,1024]{2,1,0:T(8,128)(2,1)S(1)} %get-tuple-element.34), channel_id=1, source_target_pairs={{0,12},{4,0},{8,4},{12,8},{1,13},{5,1},{9,5},{13,9},{2,14},{6,2},{... | collective-permute-start | bytes 393224 | tf_op jit(solution)/shard_map/ppermute | solution.py:234
  22.0 6.8 %collective-permute-start.12 = (bf16[2,16,1024]{2,1,0:T(8,128)(2,1)S(1)}, bf16[2,16,1024]{2,1,0:T(8,128)(2,1)S(1)}, u32[]{:S(2)}, u32[]{:S(2)}) collective-permute-start(bf16[2,16,1024]{2,1,0:T(8,128)(2,1)S(1)} %slice.49), channel_id=1, source_target_pairs={{0,1},{1,2},{2,3},{3,0},{4,5},{5,6},{6,7},{7,4},{8,9},{9,10},{10,1... | collective-permute-start | bytes 196616 | tf_op jit(solution)/shard_map/ppermute | solution.py:234
  22.5 6.3 %collective-permute-start.14 = (bf16[2,16,1024]{2,1,0:T(8,128)(2,1)S(1)}, bf16[2,16,1024]{2,1,0:T(8,128)(2,1)S(1)}, u32[]{:S(2)}, u32[]{:S(2)}) collective-permute-start(bf16[2,16,1024]{2,1,0:T(8,128)(2,1)S(1)} %slice.50), channel_id=1, source_target_pairs={{0,3},{1,0},{2,1},{3,2},{4,7},{5,4},{6,5},{7,6},{8,11},{9,8},{10,9... | collective-permute-start | bytes 196616 | tf_op jit(solution)/shard_map/ppermute | solution.py:234
  25.4 6.8 %collective-permute-start.4 = (bf16[2,16,1024]{2,1,0:T(8,128)(2,1)S(1)}, bf16[2,16,1024]{2,1,0:T(8,128)(2,1)S(1)}, u32[]{:S(2)}, u32[]{:S(2)}) collective-permute-start(bf16[2,16,1024]{2,1,0:T(8,128)(2,1)S(1)} %slice.45), channel_id=1, source_target_pairs={{0,4},{4,8},{8,12},{12,0},{1,5},{5,9},{9,13},{13,1},{2,6},{6,10},{... | collective-permute-start | bytes 196616 | tf_op jit(solution)/shard_map/ppermute | solution.py:234
  26.3 6.0 %collective-permute-start.6 = (bf16[2,16,1024]{2,1,0:T(8,128)(2,1)S(1)}, bf16[2,16,1024]{2,1,0:T(8,128)(2,1)S(1)}, u32[]{:S(2)}, u32[]{:S(2)}) collective-permute-start(bf16[2,16,1024]{2,1,0:T(8,128)(2,1)S(1)} %slice.46), channel_id=1, source_target_pairs={{0,12},{4,0},{8,4},{12,8},{1,13},{5,1},{9,5},{13,9},{2,14},{6,2},{... | collective-permute-start | bytes 196616 | tf_op jit(solution)/shard_map/ppermute | solution.py:234
  28.9 12.7 %collective-permute-start.15 = (bf16[4,4,16,1024]{3,2,1,0:T(8,128)(2,1)S(1)}, bf16[4,4,16,1024]{3,2,1,0:T(8,128)(2,1)S(1)}, u32[]{:S(2)}, u32[]{:S(2)}) collective-permute-start(bf16[4,4,16,1024]{3,2,1,0:T(8,128)(2,1)S(1)} %get-tuple-element.28), channel_id=1, source_target_pairs={{0,4},{4,8},{8,12},{12,0},{1,5},{5,9},{9,13},{13,1},{2,6},{6,10},{... | collective-permute-start | bytes 1572872 | tf_op jit(solution)/shard_map/ppermute | solution.py:234
  29.0 12.7 %collective-permute-start.17 = (bf16[4,4,16,1024]{3,2,1,0:T(8,128)(2,1)S(1)}, bf16[4,4,16,1024]{3,2,1,0:T(8,128)(2,1)S(1)}, u32[]{:S(2)}, u32[]{:S(2)}) collective-permute-start(bf16[4,4,16,1024]{3,2,1,0:T(8,128)(2,1)S(1)} %get-tuple-element.28), channel_id=1, source_target_pairs={{0,12},{4,0},{8,4},{12,8},{1,13},{5,1},{9,5},{13,9},{2,14},{6,2},{... | collective-permute-start | bytes 1572872 | tf_op jit(solution)/shard_map/ppermute | solution.py:234
  32.4 12.6 %collective-permute-start.9 = (bf16[4,4,16,1024]{3,2,1,0:T(8,128)(2,1)S(1)}, bf16[4,4,16,1024]{3,2,1,0:T(8,128)(2,1)S(1)}, u32[]{:S(2)}, u32[]{:S(2)}) collective-permute-start(bf16[4,4,16,1024]{3,2,1,0:T(8,128)(2,1)S(1)} %get-tuple-element.30), channel_id=1, source_target_pairs={{0,3},{1,0},{2,1},{3,2},{4,7},{5,4},{6,5},{7,6},{8,11},{9,8},{10,9... | collective-permute-start | bytes 1572872 | tf_op jit(solution)/shard_map/ppermute | solution.py:234
  34.5 12.5 %collective-permute-start.7 = (bf16[4,4,16,1024]{3,2,1,0:T(8,128)(2,1)S(1)}, bf16[4,4,16,1024]{3,2,1,0:T(8,128)(2,1)S(1)}, u32[]{:S(2)}, u32[]{:S(2)}) collective-permute-start(bf16[4,4,16,1024]{3,2,1,0:T(8,128)(2,1)S(1)} %get-tuple-element.30), channel_id=1, source_target_pairs={{0,1},{1,2},{2,3},{3,0},{4,5},{5,6},{6,7},{7,4},{8,9},{9,10},{10,1... | collective-permute-start | bytes 1572872 | tf_op jit(solution)/shard_map/ppermute | solution.py:234
  41.6 7.7 %collective-permute-start.16 = (bf16[2,4,16,1024]{3,2,1,0:T(8,128)(2,1)S(1)}, bf16[2,4,16,1024]{3,2,1,0:T(8,128)(2,1)S(1)}, u32[]{:S(2)}, u32[]{:S(2)}) collective-permute-start(bf16[2,4,16,1024]{3,2,1,0:T(8,128)(2,1)S(1)} %slice.51), channel_id=1, source_target_pairs={{0,4},{4,8},{8,12},{12,0},{1,5},{5,9},{9,13},{13,1},{2,6},{6,10},{... | collective-permute-start | bytes 786440 | tf_op jit(solution)/shard_map/ppermute | solution.py:234
  41.7 7.5 %collective-permute-start.18 = (bf16[2,4,16,1024]{3,2,1,0:T(8,128)(2,1)S(1)}, bf16[2,4,16,1024]{3,2,1,0:T(8,128)(2,1)S(1)}, u32[]{:S(2)}, u32[]{:S(2)}) collective-permute-start(bf16[2,4,16,1024]{3,2,1,0:T(8,128)(2,1)S(1)} %slice.52), channel_id=1, source_target_pairs={{0,12},{4,0},{8,4},{12,8},{1,13},{5,1},{9,5},{13,9},{2,14},{6,2},{... | collective-permute-start | bytes 786440 | tf_op jit(solution)/shard_map/ppermute | solution.py:234
  45.0 6.4 %collective-permute-start.10 = (bf16[2,4,16,1024]{3,2,1,0:T(8,128)(2,1)S(1)}, bf16[2,4,16,1024]{3,2,1,0:T(8,128)(2,1)S(1)}, u32[]{:S(2)}, u32[]{:S(2)}) collective-permute-start(bf16[2,4,16,1024]{3,2,1,0:T(8,128)(2,1)S(1)} %slice.48), channel_id=1, source_target_pairs={{0,3},{1,0},{2,1},{3,2},{4,7},{5,4},{6,5},{7,6},{8,11},{9,8},{10,9... | collective-permute-start | bytes 786440 | tf_op jit(solution)/shard_map/ppermute | solution.py:234
  47.0 7.7 %collective-permute-start.8 = (bf16[2,4,16,1024]{3,2,1,0:T(8,128)(2,1)S(1)}, bf16[2,4,16,1024]{3,2,1,0:T(8,128)(2,1)S(1)}, u32[]{:S(2)}, u32[]{:S(2)}) collective-permute-start(bf16[2,4,16,1024]{3,2,1,0:T(8,128)(2,1)S(1)} %slice.47), channel_id=1, source_target_pairs={{0,1},{1,2},{2,3},{3,0},{4,5},{5,6},{6,7},{7,4},{8,9},{9,10},{10,1... | collective-permute-start | bytes 786440 | tf_op jit(solution)/shard_map/ppermute | solution.py:234
  55.0 12.0 %copy-start.1 = (bf16[4,4,4,16,1024]{4,3,2,1,0:T(8,128)(2,1)}, bf16[4,4,4,16,1024]{4,3,2,1,0:T(8,128)(2,1)S(1)}, u32[]{:S(2)}) copy-start(bf16[4,4,4,16,1024]{4,3,2,1,0:T(8,128)(2,1)S(1)} %pad_maximum_fusion.1.here_hbm) | copy-start | bytes 6291460
  55.0 12.1 %copy-start.6 = (s32[16,4]{0,1:T(4,128)S(1)}, s32[16,4]{0,1:T(4,128)}, u32[]{:S(2)}) copy-start(s32[16,4]{0,1:T(4,128)} %param.6) | copy-start | bytes 772
  62.5 4.5 %collective-permute-start.19 = (bf16[4,4,4,16,1024]{4,3,2,1,0:T(8,128)(2,1)}, bf16[4,4,4,16,1024]{4,3,2,1,0:T(8,128)(2,1)}, u32[]{:S(2)}, u32[]{:S(2)}) collective-permute-start(bf16[4,4,4,16,1024]{4,3,2,1,0:T(8,128)(2,1)} %pad_maximum_fusion.here_hbm), channel_id=1, source_target_pairs={{0,16},{16,0},{1,17},{17,1},{2,18},{18,2},{3,19},{19,3},{4,20},{20... | collective-permute-start | bytes 6291464 | tf_op jit(solution)/shard_map/ppermute | solution.py:238
  67.0 13.1 %collective-permute-start.20 = (bf16[4,4,4,16,1024]{4,3,2,1,0:T(8,128)(2,1)S(1)}, bf16[4,4,4,16,1024]{4,3,2,1,0:T(8,128)(2,1)}, u32[]{:S(2)}, u32[]{:S(2)}) collective-permute-start(bf16[4,4,4,16,1024]{4,3,2,1,0:T(8,128)(2,1)S(1)} %pad_maximum_fusion.1.here_hbm), channel_id=1, source_target_pairs={{0,16},{16,0},{1,17},{17,1},{2,18},{18,2},{3,19},{19,3},{4,20},{20... | collective-permute-start | bytes 6291464 | tf_op jit(solution)/shard_map/ppermute | solution.py:238
  68.5 12.3 %copy-start.4 = (s32[16]{0:T(128)S(1)}, s32[16]{0:T(128)}, u32[]{:S(2)}) copy-start(s32[16]{0:T(128)} %counts.7) | copy-start | bytes 196
  80.1 12.9 %collective-permute-start.21 = (bf16[4,4,2,4,128,128]{5,4,3,2,1,0:T(8,128)(2,1)}, bf16[4,4,2,4,128,128]{5,4,3,2,1,0:T(8,128)(2,1)S(1)}, u32[]{:S(2)}, u32[]{:S(2)}) collective-permute-start(bf16[4,4,2,4,128,128]{5,4,3,2,1,0:T(8,128)(2,1)} %all-to-all-done.own), channel_id=1, source_target_pairs={{0,16},{16,0},{1,17},{17,1},{2,18},{18,2},{3,19},{19,3},{4,20},{20... | collective-permute-start | bytes 12582920 | tf_op jit(solution)/shard_map/ppermute | solution.py:238
  93.0 2.0 %copy-start = (bf16[4,4,2,4,128,128]{5,4,3,2,1,0:T(8,128)(2,1)}, bf16[4,4,2,4,128,128]{5,4,3,2,1,0:T(8,128)(2,1)S(1)}, u32[]{:S(2)}) copy-start(bf16[4,4,2,4,128,128]{5,4,3,2,1,0:T(8,128)(2,1)S(1)} %collective-permute-done.21.other) | copy-start | bytes 12582916
  112.1 34.1 %all-to-all-start.1 = ((bf16[64,8,1536]{2,1,0:T(8,128)(2,1)}), bf16[64,8,1536]{2,1,0:T(8,128)(2,1)S(1)}, u32[]{:S(2)}, u32[]{:S(2)}) async-start(bf16[64,8,1536]{2,1,0:T(8,128)(2,1)} %bitcast.39), calls=%async_computation.1 | async-start | bytes 3145728 | tf_op jit(solution)/shard_map/all_to_all | solution.py:292
  146.2 4.9 %copy-start.2 = (bf16[64,8,1536]{2,1,0:T(8,128)(2,1)}, bf16[64,8,1536]{2,1,0:T(8,128)(2,1)S(1)}, u32[]{:S(2)}) copy-start(bf16[64,8,1536]{2,1,0:T(8,128)(2,1)S(1)} %all-to-all-done.1.pieces) | copy-start | bytes 4718596
  146.2 28.2 %all-to-all-start.2 = ((bf16[64,8,1536]{2,1,0:T(8,128)(2,1)}), bf16[64,8,1536]{2,1,0:T(8,128)(2,1)S(1)}, u32[]{:S(2)}, u32[]{:S(2)}) async-start(bf16[64,8,1536]{2,1,0:T(8,128)(2,1)} %bitcast.38), calls=%async_computation.2 | async-start | bytes 3145728 | tf_op jit(solution)/shard_map/all_to_all | solution.py:292
  174.4 1.2 copy-start.3

commit v6 on v2

v6 whole, which is shorter than its diff:
```python
import functools

import jax
import jax.numpy as jnp
from jax import lax
from jax.experimental import pallas as pl
from jax.experimental.pallas import tpu as pltpu
from jax.sharding import Mesh, PartitionSpec as P

CORES = 2
SIDE = 4
LIVE = 1536
LANES = 128
PIECE = 128
PARTS = 2


def stacked(tensor, source, mi, aux, neigh):
    return jnp.concatenate(
        [
            jnp.concatenate([tensor[source, p, mi, j] for j in range(neigh)], axis=1)
            for p in range(aux)
        ],
        axis=0,
    )


def half_stack(tensor, source, mi, aux, neigh, size, part, piece):
    rows = piece // PARTS
    lines = []
    for p in range(aux):
        blocks = []
        for j in range(neigh):
            block = tensor[source, p, mi, j].astype(jnp.float32)
            chosen = [block[at : at + rows] for at in range(part * rows, size, piece)]
            blocks.append(jnp.concatenate(chosen, axis=0).astype(jnp.bfloat16))
        lines.append(jnp.concatenate(blocks, axis=1))
    return jnp.concatenate(lines, axis=0)


def exchange_kernel(part, place, pairs, starts, shifts, counts, own_hbm, other_hbm, here_a, there_a,
                    here_b, there_b, out_ref, own, other, density, halfway, total, sems):
    sources, aux, per_source, neigh, size, _ = own.shape
    piece, width = density.shape[-2:]
    blocks, rows, _ = halfway.shape
    x, core, z, y = place[0], place[1], place[2], place[3]
    part_size = size // PARTS

    def copy(source, target, index):
        return pltpu.make_async_copy(source, target, sems.at[index])

    own_copies = [copy(own_hbm.at[s], own.at[s], s) for s in range(sources)]
    first_copies = [
        copy(here_a, density.at[0, 0], sources),
        copy(there_a, density.at[0, 1], sources + 1),
    ]
    next_copies = [
        copy(here_b, density.at[1, 0], sources + 2),
        copy(there_b, density.at[1, 1], sources + 3),
    ]
    last_copy = copy(other_hbm, other, sources + 4)
    for one in own_copies[:1] + first_copies:
        one.start()
    for one in first_copies:
        one.wait()
    for one in own_copies[1:] + next_copies:
        one.start()
    last_copy.start()

    for half in range(2):
        if half == 1:
            for one in next_copies:
                one.wait()

        def first(b, carry):
            source, mi = b // per_source, b % per_source
            block = (source * CORES + core) * per_source + mi
            lhs = half_stack(own, source, mi, aux, neigh, size, part, piece)
            near = []
            for j in range(neigh):
                partner = pairs[block * neigh + j]
                back_x = lax.rem(x - partner // (CORES * per_source) + SIDE, SIDE)
                swap = jnp.where(partner // per_source % CORES == core, 0, 1)
                for zy in range(size // piece):
                    from_z = partner % per_source * (SIDE // per_source) + zy // SIDE
                    back_z = lax.rem(z - from_z + SIDE, SIDE)
                    back_y = lax.rem(y - zy % SIDE + SIDE, SIDE)
                    outer, inner = (back_y, back_z) if half == 0 else (back_z, back_y)
                    near.append(density[half, swap, outer, inner, back_x])
            product = jnp.dot(
                lhs, jnp.concatenate(near, axis=0), preferred_element_type=jnp.float32
            ).astype(jnp.bfloat16)
            at = pl.ds(pl.multiple_of(b * part_size, part_size), part_size)
            for k in range(width // size):
                for p in range(aux):
                    halfway[half * (width // size) + k, at, p * size : (p + 1) * size] = product[
                        p * part_size : (p + 1) * part_size, k * size : (k + 1) * size
                    ]
            return carry

        for source in range(sources):
            if half == 0:
                own_copies[source].wait()
            lax.fori_loop(source * per_source, (source + 1) * per_source, first, 0, unroll=True)

    total[...] = jnp.zeros_like(total)
    last_copy.wait()

    def add_in(tensor, which):
        def second(b, carry):
            block = (b // per_source * CORES + which) * per_source + b % per_source
            rhs = stacked(tensor, b // per_source, b % per_source, aux, neigh)
            for r in range(0, rows, PIECE):
                product = jnp.dot(
                    halfway[block, r : r + PIECE], rhs, preferred_element_type=jnp.float32
                )
                for j in range(neigh):
                    total[pairs[block * neigh + j], r : r + PIECE] += product[
                        :, j * size : (j + 1) * size
                    ]
            return carry

        lax.fori_loop(0, sources * per_source, second, 0, unroll=4)

    add_in(own, core)
    add_in(other, 1 - core)

    out_ref[...] = jnp.zeros_like(out_ref)
    row = lax.broadcasted_iota(jnp.int32, (size, 2 * LANES), 0)
    column = lax.broadcasted_iota(jnp.int32, (size, 2 * LANES), 1)
    for n in range(blocks):
        chosen = (column == row + shifts[n]) & (row < counts[n])
        moved_columns = jnp.dot(
            total[n].astype(jnp.bfloat16),
            jnp.where(chosen, 1.0, 0.0).astype(jnp.bfloat16),
            preferred_element_type=jnp.float32,
        ).astype(jnp.bfloat16)
        at = pl.ds(pl.multiple_of(starts[n] * LANES, LANES), 2 * LANES)
        out_ref[:, at] += moved_columns


def exchange_rows(part, place, pairs, starts, shifts, counts, own, other, here_a, there_a, here_b, there_b):
    sources, aux, per_source, neigh, size, _ = own.shape
    width = here_a.shape[-1]
    blocks = 2 * width // size
    rows = sources * per_source * size // PARTS
    scalar, vector = pl.BlockSpec(memory_space=pltpu.SMEM), pl.BlockSpec(memory_space=pltpu.VMEM)
    return pl.pallas_call(
        functools.partial(exchange_kernel, part),
        out_shape=jax.ShapeDtypeStruct((rows, LIVE), jnp.bfloat16),
        in_specs=[scalar] * 5 + [pl.BlockSpec(memory_space=pl.ANY)] * 6,
        out_specs=vector,
        scratch_shapes=[
            pltpu.VMEM(own.shape, jnp.bfloat16),
            pltpu.VMEM(own.shape, jnp.bfloat16),
            pltpu.VMEM((2, CORES) + here_a.shape, jnp.bfloat16),
            pltpu.VMEM((blocks, rows, aux * size), jnp.bfloat16),
            pltpu.VMEM((blocks, rows, size), jnp.float32),
            pltpu.SemaphoreType.DMA((sources + 5,)),
        ],
        compiler_params=pltpu.CompilerParams(vmem_limit_bytes=56 << 20),
        cost_estimate=pl.CostEstimate(
            flops=4 * rows * aux * neigh * size * blocks * size,
            bytes_accessed=4 * own.size + 8 * here_a.size + 2 * rows * LIVE,
            transcendentals=0,
        ),
    )(place, pairs, starts, shifts, counts, own, other, here_a, there_a, here_b, there_b)


def finish_kernel(rows_live, starts, shifts, counts, pieces, out_ref, summed):
    amount, rows, _ = pieces.shape
    summed[...] = jnp.zeros_like(summed)

    def add(i, carry):
        part = pieces[pl.ds(i * 8, 8)].astype(jnp.float32)
        summed[...] += jnp.sum(part, axis=0)
        return carry

    lax.fori_loop(0, amount // 8, add, 0)
    row = lax.broadcasted_iota(jnp.int32, (rows, LANES), 0)
    lane = lax.broadcasted_iota(jnp.int32, (rows, LANES), 1)
    for n in range(out_ref.shape[1] // LANES):
        window = summed[:, pl.ds(pl.multiple_of(starts[n] * LANES, LANES), 2 * LANES)]
        turned = pltpu.roll(window, lax.rem(2 * LANES - shifts[n], 2 * LANES), axis=1)
        live = (lane < counts[n]) & (row < rows_live[0])
        out_ref[:, n * LANES : (n + 1) * LANES] = jnp.where(live, turned[:, :LANES], 0.0)


def finish(rows_live, starts, shifts, counts, pieces, basis):
    rows = pieces.shape[1]
    scalar, vector = pl.BlockSpec(memory_space=pltpu.SMEM), pl.BlockSpec(memory_space=pltpu.VMEM)
    return pl.pallas_call(
        finish_kernel,
        out_shape=jax.ShapeDtypeStruct((rows, basis), jnp.float32),
        in_specs=[scalar] * 4 + [vector],
        out_specs=vector,
        scratch_shapes=[pltpu.VMEM((rows, LIVE), jnp.float32)],
    )(rows_live, starts, shifts, counts, pieces)


def moved(value, axis, shift):
    return lax.ppermute(value, axis, [(k, (k + shift) % SIDE) for k in range(SIDE)])


def swapped(value):
    return lax.ppermute(value, "core", [(0, 1), (1, 0)])


def ring(value, axis):
    up, down = moved(value, axis, 1), moved(value, axis, SIDE - 1)
    cut = value.shape[0] // 2
    far = [moved(up[:cut], axis, 1), moved(down[cut:], axis, SIDE - 1)]
    return jnp.stack([value, up, jnp.concatenate(far), down])


def per_device(three_index, density, pair_blocks, basis_counts):
    aux_here, own_blocks, neigh, size, _ = three_index.shape
    rows_here, basis = density.shape
    blocks = basis // size
    x, core, z, y = (lax.axis_index(name) for name in ("x", "core", "z", "y"))

    numbers = jnp.arange(blocks)
    offsets = jnp.sum(jnp.where(numbers[None, :] < numbers[:, None], basis_counts[None, :], 0), axis=1)
    starts = jnp.minimum(offsets // LANES, LIVE // LANES - 2)
    shifts = offsets - starts * LANES

    from_x = lax.rem(x - jnp.arange(SIDE) + SIDE, SIDE)
    first_row = (from_x * CORES + core) * own_blocks * size + (z * SIDE + y) * rows_here
    chosen = numbers[None, :] == (first_row // size)[:, None]
    rows_live = jnp.sum(jnp.where(chosen, basis_counts[None, :], 0), axis=1) - first_row % size
    column_live = (jnp.arange(size)[None, :] < basis_counts[:, None]).reshape(basis)
    live = (jnp.arange(rows_here)[None, :] < rows_live[:, None])[:, :, None] & column_live

    lines = jnp.stack([density] + [moved(density, "x", s) for s in range(1, SIDE)])
    lines = jnp.where(live, lines, 0)
    lines, three_index = lax.optimization_barrier((lines, three_index))
    here_a = ring(ring(lines[..., : basis // 2], "z"), "y")
    here_b = ring(ring(lines[..., basis // 2 :], "y"), "z")

    parted = three_index.reshape(SIDE, aux_here // SIDE, own_blocks, neigh, size, size)
    own = lax.all_to_all(parted, "x", 0, 0, tiled=True)
    own, here_a, here_b = lax.optimization_barrier((own, here_a, here_b))
    there_a, there_b, other = swapped(here_a), swapped(here_b), swapped(own)

    place = jnp.stack([x, core, z, y]).astype(jnp.int32)
    pairs = pair_blocks.reshape(-1)
    part_rows = rows_here // PARTS
    outputs = []
    for part in range(PARTS):
        partial = exchange_rows(
            part, place, pairs, starts, shifts, basis_counts, own, other,
            here_a, there_a, here_b, there_b,
        )
        partial = partial.reshape(-1, part_rows, LIVE)
        pieces = lax.all_to_all(partial, ("x", "z", "y"), 0, 0, tiled=True)
        still = (rows_live[0] - part * part_rows).astype(jnp.int32).reshape(1)
        outputs.append(finish(still, starts, shifts, basis_counts, pieces, basis))
    return jnp.concatenate(outputs, axis=0)


def solution(mesh):
    devices = mesh.devices.reshape(SIDE, CORES, SIDE, SIDE)
    fine = Mesh(devices, ("x", "core", "z", "y"))
    in_specs = (P(("z", "y"), ("x", "core")), P(("x", "core", "z", "y"), None), P(), P())
    out_specs = P(("x", "core", "z", "y"), None)
    return jax.shard_map(
        per_device, mesh=fine, in_specs=in_specs, out_specs=out_specs, check_vma=False
    )
```

time: 177 us -> 162 us (0.915)
  blocking collectives: 106 us -> 0 us
  starting transfers between devices: 0.01 us -> 52.8 us
  waiting for transfers between devices: 17.8 us -> 57.5 us
  between operations: 14.1 us -> 0.27 us
  Pallas kernels: 34.9 us -> 40.5 us
  other arithmetic: 3.71 us -> 7.9 us
  local copies, waits for them, and re-layouts: 0.19 us -> 2.11 us
    all_to_all x2 -> x0, blocking collectives: 106 us -> none  [the longest x1 58.1 us: per_device(): own = lax.all_to_all(parted, 'x', 0, 0, tiled=True)]
    all_to_all x0 -> x3, waiting for transfers between devices: none -> 34.6 us  [the longest x2 27 us: per_device(): pieces = lax.all_to_all(partial, ('x', 'z', 'y'), 0, 0, tiled=True)]
    ppermute x1 -> x22, starting transfers between devices: 0.01 us -> 33.1 us  [the longest x19 32.6 us: moved(): lax.ppermute(value, axis, [(k, (k + shift) % SIDE) for k in range(SIDE)])]
    all_to_all x0 -> x3, starting transfers between devices: none -> 19.6 us  [the longest x2 14.8 us: per_device(): pieces = lax.all_to_all(partial, ('x', 'z', 'y'), 0, 0, tiled=True)]
    ppermute x1 -> x22, waiting for transfers between devices: 7.16 us -> 22.9 us  [the longest x19 12 us: moved(): lax.ppermute(value, axis, [(k, (k + shift) % SIDE) for k in range(SIDE)])]
    all_gather x1 -> x0, waiting for transfers between devices: 10.6 us -> none  [per_device(): whole = lax.all_gather(kept, ('x', 'core', 'z', 'y'), axis=0, tiled=True)]
    pallas_call x1 -> x2, Pallas kernels: 31.8 us -> 35.1 us  [exchange_rows(): pl.pallas_call(functools.partial(exchange_kernel, part), out_shape=jax.Sh...]
    another operation x0 -> x9, other arithmetic: none -> 3.04 us  [the longest x8 2.39 us: ring(): return jnp.stack([value, up, jnp.concatenate(far), down])]
  transfers between devices with their start and end apart: 2 -> 25, of which waited for: 2 -> 8; matrix products, arithmetic and copies ran while one was open for 0% -> 4% of each run, Pallas kernels for 0% -> 13%
where the time goes in v6:
time: 162 us; the launch traced here: 161 us
  waiting for transfers between devices  57.5 us (35%)
  starting transfers between devices  52.8 us (33%)
  Pallas kernels  40.5 us (25%)
  other arithmetic  7.9 us (5%)
  local copies, waits for them, and re-layouts  2.11 us (1%)
    pallas_call x2, Pallas kernels, exchange_rows(): pl.pallas_call(functools.partial(exchange_kernel, part), out_shape=jax.Sh...  35.1 us
    ppermute x19, starting transfers between devices, moved(): lax.ppermute(value, axis, [(k, (k + shift) % SIDE) for k in range(SIDE)])  32.6 us
    all_to_all x2, waiting for transfers between devices, per_device(): pieces = lax.all_to_all(partial, ('x', 'z', 'y'), 0, 0, tiled=True)  27 us
    all_to_all x2, starting transfers between devices, per_device(): pieces = lax.all_to_all(partial, ('x', 'z', 'y'), 0, 0, tiled=True)  14.8 us
    ppermute x19, waiting for transfers between devices, moved(): lax.ppermute(value, axis, [(k, (k + shift) % SIDE) for k in range(SIDE)])  12 us
    ppermute x3, waiting for transfers between devices, swapped(): return lax.ppermute(value, 'core', [(0, 1), (1, 0)])  10.9 us
    all_to_all x1, waiting for transfers between devices, per_device(): own = lax.all_to_all(parted, 'x', 0, 0, tiled=True)  7.57 us
    pallas_call x2, Pallas kernels, finish(): pl.pallas_call(finish_kernel, out_shape=jax.ShapeDtypeStruct((rows, basis...  5.45 us
  transfers between devices with their start and end apart: 25, of which 8 were waited for; matrix products, arithmetic and copies ran while one was open for 4% of the time, Pallas kernels for 13%

profile of v6, /device:TPU:0, one launch (start us, length us, event | category | flops | bytes accessed | tf_op | source)
XLA Modules:
  0.0 161.1 jit_solution(6873205243669755802)
XLA Ops:
  0.0 1.6 collective-permute-start
  1.6 1.7 %collective-permute-start.2 = (bf16[16,2048]{1,0:T(8,128)(2,1)}, bf16[16,2048]{1,0:T(8,128)(2,1)S(1)}, u32[]{:S(2)}, u32[]{:S(2)}) collective-permute-start(bf16[16,2048]{1,0:T(8,128)(2,1)} %param.5), channel_id=1, source_target_pairs={{0,96},{32,0},{64,32},{96,64},{1,97},{33,1},{65,33},{97,65},{2,98}... | collective-permute-start | bytes 196616 | tf_op jit(solution)/shard_map/ppermute | solution.py:202
  3.2 1.9 %collective-permute-start.1 = (bf16[16,2048]{1,0:T(8,128)(2,1)}, bf16[16,2048]{1,0:T(8,128)(2,1)S(1)}, u32[]{:S(2)}, u32[]{:S(2)}) collective-permute-start(bf16[16,2048]{1,0:T(8,128)(2,1)} %param.5), channel_id=1, source_target_pairs={{0,64},{32,96},{64,0},{96,32},{1,65},{33,97},{65,1},{97,33},{2,66}... | collective-permute-start | bytes 196616 | tf_op jit(solution)/shard_map/ppermute | solution.py:202
  5.1 0.7 fusion
  5.9 0.8 select_reduce_fusion.1
  6.8 2.4 %collective-permute-done.1 = bf16[16,2048]{1,0:T(8,128)(2,1)S(1)} collective-permute-done((bf16[16,2048]{1,0:T(8,128)(2,1)}, bf16[16,2048]{1,0:T(8,128)(2,1)S(1)}, u32[]{:S(2)}, u32[]{:S(2)}) %collective-permute-start.1) | collective-permute-done | bytes 65568 | tf_op jit(solution)/shard_map/ppermute | solution.py:202
  9.2 1.0 and_select_fusion
  10.2 4.9 %all-to-all-start = ((bf16[4,4,2,4,128,128]{5,4,3,2,1,0:T(8,128)(2,1)}), bf16[4,4,2,4,128,128]{5,4,3,2,1,0:T(8,128)(2,1)}, u32[]{:S(2)}, u32[]{:S(2)}) async-start(bf16[4,4,2,4,128,128]{5,4,3,2,1,0:T(8,128)(2,1)} %bitcast.38), calls=%async_computation | async-start | bytes 8388608 | tf_op jit(solution)/shard_map/all_to_all | solution.py:241
  15.1 1.7 %collective-permute-start.11 = (bf16[4,16,1024]{2,1,0:T(8,128)(2,1)S(1)}, bf16[4,16,1024]{2,1,0:T(8,128)(2,1)S(1)}, u32[]{:S(2)}, u32[]{:S(2)}) collective-permute-start(bf16[4,16,1024]{2,1,0:T(8,128)(2,1)S(1)} %get-tuple-element.23), channel_id=1, source_target_pairs={{0,1},{1,2},{2,3},{3,0},{4,5},{5,6},{6,7},{7,4},{8,9},{9,10},{10,1... | collective-permute-start | bytes 393224 | tf_op jit(solution)/shard_map/ppermute | solution.py:202
  16.9 1.6 collective-permute-start.13
  18.4 2.0 %collective-permute-start.3 = (bf16[4,16,1024]{2,1,0:T(8,128)(2,1)S(1)}, bf16[4,16,1024]{2,1,0:T(8,128)(2,1)S(1)}, u32[]{:S(2)}, u32[]{:S(2)}) collective-permute-start(bf16[4,16,1024]{2,1,0:T(8,128)(2,1)S(1)} %get-tuple-element.24), channel_id=1, source_target_pairs={{0,4},{4,8},{8,12},{12,0},{1,5},{5,9},{9,13},{13,1},{2,6},{6,10},{... | collective-permute-start | bytes 393224 | tf_op jit(solution)/shard_map/ppermute | solution.py:202
  20.4 2.1 %collective-permute-start.5 = (bf16[4,16,1024]{2,1,0:T(8,128)(2,1)S(1)}, bf16[4,16,1024]{2,1,0:T(8,128)(2,1)S(1)}, u32[]{:S(2)}, u32[]{:S(2)}) collective-permute-start(bf16[4,16,1024]{2,1,0:T(8,128)(2,1)S(1)} %get-tuple-element.24), channel_id=1, source_target_pairs={{0,12},{4,0},{8,4},{12,8},{1,13},{5,1},{9,5},{13,9},{2,14},{6,2},{... | collective-permute-start | bytes 393224 | tf_op jit(solution)/shard_map/ppermute | solution.py:202
  22.6 0.4 collective-permute-start.12
  23.0 2.9 %collective-permute-start.14 = (bf16[2,16,1024]{2,1,0:T(8,128)(2,1)S(1)}, bf16[2,16,1024]{2,1,0:T(8,128)(2,1)S(1)}, u32[]{:S(2)}, u32[]{:S(2)}) collective-permute-start(bf16[2,16,1024]{2,1,0:T(8,128)(2,1)S(1)} %slice.50), channel_id=1, source_target_pairs={{0,3},{1,0},{2,1},{3,2},{4,7},{5,4},{6,5},{7,6},{8,11},{9,8},{10,9... | collective-permute-start | bytes 196616 | tf_op jit(solution)/shard_map/ppermute | solution.py:202
  26.0 0.8 collective-permute-start.4
  26.8 2.6 %collective-permute-start.6 = (bf16[2,16,1024]{2,1,0:T(8,128)(2,1)S(1)}, bf16[2,16,1024]{2,1,0:T(8,128)(2,1)S(1)}, u32[]{:S(2)}, u32[]{:S(2)}) collective-permute-start(bf16[2,16,1024]{2,1,0:T(8,128)(2,1)S(1)} %slice.46), channel_id=1, source_target_pairs={{0,12},{4,0},{8,4},{12,8},{1,13},{5,1},{9,5},{13,9},{2,14},{6,2},{... | collective-permute-start | bytes 196616 | tf_op jit(solution)/shard_map/ppermute | solution.py:202
  29.4 0.1 fusion.8
  29.5 0.1 collective-permute-start.15
  29.6 3.2 %collective-permute-start.17 = (bf16[4,4,16,1024]{3,2,1,0:T(8,128)(2,1)S(1)}, bf16[4,4,16,1024]{3,2,1,0:T(8,128)(2,1)S(1)}, u32[]{:S(2)}, u32[]{:S(2)}) collective-permute-start(bf16[4,4,16,1024]{3,2,1,0:T(8,128)(2,1)S(1)} %get-tuple-element.18), channel_id=1, source_target_pairs={{0,12},{4,0},{8,4},{12,8},{1,13},{5,1},{9,5},{13,9},{2,14},{6,2},{... | collective-permute-start | bytes 1572872 | tf_op jit(solution)/shard_map/ppermute | solution.py:202
  32.8 0.1 fusion.9
  33.0 3.2 %collective-permute-start.9 = (bf16[4,4,16,1024]{3,2,1,0:T(8,128)(2,1)S(1)}, bf16[4,4,16,1024]{3,2,1,0:T(8,128)(2,1)S(1)}, u32[]{:S(2)}, u32[]{:S(2)}) collective-permute-start(bf16[4,4,16,1024]{3,2,1,0:T(8,128)(2,1)S(1)} %get-tuple-element.20), channel_id=1, source_target_pairs={{0,3},{1,0},{2,1},{3,2},{4,7},{5,4},{6,5},{7,6},{8,11},{9,8},{10,9... | collective-permute-start | bytes 1572872 | tf_op jit(solution)/shard_map/ppermute | solution.py:202
  36.2 5.4 %collective-permute-done.15 = bf16[4,4,16,1024]{3,2,1,0:T(8,128)(2,1)S(1)} collective-permute-done((bf16[4,4,16,1024]{3,2,1,0:T(8,128)(2,1)S(1)}, bf16[4,4,16,1024]{3,2,1,0:T(8,128)(2,1)S(1)}, u32[]{:S(2)}, u32[]{:S(2)}) %collective-permute-start.15) | collective-permute-done | bytes 524320 | tf_op jit(solution)/shard_map/ppermute | solution.py:202
  41.6 0.1 collective-permute-start.16
  41.7 3.3 %collective-permute-start.18 = (bf16[2,4,16,1024]{3,2,1,0:T(8,128)(2,1)S(1)}, bf16[2,4,16,1024]{3,2,1,0:T(8,128)(2,1)S(1)}, u32[]{:S(2)}, u32[]{:S(2)}) collective-permute-start(bf16[2,4,16,1024]{3,2,1,0:T(8,128)(2,1)S(1)} %slice.52), channel_id=1, source_target_pairs={{0,12},{4,0},{8,4},{12,8},{1,13},{5,1},{9,5},{13,9},{2,14},{6,2},{... | collective-permute-start | bytes 786440 | tf_op jit(solution)/shard_map/ppermute | solution.py:202
  45.0 0.1 collective-permute-start.8
  45.2 3.2 %collective-permute-start.10 = (bf16[2,4,16,1024]{3,2,1,0:T(8,128)(2,1)S(1)}, bf16[2,4,16,1024]{3,2,1,0:T(8,128)(2,1)S(1)}, u32[]{:S(2)}, u32[]{:S(2)}) collective-permute-start(bf16[2,4,16,1024]{3,2,1,0:T(8,128)(2,1)S(1)} %slice.48), channel_id=1, source_target_pairs={{0,3},{1,0},{2,1},{3,2},{4,7},{5,4},{6,5},{7,6},{8,11},{9,8},{10,9... | collective-permute-start | bytes 786440 | tf_op jit(solution)/shard_map/ppermute | solution.py:202
  48.4 0.8 collective-permute-done.16
  49.3 3.4 %collective-permute-done.8 = bf16[2,4,16,1024]{3,2,1,0:T(8,128)(2,1)S(1)} collective-permute-done((bf16[2,4,16,1024]{3,2,1,0:T(8,128)(2,1)S(1)}, bf16[2,4,16,1024]{3,2,1,0:T(8,128)(2,1)S(1)}, u32[]{:S(2)}, u32[]{:S(2)}) %collective-permute-start.8) | collective-permute-done | bytes 262176 | tf_op jit(solution)/shard_map/ppermute | solution.py:202
  52.7 0.3 pad_maximum_fusion.1.here_b
  53.0 1.8 %pad_maximum_fusion.here_a = bf16[4,4,4,16,1024]{4,3,2,1,0:T(8,128)(2,1)} fusion(bf16[1,4,4,16,1024]{4,3,2,1,0:T(8,128)(2,1)S(1)} %bitcast.44, bf16[1,4,4,16,1024]{4,3,2,1,0:T(8,128)(2,1)S(1)} %maximum_bitcast_fusion, bf16[1,4,4,16,1024]{4,3,2,1,0:T(8,128)(2,1)S(1)} %bitcast.43, bf16[1,4,4,16,1024]{4,3,2,1,0:T(8,128)(2,1)S(1)} %get-tuple-element.19), kind=kLoop, calls=%fused_computation | loop fusion | flops 3145728 | bytes 4194304 | tf_op jit(solution)/shard_map/stack | solution.py:213
  54.9 7.6 %all-to-all-done.own_hbm = bf16[4,4,2,4,128,128]{5,4,3,2,1,0:T(8,128)(2,1)} async-done(((bf16[4,4,2,4,128,128]{5,4,3,2,1,0:T(8,128)(2,1)}), bf16[4,4,2,4,128,128]{5,4,3,2,1,0:T(8,128)(2,1)}, u32[]{:S(2)}, u32[]{:S(2)}) %all-to-all-start) | async-done | bytes 4194336 | tf_op jit(solution)/shard_map/all_to_all | solution.py:241
  62.4 0.5 collective-permute-start.20
  63.0 0.1 copy.7
  63.0 0.7 reshape.98.pairs
  63.7 0.7 pad_add_fusion.place
  64.4 0.1 select_reduce_fusion
  64.5 0.5 multiply_subtract_fusion
  65.0 10.9 %collective-permute-done.20.there_a = bf16[4,4,4,16,1024]{4,3,2,1,0:T(8,128)(2,1)} collective-permute-done((bf16[4,4,4,16,1024]{4,3,2,1,0:T(8,128)(2,1)}, bf16[4,4,4,16,1024]{4,3,2,1,0:T(8,128)(2,1)}, u32[]{:S(2)}, u32[]{:S(2)}) %collective-permute-start.20) | collective-permute-done | bytes 2097184 | tf_op jit(solution)/shard_map/ppermute | solution.py:206
  75.9 17.5 %shard_map.46 = bf16[512,1536]{1,0:T(8,128)(2,1)} custom-call(s32[4]{0:T(128)} %pad_add_fusion.place, s32[64]{0:T(128)} %reshape.98.pairs, s32[16]{0:T(128)} %get-tuple-element.16.starts, s32[16]{0:T(128)} %get-tuple-element.15.shifts, s32[16]{0:T(128)} %counts.7, bf16[4,4,2,4,128,128]{5,4,3,2,1,0:T(8,128)(2,1)} %all-to-all-done.own_hbm, ...), custom_call_target="tpu_custom_call" | custom-call | flops 8589934592 | bytes 18350080 | tf_op jit(solution)/shard_map/pallas_call | solution.py:148
  93.5 9.9 %all-to-all-start.1 = ((bf16[64,8,1536]{2,1,0:T(8,128)(2,1)}), bf16[64,8,1536]{2,1,0:T(8,128)(2,1)S(1)}, u32[]{:S(2)}, u32[]{:S(2)}) async-start(bf16[64,8,1536]{2,1,0:T(8,128)(2,1)} %bitcast.40), calls=%async_computation.1 | async-start | bytes 3145728 | tf_op jit(solution)/shard_map/all_to_all | solution.py:255
  103.4 17.6 %shard_map.48 = bf16[512,1536]{1,0:T(8,128)(2,1)} custom-call(s32[4]{0:T(128)} %pad_add_fusion.place, s32[64]{0:T(128)} %reshape.98.pairs, s32[16]{0:T(128)} %get-tuple-element.16.starts, s32[16]{0:T(128)} %get-tuple-element.15.shifts, s32[16]{0:T(128)} %counts.7, bf16[4,4,2,4,128,128]{5,4,3,2,1,0:T(8,128)(2,1)} %all-to-all-done.own_hbm, ...), custom_call_target="tpu_custom_call" | custom-call | flops 8589934592 | bytes 18350080 | tf_op jit(solution)/shard_map/pallas_call | solution.py:148
  121.0 6.7 %all-to-all-done.1.pieces = bf16[64,8,1536]{2,1,0:T(8,128)(2,1)S(1)} async-done(((bf16[64,8,1536]{2,1,0:T(8,128)(2,1)}), bf16[64,8,1536]{2,1,0:T(8,128)(2,1)S(1)}, u32[]{:S(2)}, u32[]{:S(2)}) %all-to-all-start.1) | async-done | bytes 1572896 | tf_op jit(solution)/shard_map/all_to_all | solution.py:255
  127.7 4.8 %all-to-all-start.2 = ((bf16[64,8,1536]{2,1,0:T(8,128)(2,1)}), bf16[64,8,1536]{2,1,0:T(8,128)(2,1)S(1)}, u32[]{:S(2)}, u32[]{:S(2)}) async-start(bf16[64,8,1536]{2,1,0:T(8,128)(2,1)} %bitcast.39), calls=%async_computation.2 | async-start | bytes 3145728 | tf_op jit(solution)/shard_map/all_to_all | solution.py:255
  132.5 3.0 %shard_map.47 = f32[8,2048]{1,0:T(8,128)} custom-call(s32[1]{0:T(128)} %bitcast.54, s32[16]{0:T(128)} %get-tuple-element.16.starts, s32[16]{0:T(128)} %get-tuple-element.15.shifts, s32[16]{0:T(128)} %counts.7, bf16[64,8,1536]{2,1,0:T(8,128)(2,1)} %copy-done), custom_call_target="tpu_custom_call" | custom-call | tf_op jit(solution)/shard_map/pallas_call | solution.py:192
  135.6 20.3 %all-to-all-done.2.pieces = bf16[64,8,1536]{2,1,0:T(8,128)(2,1)S(1)} async-done(((bf16[64,8,1536]{2,1,0:T(8,128)(2,1)}), bf16[64,8,1536]{2,1,0:T(8,128)(2,1)S(1)}, u32[]{:S(2)}, u32[]{:S(2)}) %all-to-all-start.2) | async-done | bytes 1572896 | tf_op jit(solution)/shard_map/all_to_all | solution.py:255
  155.9 1.2 copy-done.1
  157.1 2.4 %shard_map.49 = f32[8,2048]{1,0:T(8,128)} custom-call(s32[1]{0:T(128)S(6)} %sub.40.rows_live, s32[16]{0:T(128)} %get-tuple-element.16.starts, s32[16]{0:T(128)} %get-tuple-element.15.shifts, s32[16]{0:T(128)} %counts.7, bf16[64,8,1536]{2,1,0:T(8,128)(2,1)} %copy-done.1), custom_call_target="tpu_custom_call" | custom-call | tf_op jit(solution)/shard_map/pallas_call | solution.py:192
  159.5 1.5 pad_maximum_fusion.4
  (47 shorter events, 0.5 us)
Async XLA Ops:
  0.0 6.8 %collective-permute-start = (bf16[16,2048]{1,0:T(8,128)(2,1)}, bf16[16,2048]{1,0:T(8,128)(2,1)S(1)}, u32[]{:S(2)}, u32[]{:S(2)}) collective-permute-start(bf16[16,2048]{1,0:T(8,128)(2,1)} %param.5), channel_id=1, source_target_pairs={{0,32},{32,64},{64,96},{96,0},{1,33},{33,65},{65,97},{97,1},{2,34}... | collective-permute-start | bytes 196616 | tf_op jit(solution)/shard_map/ppermute | solution.py:202
  1.6 5.3 %collective-permute-start.2 = (bf16[16,2048]{1,0:T(8,128)(2,1)}, bf16[16,2048]{1,0:T(8,128)(2,1)S(1)}, u32[]{:S(2)}, u32[]{:S(2)}) collective-permute-start(bf16[16,2048]{1,0:T(8,128)(2,1)} %param.5), channel_id=1, source_target_pairs={{0,96},{32,0},{64,32},{96,64},{1,97},{33,1},{65,33},{97,65},{2,98}... | collective-permute-start | bytes 196616 | tf_op jit(solution)/shard_map/ppermute | solution.py:202
  3.2 6.0 %collective-permute-start.1 = (bf16[16,2048]{1,0:T(8,128)(2,1)}, bf16[16,2048]{1,0:T(8,128)(2,1)S(1)}, u32[]{:S(2)}, u32[]{:S(2)}) collective-permute-start(bf16[16,2048]{1,0:T(8,128)(2,1)} %param.5), channel_id=1, source_target_pairs={{0,64},{32,96},{64,0},{96,32},{1,65},{33,97},{65,1},{97,33},{2,66}... | collective-permute-start | bytes 196616 | tf_op jit(solution)/shard_map/ppermute | solution.py:202
  6.7 125.8 %copy-start.4 = (s32[4]{0:T(128)}, s32[4]{0:T(128)S(1)}, u32[]{:S(2)}) copy-start(s32[4]{0:T(128)S(1)} %fusion.1) | copy-start | bytes 52
  10.2 52.2 %all-to-all-start = ((bf16[4,4,2,4,128,128]{5,4,3,2,1,0:T(8,128)(2,1)}), bf16[4,4,2,4,128,128]{5,4,3,2,1,0:T(8,128)(2,1)}, u32[]{:S(2)}, u32[]{:S(2)}) async-start(bf16[4,4,2,4,128,128]{5,4,3,2,1,0:T(8,128)(2,1)} %bitcast.38), calls=%async_computation | async-start | bytes 8388608 | tf_op jit(solution)/shard_map/all_to_all | solution.py:241
  15.1 7.4 %collective-permute-start.11 = (bf16[4,16,1024]{2,1,0:T(8,128)(2,1)S(1)}, bf16[4,16,1024]{2,1,0:T(8,128)(2,1)S(1)}, u32[]{:S(2)}, u32[]{:S(2)}) collective-permute-start(bf16[4,16,1024]{2,1,0:T(8,128)(2,1)S(1)} %get-tuple-element.23), channel_id=1, source_target_pairs={{0,1},{1,2},{2,3},{3,0},{4,5},{5,6},{6,7},{7,4},{8,9},{9,10},{10,1... | collective-permute-start | bytes 393224 | tf_op jit(solution)/shard_map/ppermute | solution.py:202
  16.9 6.2 %collective-permute-start.13 = (bf16[4,16,1024]{2,1,0:T(8,128)(2,1)S(1)}, bf16[4,16,1024]{2,1,0:T(8,128)(2,1)S(1)}, u32[]{:S(2)}, u32[]{:S(2)}) collective-permute-start(bf16[4,16,1024]{2,1,0:T(8,128)(2,1)S(1)} %get-tuple-element.23), channel_id=1, source_target_pairs={{0,3},{1,0},{2,1},{3,2},{4,7},{5,4},{6,5},{7,6},{8,11},{9,8},{10,9... | collective-permute-start | bytes 393224 | tf_op jit(solution)/shard_map/ppermute | solution.py:202
  18.4 7.5 %collective-permute-start.3 = (bf16[4,16,1024]{2,1,0:T(8,128)(2,1)S(1)}, bf16[4,16,1024]{2,1,0:T(8,128)(2,1)S(1)}, u32[]{:S(2)}, u32[]{:S(2)}) collective-permute-start(bf16[4,16,1024]{2,1,0:T(8,128)(2,1)S(1)} %get-tuple-element.24), channel_id=1, source_target_pairs={{0,4},{4,8},{8,12},{12,0},{1,5},{5,9},{9,13},{13,1},{2,6},{6,10},{... | collective-permute-start | bytes 393224 | tf_op jit(solution)/shard_map/ppermute | solution.py:202
  20.4 6.3 %collective-permute-start.5 = (bf16[4,16,1024]{2,1,0:T(8,128)(2,1)S(1)}, bf16[4,16,1024]{2,1,0:T(8,128)(2,1)S(1)}, u32[]{:S(2)}, u32[]{:S(2)}) collective-permute-start(bf16[4,16,1024]{2,1,0:T(8,128)(2,1)S(1)} %get-tuple-element.24), channel_id=1, source_target_pairs={{0,12},{4,0},{8,4},{12,8},{1,13},{5,1},{9,5},{13,9},{2,14},{6,2},{... | collective-permute-start | bytes 393224 | tf_op jit(solution)/shard_map/ppermute | solution.py:202
  22.6 6.8 %collective-permute-start.12 = (bf16[2,16,1024]{2,1,0:T(8,128)(2,1)S(1)}, bf16[2,16,1024]{2,1,0:T(8,128)(2,1)S(1)}, u32[]{:S(2)}, u32[]{:S(2)}) collective-permute-start(bf16[2,16,1024]{2,1,0:T(8,128)(2,1)S(1)} %slice.49), channel_id=1, source_target_pairs={{0,1},{1,2},{2,3},{3,0},{4,5},{5,6},{6,7},{7,4},{8,9},{9,10},{10,1... | collective-permute-start | bytes 196616 | tf_op jit(solution)/shard_map/ppermute | solution.py:202
  23.0 6.3 %collective-permute-start.14 = (bf16[2,16,1024]{2,1,0:T(8,128)(2,1)S(1)}, bf16[2,16,1024]{2,1,0:T(8,128)(2,1)S(1)}, u32[]{:S(2)}, u32[]{:S(2)}) collective-permute-start(bf16[2,16,1024]{2,1,0:T(8,128)(2,1)S(1)} %slice.50), channel_id=1, source_target_pairs={{0,3},{1,0},{2,1},{3,2},{4,7},{5,4},{6,5},{7,6},{8,11},{9,8},{10,9... | collective-permute-start | bytes 196616 | tf_op jit(solution)/shard_map/ppermute | solution.py:202
  26.0 6.8 %collective-permute-start.4 = (bf16[2,16,1024]{2,1,0:T(8,128)(2,1)S(1)}, bf16[2,16,1024]{2,1,0:T(8,128)(2,1)S(1)}, u32[]{:S(2)}, u32[]{:S(2)}) collective-permute-start(bf16[2,16,1024]{2,1,0:T(8,128)(2,1)S(1)} %slice.45), channel_id=1, source_target_pairs={{0,4},{4,8},{8,12},{12,0},{1,5},{5,9},{9,13},{13,1},{2,6},{6,10},{... | collective-permute-start | bytes 196616 | tf_op jit(solution)/shard_map/ppermute | solution.py:202
  26.8 6.0 %collective-permute-start.6 = (bf16[2,16,1024]{2,1,0:T(8,128)(2,1)S(1)}, bf16[2,16,1024]{2,1,0:T(8,128)(2,1)S(1)}, u32[]{:S(2)}, u32[]{:S(2)}) collective-permute-start(bf16[2,16,1024]{2,1,0:T(8,128)(2,1)S(1)} %slice.46), channel_id=1, source_target_pairs={{0,12},{4,0},{8,4},{12,8},{1,13},{5,1},{9,5},{13,9},{2,14},{6,2},{... | collective-permute-start | bytes 196616 | tf_op jit(solution)/shard_map/ppermute | solution.py:202
  29.5 12.1 %collective-permute-start.15 = (bf16[4,4,16,1024]{3,2,1,0:T(8,128)(2,1)S(1)}, bf16[4,4,16,1024]{3,2,1,0:T(8,128)(2,1)S(1)}, u32[]{:S(2)}, u32[]{:S(2)}) collective-permute-start(bf16[4,4,16,1024]{3,2,1,0:T(8,128)(2,1)S(1)} %get-tuple-element.18), channel_id=1, source_target_pairs={{0,4},{4,8},{8,12},{12,0},{1,5},{5,9},{9,13},{13,1},{2,6},{6,10},{... | collective-permute-start | bytes 1572872 | tf_op jit(solution)/shard_map/ppermute | solution.py:202
  29.6 12.1 %collective-permute-start.17 = (bf16[4,4,16,1024]{3,2,1,0:T(8,128)(2,1)S(1)}, bf16[4,4,16,1024]{3,2,1,0:T(8,128)(2,1)S(1)}, u32[]{:S(2)}, u32[]{:S(2)}) collective-permute-start(bf16[4,4,16,1024]{3,2,1,0:T(8,128)(2,1)S(1)} %get-tuple-element.18), channel_id=1, source_target_pairs={{0,12},{4,0},{8,4},{12,8},{1,13},{5,1},{9,5},{13,9},{2,14},{6,2},{... | collective-permute-start | bytes 1572872 | tf_op jit(solution)/shard_map/ppermute | solution.py:202
  32.9 12.1 %collective-permute-start.7 = (bf16[4,4,16,1024]{3,2,1,0:T(8,128)(2,1)S(1)}, bf16[4,4,16,1024]{3,2,1,0:T(8,128)(2,1)S(1)}, u32[]{:S(2)}, u32[]{:S(2)}) collective-permute-start(bf16[4,4,16,1024]{3,2,1,0:T(8,128)(2,1)S(1)} %get-tuple-element.20), channel_id=1, source_target_pairs={{0,1},{1,2},{2,3},{3,0},{4,5},{5,6},{6,7},{7,4},{8,9},{9,10},{10,1... | collective-permute-start | bytes 1572872 | tf_op jit(solution)/shard_map/ppermute | solution.py:202
  33.0 12.2 %collective-permute-start.9 = (bf16[4,4,16,1024]{3,2,1,0:T(8,128)(2,1)S(1)}, bf16[4,4,16,1024]{3,2,1,0:T(8,128)(2,1)S(1)}, u32[]{:S(2)}, u32[]{:S(2)}) collective-permute-start(bf16[4,4,16,1024]{3,2,1,0:T(8,128)(2,1)S(1)} %get-tuple-element.20), channel_id=1, source_target_pairs={{0,3},{1,0},{2,1},{3,2},{4,7},{5,4},{6,5},{7,6},{8,11},{9,8},{10,9... | collective-permute-start | bytes 1572872 | tf_op jit(solution)/shard_map/ppermute | solution.py:202
  41.6 7.7 %collective-permute-start.16 = (bf16[2,4,16,1024]{3,2,1,0:T(8,128)(2,1)S(1)}, bf16[2,4,16,1024]{3,2,1,0:T(8,128)(2,1)S(1)}, u32[]{:S(2)}, u32[]{:S(2)}) collective-permute-start(bf16[2,4,16,1024]{3,2,1,0:T(8,128)(2,1)S(1)} %slice.51), channel_id=1, source_target_pairs={{0,4},{4,8},{8,12},{12,0},{1,5},{5,9},{9,13},{13,1},{2,6},{6,10},{... | collective-permute-start | bytes 786440 | tf_op jit(solution)/shard_map/ppermute | solution.py:202
  41.7 7.5 %collective-permute-start.18 = (bf16[2,4,16,1024]{3,2,1,0:T(8,128)(2,1)S(1)}, bf16[2,4,16,1024]{3,2,1,0:T(8,128)(2,1)S(1)}, u32[]{:S(2)}, u32[]{:S(2)}) collective-permute-start(bf16[2,4,16,1024]{3,2,1,0:T(8,128)(2,1)S(1)} %slice.52), channel_id=1, source_target_pairs={{0,12},{4,0},{8,4},{12,8},{1,13},{5,1},{9,5},{13,9},{2,14},{6,2},{... | collective-permute-start | bytes 786440 | tf_op jit(solution)/shard_map/ppermute | solution.py:202
  45.0 7.7 %collective-permute-start.8 = (bf16[2,4,16,1024]{3,2,1,0:T(8,128)(2,1)S(1)}, bf16[2,4,16,1024]{3,2,1,0:T(8,128)(2,1)S(1)}, u32[]{:S(2)}, u32[]{:S(2)}) collective-permute-start(bf16[2,4,16,1024]{3,2,1,0:T(8,128)(2,1)S(1)} %slice.47), channel_id=1, source_target_pairs={{0,1},{1,2},{2,3},{3,0},{4,5},{5,6},{6,7},{7,4},{8,9},{9,10},{10,1... | collective-permute-start | bytes 786440 | tf_op jit(solution)/shard_map/ppermute | solution.py:202
  45.2 7.5 %collective-permute-start.10 = (bf16[2,4,16,1024]{3,2,1,0:T(8,128)(2,1)S(1)}, bf16[2,4,16,1024]{3,2,1,0:T(8,128)(2,1)S(1)}, u32[]{:S(2)}, u32[]{:S(2)}) collective-permute-start(bf16[2,4,16,1024]{3,2,1,0:T(8,128)(2,1)S(1)} %slice.48), channel_id=1, source_target_pairs={{0,3},{1,0},{2,1},{3,2},{4,7},{5,4},{6,5},{7,6},{8,11},{9,8},{10,9... | collective-permute-start | bytes 786440 | tf_op jit(solution)/shard_map/ppermute | solution.py:202
  53.0 9.9 %copy-start.2 = (bf16[4,4,4,16,1024]{4,3,2,1,0:T(8,128)(2,1)}, bf16[4,4,4,16,1024]{4,3,2,1,0:T(8,128)(2,1)S(1)}, u32[]{:S(2)}) copy-start(bf16[4,4,4,16,1024]{4,3,2,1,0:T(8,128)(2,1)S(1)} %pad_maximum_fusion.1.here_b) | copy-start | bytes 6291460
  53.0 9.9 %copy-start.5 = (s32[16,4]{0,1:T(4,128)S(1)}, s32[16,4]{0,1:T(4,128)}, u32[]{:S(2)}) copy-start(s32[16,4]{0,1:T(4,128)} %param.6) | copy-start | bytes 772
  53.0 11.4 %copy-start.3 = (s32[16]{0:T(128)S(1)}, s32[16]{0:T(128)}, u32[]{:S(2)}) copy-start(s32[16]{0:T(128)} %counts.7) | copy-start | bytes 196
  62.4 13.5 %collective-permute-start.19 = (bf16[4,4,2,4,128,128]{5,4,3,2,1,0:T(8,128)(2,1)}, bf16[4,4,2,4,128,128]{5,4,3,2,1,0:T(8,128)(2,1)}, u32[]{:S(2)}, u32[]{:S(2)}) collective-permute-start(bf16[4,4,2,4,128,128]{5,4,3,2,1,0:T(8,128)(2,1)} %all-to-all-done.own_hbm), channel_id=1, source_target_pairs={{0,16},{16,0},{1,17},{17,1},{2,18},{18,2},{3,19},{19,3},{4,20},{20... | collective-permute-start | bytes 12582920 | tf_op jit(solution)/shard_map/ppermute | solution.py:206
  62.4 13.5 %collective-permute-start.20 = (bf16[4,4,4,16,1024]{4,3,2,1,0:T(8,128)(2,1)}, bf16[4,4,4,16,1024]{4,3,2,1,0:T(8,128)(2,1)}, u32[]{:S(2)}, u32[]{:S(2)}) collective-permute-start(bf16[4,4,4,16,1024]{4,3,2,1,0:T(8,128)(2,1)} %pad_maximum_fusion.here_a), channel_id=1, source_target_pairs={{0,16},{16,0},{1,17},{17,1},{2,18},{18,2},{3,19},{19,3},{4,20},{20... | collective-permute-start | bytes 6291464 | tf_op jit(solution)/shard_map/ppermute | solution.py:206
  63.0 13.0 %collective-permute-start.21 = (bf16[4,4,4,16,1024]{4,3,2,1,0:T(8,128)(2,1)S(1)}, bf16[4,4,4,16,1024]{4,3,2,1,0:T(8,128)(2,1)}, u32[]{:S(2)}, u32[]{:S(2)}) collective-permute-start(bf16[4,4,4,16,1024]{4,3,2,1,0:T(8,128)(2,1)S(1)} %pad_maximum_fusion.1.here_b), channel_id=1, source_target_pairs={{0,16},{16,0},{1,17},{17,1},{2,18},{18,2},{3,19},{19,3},{4,20},{20... | collective-permute-start | bytes 6291464 | tf_op jit(solution)/shard_map/ppermute | solution.py:206
  93.5 34.2 %all-to-all-start.1 = ((bf16[64,8,1536]{2,1,0:T(8,128)(2,1)}), bf16[64,8,1536]{2,1,0:T(8,128)(2,1)S(1)}, u32[]{:S(2)}, u32[]{:S(2)}) async-start(bf16[64,8,1536]{2,1,0:T(8,128)(2,1)} %bitcast.40), calls=%async_computation.1 | async-start | bytes 3145728 | tf_op jit(solution)/shard_map/all_to_all | solution.py:255
  127.7 4.9 %copy-start = (bf16[64,8,1536]{2,1,0:T(8,128)(2,1)}, bf16[64,8,1536]{2,1,0:T(8,128)(2,1)S(1)}, u32[]{:S(2)}) copy-start(bf16[64,8,1536]{2,1,0:T(8,128)(2,1)S(1)} %all-to-all-done.1.pieces) | copy-start | bytes 4718596
  127.7 28.2 %all-to-all-start.2 = ((bf16[64,8,1536]{2,1,0:T(8,128)(2,1)}), bf16[64,8,1536]{2,1,0:T(8,128)(2,1)S(1)}, u32[]{:S(2)}, u32[]{:S(2)}) async-start(bf16[64,8,1536]{2,1,0:T(8,128)(2,1)} %bitcast.39), calls=%async_computation.2 | async-start | bytes 3145728 | tf_op jit(solution)/shard_map/all_to_all | solution.py:255
  155.9 1.2 copy-start.1

commit v7 on v6

--- a/solution.py
+++ b/solution.py
@@ -1,5 +1,3 @@
-import functools
-
 import jax
 import jax.numpy as jnp
 from jax import lax
@@ -12,7 +10,6 @@
 LIVE = 1536
 LANES = 128
 PIECE = 128
-PARTS = 2
 
 
 def stacked(tensor, source, mi, aux, neigh):
@@ -25,26 +22,12 @@
     )
 
 
-def half_stack(tensor, source, mi, aux, neigh, size, part, piece):
-    rows = piece // PARTS
-    lines = []
-    for p in range(aux):
-        blocks = []
-        for j in range(neigh):
-            block = tensor[source, p, mi, j].astype(jnp.float32)
-            chosen = [block[at : at + rows] for at in range(part * rows, size, piece)]
-            blocks.append(jnp.concatenate(chosen, axis=0).astype(jnp.bfloat16))
-        lines.append(jnp.concatenate(blocks, axis=1))
-    return jnp.concatenate(lines, axis=0)
-
-
-def exchange_kernel(part, place, pairs, starts, shifts, counts, own_hbm, other_hbm, here_a, there_a,
+def exchange_kernel(place, pairs, starts, shifts, counts, own_hbm, other_hbm, here_a, there_a,
                     here_b, there_b, out_ref, own, other, density, halfway, total, sems):
     sources, aux, per_source, neigh, size, _ = own.shape
     piece, width = density.shape[-2:]
     blocks, rows, _ = halfway.shape
     x, core, z, y = place[0], place[1], place[2], place[3]
-    part_size = size // PARTS
 
     def copy(source, target, index):
         return pltpu.make_async_copy(source, target, sems.at[index])
@@ -75,7 +58,7 @@
         def first(b, carry):
             source, mi = b // per_source, b % per_source
             block = (source * CORES + core) * per_source + mi
-            lhs = half_stack(own, source, mi, aux, neigh, size, part, piece)
+            lhs = stacked(own, source, mi, aux, neigh)
             near = []
             for j in range(neigh):
                 partner = pairs[block * neigh + j]
@@ -90,11 +73,11 @@
             product = jnp.dot(
                 lhs, jnp.concatenate(near, axis=0), preferred_element_type=jnp.float32
             ).astype(jnp.bfloat16)
-            at = pl.ds(pl.multiple_of(b * part_size, part_size), part_size)
+            at = pl.ds(pl.multiple_of(b * size, size), size)
             for k in range(width // size):
                 for p in range(aux):
                     halfway[half * (width // size) + k, at, p * size : (p + 1) * size] = product[
-                        p * part_size : (p + 1) * part_size, k * size : (k + 1) * size
+                        p * size : (p + 1) * size, k * size : (k + 1) * size
                     ]
             return carry
 
@@ -139,14 +122,14 @@
         out_ref[:, at] += moved_columns
 
 
-def exchange_rows(part, place, pairs, starts, shifts, counts, own, other, here_a, there_a, here_b, there_b):
+def exchange_rows(place, pairs, starts, shifts, counts, own, other, here_a, there_a, here_b, there_b):
     sources, aux, per_source, neigh, size, _ = own.shape
     width = here_a.shape[-1]
     blocks = 2 * width // size
-    rows = sources * per_source * size // PARTS
+    rows = sources * per_source * size
     scalar, vector = pl.BlockSpec(memory_space=pltpu.SMEM), pl.BlockSpec(memory_space=pltpu.VMEM)
     return pl.pallas_call(
-        functools.partial(exchange_kernel, part),
+        exchange_kernel,
         out_shape=jax.ShapeDtypeStruct((rows, LIVE), jnp.bfloat16),
         in_specs=[scalar] * 5 + [pl.BlockSpec(memory_space=pl.ANY)] * 6,
         out_specs=vector,
@@ -244,18 +227,13 @@
 
     place = jnp.stack([x, core, z, y]).astype(jnp.int32)
     pairs = pair_blocks.reshape(-1)
-    part_rows = rows_here // PARTS
-    outputs = []
-    for part in range(PARTS):
-        partial = exchange_rows(
-            part, place, pairs, starts, shifts, basis_counts, own, other,
-            here_a, there_a, here_b, there_b,
-        )
-        partial = partial.reshape(-1, part_rows, LIVE)
-        pieces = lax.all_to_all(partial, ("x", "z", "y"), 0, 0, tiled=True)
-        still = (rows_live[0] - part * part_rows).astype(jnp.int32).reshape(1)
-        outputs.append(finish(still, starts, shifts, basis_counts, pieces, basis))
-    return jnp.concatenate(outputs, axis=0)
+    partial = exchange_rows(
+        place, pairs, starts, shifts, basis_counts, own, other, here_a, there_a, here_b, there_b
+    )
+    partial = partial.reshape(-1, rows_here, LIVE)
+    pieces = lax.all_to_all(partial, ("x", "z", "y"), 0, 0, tiled=True)
+    still = rows_live[0].astype(jnp.int32).reshape(1)
+    return finish(still, starts, shifts, basis_counts, pieces, basis)
 
 
 def solution(mesh):

time: 162 us -> 160 us (0.988)
  blocking collectives: 0 us -> 51.1 us
  waiting for transfers between devices: 57.5 us -> 30.4 us
  starting transfers between devices: 52.8 us -> 38 us
  Pallas kernels: 40.5 us -> 32.1 us
    all_to_all x0 -> x1, blocking collectives: none -> 51.1 us  [per_device(): pieces = lax.all_to_all(partial, ('x', 'z', 'y'), 0, 0, tiled=True)]
    all_to_all x2 -> x0, waiting for transfers between devices: 27 us -> none  [per_device(): pieces = lax.all_to_all(partial, ('x', 'z', 'y'), 0, 0, tiled=True)]
    all_to_all x2 -> x0, starting transfers between devices: 14.8 us -> none  [per_device(): pieces = lax.all_to_all(partial, ('x', 'z', 'y'), 0, 0, tiled=True)]
    pallas_call x2 -> x1, Pallas kernels: 35.1 us -> 28.4 us  [exchange_rows(): pl.pallas_call(exchange_kernel, out_shape=jax.ShapeDtypeStruct((rows, LIV...]
    pallas_call x2 -> x1, Pallas kernels: 5.45 us -> 3.71 us  [finish(): pl.pallas_call(finish_kernel, out_shape=jax.ShapeDtypeStruct((rows, basis...]
  transfers between devices with their start and end apart: 25 -> 23, of which waited for: 8 -> 6; matrix products, arithmetic and copies ran while one was open for 4% -> 4% of each run, Pallas kernels for 13% -> 0%
where the time goes in v7:
time: 160 us; the launch traced here: 159 us
  blocking collectives  51.1 us (32%)
  starting transfers between devices  38 us (24%)
  Pallas kernels  32.1 us (20%)
  waiting for transfers between devices  30.4 us (19%)
  other arithmetic  6.55 us (4%)
    all_to_all x1, blocking collectives, per_device(): pieces = lax.all_to_all(partial, ('x', 'z', 'y'), 0, 0, tiled=True)  51.1 us
    ppermute x19, starting transfers between devices, moved(): lax.ppermute(value, axis, [(k, (k + shift) % SIDE) for k in range(SIDE)])  32.6 us
    pallas_call x1, Pallas kernels, exchange_rows(): pl.pallas_call(exchange_kernel, out_shape=jax.ShapeDtypeStruct((rows, LIV...  28.4 us
    ppermute x19, waiting for transfers between devices, moved(): lax.ppermute(value, axis, [(k, (k + shift) % SIDE) for k in range(SIDE)])  12 us
    ppermute x3, waiting for transfers between devices, swapped(): return lax.ppermute(value, 'core', [(0, 1), (1, 0)])  10.9 us
    all_to_all x1, waiting for transfers between devices, per_device(): own = lax.all_to_all(parted, 'x', 0, 0, tiled=True)  7.43 us
    all_to_all x1, starting transfers between devices, per_device(): own = lax.all_to_all(parted, 'x', 0, 0, tiled=True)  4.9 us
    pallas_call x1, Pallas kernels, finish(): pl.pallas_call(finish_kernel, out_shape=jax.ShapeDtypeStruct((rows, basis...  3.71 us
  transfers between devices with their start and end apart: 23, of which 6 were waited for; matrix products, arithmetic and copies ran while one was open for 4% of the time, Pallas kernels for 0%

profile of v7, /device:TPU:0, one launch (start us, length us, event | category | flops | bytes accessed | tf_op | source)
XLA Modules:
  0.0 159.3 jit_solution(2541171371948618122)
XLA Ops:
  0.0 1.6 collective-permute-start
  1.6 1.7 %collective-permute-start.2 = (bf16[16,2048]{1,0:T(8,128)(2,1)}, bf16[16,2048]{1,0:T(8,128)(2,1)S(1)}, u32[]{:S(2)}, u32[]{:S(2)}) collective-permute-start(bf16[16,2048]{1,0:T(8,128)(2,1)} %param.5), channel_id=1, source_target_pairs={{0,96},{32,0},{64,32},{96,64},{1,97},{33,1},{65,33},{97,65},{2,98}... | collective-permute-start | bytes 196616 | tf_op jit(solution)/shard_map/ppermute | solution.py:185
  3.2 1.9 %collective-permute-start.1 = (bf16[16,2048]{1,0:T(8,128)(2,1)}, bf16[16,2048]{1,0:T(8,128)(2,1)S(1)}, u32[]{:S(2)}, u32[]{:S(2)}) collective-permute-start(bf16[16,2048]{1,0:T(8,128)(2,1)} %param.5), channel_id=1, source_target_pairs={{0,64},{32,96},{64,0},{96,32},{1,65},{33,97},{65,1},{97,33},{2,66}... | collective-permute-start | bytes 196616 | tf_op jit(solution)/shard_map/ppermute | solution.py:185
  5.1 0.7 fusion
  5.9 0.8 select_reduce_fusion.1
  6.8 0.1 iota_compare_fusion.2
  6.8 0.0 collective-permute-done
  6.8 0.0 collective-permute-done.2
  6.8 2.4 %collective-permute-done.1 = bf16[16,2048]{1,0:T(8,128)(2,1)S(1)} collective-permute-done((bf16[16,2048]{1,0:T(8,128)(2,1)}, bf16[16,2048]{1,0:T(8,128)(2,1)S(1)}, u32[]{:S(2)}, u32[]{:S(2)}) %collective-permute-start.1) | collective-permute-done | bytes 65568 | tf_op jit(solution)/shard_map/ppermute | solution.py:185
  9.2 1.0 and_select_fusion
  10.2 4.9 %all-to-all-start = ((bf16[4,4,2,4,128,128]{5,4,3,2,1,0:T(8,128)(2,1)}), bf16[4,4,2,4,128,128]{5,4,3,2,1,0:T(8,128)(2,1)}, u32[]{:S(2)}, u32[]{:S(2)}) async-start(bf16[4,4,2,4,128,128]{5,4,3,2,1,0:T(8,128)(2,1)} %bitcast.37), calls=%async_computation | async-start | bytes 8388608 | tf_op jit(solution)/shard_map/all_to_all | solution.py:224
  15.2 1.7 %collective-permute-start.11 = (bf16[4,16,1024]{2,1,0:T(8,128)(2,1)S(1)}, bf16[4,16,1024]{2,1,0:T(8,128)(2,1)S(1)}, u32[]{:S(2)}, u32[]{:S(2)}) collective-permute-start(bf16[4,16,1024]{2,1,0:T(8,128)(2,1)S(1)} %get-tuple-element.23), channel_id=1, source_target_pairs={{0,1},{1,2},{2,3},{3,0},{4,5},{5,6},{6,7},{7,4},{8,9},{9,10},{10,1... | collective-permute-start | bytes 393224 | tf_op jit(solution)/shard_map/ppermute | solution.py:185
  16.9 1.6 collective-permute-start.13
  18.5 2.0 %collective-permute-start.3 = (bf16[4,16,1024]{2,1,0:T(8,128)(2,1)S(1)}, bf16[4,16,1024]{2,1,0:T(8,128)(2,1)S(1)}, u32[]{:S(2)}, u32[]{:S(2)}) collective-permute-start(bf16[4,16,1024]{2,1,0:T(8,128)(2,1)S(1)} %get-tuple-element.24), channel_id=1, source_target_pairs={{0,4},{4,8},{8,12},{12,0},{1,5},{5,9},{9,13},{13,1},{2,6},{6,10},{... | collective-permute-start | bytes 393224 | tf_op jit(solution)/shard_map/ppermute | solution.py:185
  20.5 2.1 %collective-permute-start.5 = (bf16[4,16,1024]{2,1,0:T(8,128)(2,1)S(1)}, bf16[4,16,1024]{2,1,0:T(8,128)(2,1)S(1)}, u32[]{:S(2)}, u32[]{:S(2)}) collective-permute-start(bf16[4,16,1024]{2,1,0:T(8,128)(2,1)S(1)} %get-tuple-element.24), channel_id=1, source_target_pairs={{0,12},{4,0},{8,4},{12,8},{1,13},{5,1},{9,5},{13,9},{2,14},{6,2},{... | collective-permute-start | bytes 393224 | tf_op jit(solution)/shard_map/ppermute | solution.py:185
  22.6 0.4 collective-permute-start.12
  23.1 2.9 %collective-permute-start.14 = (bf16[2,16,1024]{2,1,0:T(8,128)(2,1)S(1)}, bf16[2,16,1024]{2,1,0:T(8,128)(2,1)S(1)}, u32[]{:S(2)}, u32[]{:S(2)}) collective-permute-start(bf16[2,16,1024]{2,1,0:T(8,128)(2,1)S(1)} %slice.49), channel_id=1, source_target_pairs={{0,3},{1,0},{2,1},{3,2},{4,7},{5,4},{6,5},{7,6},{8,11},{9,8},{10,9... | collective-permute-start | bytes 196616 | tf_op jit(solution)/shard_map/ppermute | solution.py:185
  26.0 0.8 collective-permute-start.4
  26.8 2.6 %collective-permute-start.6 = (bf16[2,16,1024]{2,1,0:T(8,128)(2,1)S(1)}, bf16[2,16,1024]{2,1,0:T(8,128)(2,1)S(1)}, u32[]{:S(2)}, u32[]{:S(2)}) collective-permute-start(bf16[2,16,1024]{2,1,0:T(8,128)(2,1)S(1)} %slice.45), channel_id=1, source_target_pairs={{0,12},{4,0},{8,4},{12,8},{1,13},{5,1},{9,5},{13,9},{2,14},{6,2},{... | collective-permute-start | bytes 196616 | tf_op jit(solution)/shard_map/ppermute | solution.py:185
  29.4 0.1 fusion.8
  29.5 0.1 collective-permute-start.15
  29.6 3.2 %collective-permute-start.17 = (bf16[4,4,16,1024]{3,2,1,0:T(8,128)(2,1)S(1)}, bf16[4,4,16,1024]{3,2,1,0:T(8,128)(2,1)S(1)}, u32[]{:S(2)}, u32[]{:S(2)}) collective-permute-start(bf16[4,4,16,1024]{3,2,1,0:T(8,128)(2,1)S(1)} %get-tuple-element.18), channel_id=1, source_target_pairs={{0,12},{4,0},{8,4},{12,8},{1,13},{5,1},{9,5},{13,9},{2,14},{6,2},{... | collective-permute-start | bytes 1572872 | tf_op jit(solution)/shard_map/ppermute | solution.py:185
  32.9 0.1 fusion.9
  33.0 0.1 collective-permute-start.7
  33.0 3.2 %collective-permute-start.9 = (bf16[4,4,16,1024]{3,2,1,0:T(8,128)(2,1)S(1)}, bf16[4,4,16,1024]{3,2,1,0:T(8,128)(2,1)S(1)}, u32[]{:S(2)}, u32[]{:S(2)}) collective-permute-start(bf16[4,4,16,1024]{3,2,1,0:T(8,128)(2,1)S(1)} %get-tuple-element.20), channel_id=1, source_target_pairs={{0,3},{1,0},{2,1},{3,2},{4,7},{5,4},{6,5},{7,6},{8,11},{9,8},{10,9... | collective-permute-start | bytes 1572872 | tf_op jit(solution)/shard_map/ppermute | solution.py:185
  36.3 5.4 %collective-permute-done.15 = bf16[4,4,16,1024]{3,2,1,0:T(8,128)(2,1)S(1)} collective-permute-done((bf16[4,4,16,1024]{3,2,1,0:T(8,128)(2,1)S(1)}, bf16[4,4,16,1024]{3,2,1,0:T(8,128)(2,1)S(1)}, u32[]{:S(2)}, u32[]{:S(2)}) %collective-permute-start.15) | collective-permute-done | bytes 524320 | tf_op jit(solution)/shard_map/ppermute | solution.py:185
  41.7 0.1 collective-permute-start.16
  41.8 3.3 %collective-permute-start.18 = (bf16[2,4,16,1024]{3,2,1,0:T(8,128)(2,1)S(1)}, bf16[2,4,16,1024]{3,2,1,0:T(8,128)(2,1)S(1)}, u32[]{:S(2)}, u32[]{:S(2)}) collective-permute-start(bf16[2,4,16,1024]{3,2,1,0:T(8,128)(2,1)S(1)} %slice.51), channel_id=1, source_target_pairs={{0,12},{4,0},{8,4},{12,8},{1,13},{5,1},{9,5},{13,9},{2,14},{6,2},{... | collective-permute-start | bytes 786440 | tf_op jit(solution)/shard_map/ppermute | solution.py:185
  45.1 0.1 collective-permute-start.8
  45.2 3.2 %collective-permute-start.10 = (bf16[2,4,16,1024]{3,2,1,0:T(8,128)(2,1)S(1)}, bf16[2,4,16,1024]{3,2,1,0:T(8,128)(2,1)S(1)}, u32[]{:S(2)}, u32[]{:S(2)}) collective-permute-start(bf16[2,4,16,1024]{3,2,1,0:T(8,128)(2,1)S(1)} %slice.47), channel_id=1, source_target_pairs={{0,3},{1,0},{2,1},{3,2},{4,7},{5,4},{6,5},{7,6},{8,11},{9,8},{10,9... | collective-permute-start | bytes 786440 | tf_op jit(solution)/shard_map/ppermute | solution.py:185
  48.5 0.8 collective-permute-done.16
  49.4 3.4 %collective-permute-done.8 = bf16[2,4,16,1024]{3,2,1,0:T(8,128)(2,1)S(1)} collective-permute-done((bf16[2,4,16,1024]{3,2,1,0:T(8,128)(2,1)S(1)}, bf16[2,4,16,1024]{3,2,1,0:T(8,128)(2,1)S(1)}, u32[]{:S(2)}, u32[]{:S(2)}) %collective-permute-start.8) | collective-permute-done | bytes 262176 | tf_op jit(solution)/shard_map/ppermute | solution.py:185
  52.8 0.3 pad_maximum_fusion.1.here_b
  53.1 0.0 copy-start.1
  53.1 0.0 copy-start.2
  53.1 2.0 %pad_maximum_fusion.here_a = bf16[4,4,4,16,1024]{4,3,2,1,0:T(8,128)(2,1)} fusion(bf16[1,4,4,16,1024]{4,3,2,1,0:T(8,128)(2,1)S(1)} %bitcast.42, bf16[1,4,4,16,1024]{4,3,2,1,0:T(8,128)(2,1)S(1)} %maximum_bitcast_fusion, bf16[1,4,4,16,1024]{4,3,2,1,0:T(8,128)(2,1)S(1)} %bitcast.41, bf16[1,4,4,16,1024]{4,3,2,1,0:T(8,128)(2,1)S(1)} %get-tuple-element.19), kind=kLoop, calls=%fused_computation | loop fusion | flops 3145728 | bytes 4194304 | tf_op jit(solution)/shard_map/stack | solution.py:196
  55.1 7.4 %all-to-all-done.own_hbm = bf16[4,4,2,4,128,128]{5,4,3,2,1,0:T(8,128)(2,1)} async-done(((bf16[4,4,2,4,128,128]{5,4,3,2,1,0:T(8,128)(2,1)}), bf16[4,4,2,4,128,128]{5,4,3,2,1,0:T(8,128)(2,1)}, u32[]{:S(2)}, u32[]{:S(2)}) %all-to-all-start) | async-done | bytes 4194336 | tf_op jit(solution)/shard_map/all_to_all | solution.py:224
  62.5 0.5 collective-permute-start.20
  63.0 0.0 collective-permute-start.21
  63.0 0.1 copy.7
  63.1 0.6 reshape.91.pairs
  63.7 0.7 pad_add_fusion.place
  64.4 0.1 select_reduce_fusion
  64.5 0.6 multiply_subtract_fusion
  65.1 10.9 %collective-permute-done.20.there_a = bf16[4,4,4,16,1024]{4,3,2,1,0:T(8,128)(2,1)} collective-permute-done((bf16[4,4,4,16,1024]{4,3,2,1,0:T(8,128)(2,1)}, bf16[4,4,4,16,1024]{4,3,2,1,0:T(8,128)(2,1)}, u32[]{:S(2)}, u32[]{:S(2)}) %collective-permute-start.20) | collective-permute-done | bytes 2097184 | tf_op jit(solution)/shard_map/ppermute | solution.py:189
  76.0 28.4 %shard_map.46 = bf16[1024,1536]{1,0:T(8,128)(2,1)} custom-call(s32[4]{0:T(128)} %pad_add_fusion.place, s32[64]{0:T(128)} %reshape.91.pairs, s32[16]{0:T(128)} %get-tuple-element.16.starts, s32[16]{0:T(128)} %get-tuple-element.15.shifts, s32[16]{0:T(128)} %counts.3, bf16[4,4,2,4,128,128]{5,4,3,2,1,0:T(8,128)(2,1)} %all-to-all-done.own_hbm, ...), custom_call_target="tpu_custom_call" | custom-call | flops 17179869184 | bytes 19922944 | tf_op jit(solution)/shard_map/pallas_call | solution.py:131
  104.4 51.1 %all_to_all.10.pieces = bf16[64,16,1536]{2,1,0:T(8,128)(2,1)} all-to-all(bf16[64,16,1536]{2,1,0:T(8,128)(2,1)} %bitcast.38), channel_id=1, replica_groups=mesh['x'=4,'core'=2,'z'=4,'y'=4] {'x','z','y'}, dimensions={0} | all-to-all | bytes 6291456 | tf_op jit(solution)/shard_map/all_to_all | solution.py:234
  155.6 3.7 %shard_map.47 = f32[16,2048]{1,0:T(8,128)} custom-call(s32[1]{0:T(128)} %bitcast.51, s32[16]{0:T(128)} %get-tuple-element.16.starts, s32[16]{0:T(128)} %get-tuple-element.15.shifts, s32[16]{0:T(128)} %counts.3, bf16[64,16,1536]{2,1,0:T(8,128)(2,1)} %all_to_all.10.pieces), custom_call_target="tpu_custom_call" | custom-call | tf_op jit(solution)/shard_map/pallas_call | solution.py:175
  (37 shorter events, 0.4 us)
Async XLA Ops:
  0.0 6.8 %collective-permute-start = (bf16[16,2048]{1,0:T(8,128)(2,1)}, bf16[16,2048]{1,0:T(8,128)(2,1)S(1)}, u32[]{:S(2)}, u32[]{:S(2)}) collective-permute-start(bf16[16,2048]{1,0:T(8,128)(2,1)} %param.5), channel_id=1, source_target_pairs={{0,32},{32,64},{64,96},{96,0},{1,33},{33,65},{65,97},{97,1},{2,34}... | collective-permute-start | bytes 196616 | tf_op jit(solution)/shard_map/ppermute | solution.py:185
  1.6 5.3 %collective-permute-start.2 = (bf16[16,2048]{1,0:T(8,128)(2,1)}, bf16[16,2048]{1,0:T(8,128)(2,1)S(1)}, u32[]{:S(2)}, u32[]{:S(2)}) collective-permute-start(bf16[16,2048]{1,0:T(8,128)(2,1)} %param.5), channel_id=1, source_target_pairs={{0,96},{32,0},{64,32},{96,64},{1,97},{33,1},{65,33},{97,65},{2,98}... | collective-permute-start | bytes 196616 | tf_op jit(solution)/shard_map/ppermute | solution.py:185
  3.2 6.0 %collective-permute-start.1 = (bf16[16,2048]{1,0:T(8,128)(2,1)}, bf16[16,2048]{1,0:T(8,128)(2,1)S(1)}, u32[]{:S(2)}, u32[]{:S(2)}) collective-permute-start(bf16[16,2048]{1,0:T(8,128)(2,1)} %param.5), channel_id=1, source_target_pairs={{0,64},{32,96},{64,0},{96,32},{1,65},{33,97},{65,1},{97,33},{2,66}... | collective-permute-start | bytes 196616 | tf_op jit(solution)/shard_map/ppermute | solution.py:185
  6.7 3.5 %copy-start.3 = (s32[4]{0:T(128)}, s32[4]{0:T(128)S(1)}, u32[]{:S(2)}) copy-start(s32[4]{0:T(128)S(1)} %fusion.1) | copy-start | bytes 52
  10.2 52.3 %all-to-all-start = ((bf16[4,4,2,4,128,128]{5,4,3,2,1,0:T(8,128)(2,1)}), bf16[4,4,2,4,128,128]{5,4,3,2,1,0:T(8,128)(2,1)}, u32[]{:S(2)}, u32[]{:S(2)}) async-start(bf16[4,4,2,4,128,128]{5,4,3,2,1,0:T(8,128)(2,1)} %bitcast.37), calls=%async_computation | async-start | bytes 8388608 | tf_op jit(solution)/shard_map/all_to_all | solution.py:224
  15.2 7.4 %collective-permute-start.11 = (bf16[4,16,1024]{2,1,0:T(8,128)(2,1)S(1)}, bf16[4,16,1024]{2,1,0:T(8,128)(2,1)S(1)}, u32[]{:S(2)}, u32[]{:S(2)}) collective-permute-start(bf16[4,16,1024]{2,1,0:T(8,128)(2,1)S(1)} %get-tuple-element.23), channel_id=1, source_target_pairs={{0,1},{1,2},{2,3},{3,0},{4,5},{5,6},{6,7},{7,4},{8,9},{9,10},{10,1... | collective-permute-start | bytes 393224 | tf_op jit(solution)/shard_map/ppermute | solution.py:185
  16.9 6.2 %collective-permute-start.13 = (bf16[4,16,1024]{2,1,0:T(8,128)(2,1)S(1)}, bf16[4,16,1024]{2,1,0:T(8,128)(2,1)S(1)}, u32[]{:S(2)}, u32[]{:S(2)}) collective-permute-start(bf16[4,16,1024]{2,1,0:T(8,128)(2,1)S(1)} %get-tuple-element.23), channel_id=1, source_target_pairs={{0,3},{1,0},{2,1},{3,2},{4,7},{5,4},{6,5},{7,6},{8,11},{9,8},{10,9... | collective-permute-start | bytes 393224 | tf_op jit(solution)/shard_map/ppermute | solution.py:185
  18.5 7.5 %collective-permute-start.3 = (bf16[4,16,1024]{2,1,0:T(8,128)(2,1)S(1)}, bf16[4,16,1024]{2,1,0:T(8,128)(2,1)S(1)}, u32[]{:S(2)}, u32[]{:S(2)}) collective-permute-start(bf16[4,16,1024]{2,1,0:T(8,128)(2,1)S(1)} %get-tuple-element.24), channel_id=1, source_target_pairs={{0,4},{4,8},{8,12},{12,0},{1,5},{5,9},{9,13},{13,1},{2,6},{6,10},{... | collective-permute-start | bytes 393224 | tf_op jit(solution)/shard_map/ppermute | solution.py:185
  20.5 6.3 %collective-permute-start.5 = (bf16[4,16,1024]{2,1,0:T(8,128)(2,1)S(1)}, bf16[4,16,1024]{2,1,0:T(8,128)(2,1)S(1)}, u32[]{:S(2)}, u32[]{:S(2)}) collective-permute-start(bf16[4,16,1024]{2,1,0:T(8,128)(2,1)S(1)} %get-tuple-element.24), channel_id=1, source_target_pairs={{0,12},{4,0},{8,4},{12,8},{1,13},{5,1},{9,5},{13,9},{2,14},{6,2},{... | collective-permute-start | bytes 393224 | tf_op jit(solution)/shard_map/ppermute | solution.py:185
  22.6 6.8 %collective-permute-start.12 = (bf16[2,16,1024]{2,1,0:T(8,128)(2,1)S(1)}, bf16[2,16,1024]{2,1,0:T(8,128)(2,1)S(1)}, u32[]{:S(2)}, u32[]{:S(2)}) collective-permute-start(bf16[2,16,1024]{2,1,0:T(8,128)(2,1)S(1)} %slice.48), channel_id=1, source_target_pairs={{0,1},{1,2},{2,3},{3,0},{4,5},{5,6},{6,7},{7,4},{8,9},{9,10},{10,1... | collective-permute-start | bytes 196616 | tf_op jit(solution)/shard_map/ppermute | solution.py:185
  23.1 6.3 %collective-permute-start.14 = (bf16[2,16,1024]{2,1,0:T(8,128)(2,1)S(1)}, bf16[2,16,1024]{2,1,0:T(8,128)(2,1)S(1)}, u32[]{:S(2)}, u32[]{:S(2)}) collective-permute-start(bf16[2,16,1024]{2,1,0:T(8,128)(2,1)S(1)} %slice.49), channel_id=1, source_target_pairs={{0,3},{1,0},{2,1},{3,2},{4,7},{5,4},{6,5},{7,6},{8,11},{9,8},{10,9... | collective-permute-start | bytes 196616 | tf_op jit(solution)/shard_map/ppermute | solution.py:185
  26.0 6.8 %collective-permute-start.4 = (bf16[2,16,1024]{2,1,0:T(8,128)(2,1)S(1)}, bf16[2,16,1024]{2,1,0:T(8,128)(2,1)S(1)}, u32[]{:S(2)}, u32[]{:S(2)}) collective-permute-start(bf16[2,16,1024]{2,1,0:T(8,128)(2,1)S(1)} %slice.44), channel_id=1, source_target_pairs={{0,4},{4,8},{8,12},{12,0},{1,5},{5,9},{9,13},{13,1},{2,6},{6,10},{... | collective-permute-start | bytes 196616 | tf_op jit(solution)/shard_map/ppermute | solution.py:185
  26.8 6.0 %collective-permute-start.6 = (bf16[2,16,1024]{2,1,0:T(8,128)(2,1)S(1)}, bf16[2,16,1024]{2,1,0:T(8,128)(2,1)S(1)}, u32[]{:S(2)}, u32[]{:S(2)}) collective-permute-start(bf16[2,16,1024]{2,1,0:T(8,128)(2,1)S(1)} %slice.45), channel_id=1, source_target_pairs={{0,12},{4,0},{8,4},{12,8},{1,13},{5,1},{9,5},{13,9},{2,14},{6,2},{... | collective-permute-start | bytes 196616 | tf_op jit(solution)/shard_map/ppermute | solution.py:185
  29.5 12.1 %collective-permute-start.15 = (bf16[4,4,16,1024]{3,2,1,0:T(8,128)(2,1)S(1)}, bf16[4,4,16,1024]{3,2,1,0:T(8,128)(2,1)S(1)}, u32[]{:S(2)}, u32[]{:S(2)}) collective-permute-start(bf16[4,4,16,1024]{3,2,1,0:T(8,128)(2,1)S(1)} %get-tuple-element.18), channel_id=1, source_target_pairs={{0,4},{4,8},{8,12},{12,0},{1,5},{5,9},{9,13},{13,1},{2,6},{6,10},{... | collective-permute-start | bytes 1572872 | tf_op jit(solution)/shard_map/ppermute | solution.py:185
  29.6 12.1 %collective-permute-start.17 = (bf16[4,4,16,1024]{3,2,1,0:T(8,128)(2,1)S(1)}, bf16[4,4,16,1024]{3,2,1,0:T(8,128)(2,1)S(1)}, u32[]{:S(2)}, u32[]{:S(2)}) collective-permute-start(bf16[4,4,16,1024]{3,2,1,0:T(8,128)(2,1)S(1)} %get-tuple-element.18), channel_id=1, source_target_pairs={{0,12},{4,0},{8,4},{12,8},{1,13},{5,1},{9,5},{13,9},{2,14},{6,2},{... | collective-permute-start | bytes 1572872 | tf_op jit(solution)/shard_map/ppermute | solution.py:185
  33.0 12.1 %collective-permute-start.7 = (bf16[4,4,16,1024]{3,2,1,0:T(8,128)(2,1)S(1)}, bf16[4,4,16,1024]{3,2,1,0:T(8,128)(2,1)S(1)}, u32[]{:S(2)}, u32[]{:S(2)}) collective-permute-start(bf16[4,4,16,1024]{3,2,1,0:T(8,128)(2,1)S(1)} %get-tuple-element.20), channel_id=1, source_target_pairs={{0,1},{1,2},{2,3},{3,0},{4,5},{5,6},{6,7},{7,4},{8,9},{9,10},{10,1... | collective-permute-start | bytes 1572872 | tf_op jit(solution)/shard_map/ppermute | solution.py:185
  33.0 12.2 %collective-permute-start.9 = (bf16[4,4,16,1024]{3,2,1,0:T(8,128)(2,1)S(1)}, bf16[4,4,16,1024]{3,2,1,0:T(8,128)(2,1)S(1)}, u32[]{:S(2)}, u32[]{:S(2)}) collective-permute-start(bf16[4,4,16,1024]{3,2,1,0:T(8,128)(2,1)S(1)} %get-tuple-element.20), channel_id=1, source_target_pairs={{0,3},{1,0},{2,1},{3,2},{4,7},{5,4},{6,5},{7,6},{8,11},{9,8},{10,9... | collective-permute-start | bytes 1572872 | tf_op jit(solution)/shard_map/ppermute | solution.py:185
  41.7 7.7 %collective-permute-start.16 = (bf16[2,4,16,1024]{3,2,1,0:T(8,128)(2,1)S(1)}, bf16[2,4,16,1024]{3,2,1,0:T(8,128)(2,1)S(1)}, u32[]{:S(2)}, u32[]{:S(2)}) collective-permute-start(bf16[2,4,16,1024]{3,2,1,0:T(8,128)(2,1)S(1)} %slice.50), channel_id=1, source_target_pairs={{0,4},{4,8},{8,12},{12,0},{1,5},{5,9},{9,13},{13,1},{2,6},{6,10},{... | collective-permute-start | bytes 786440 | tf_op jit(solution)/shard_map/ppermute | solution.py:185
  41.8 7.5 %collective-permute-start.18 = (bf16[2,4,16,1024]{3,2,1,0:T(8,128)(2,1)S(1)}, bf16[2,4,16,1024]{3,2,1,0:T(8,128)(2,1)S(1)}, u32[]{:S(2)}, u32[]{:S(2)}) collective-permute-start(bf16[2,4,16,1024]{3,2,1,0:T(8,128)(2,1)S(1)} %slice.51), channel_id=1, source_target_pairs={{0,12},{4,0},{8,4},{12,8},{1,13},{5,1},{9,5},{13,9},{2,14},{6,2},{... | collective-permute-start | bytes 786440 | tf_op jit(solution)/shard_map/ppermute | solution.py:185
  45.1 7.7 %collective-permute-start.8 = (bf16[2,4,16,1024]{3,2,1,0:T(8,128)(2,1)S(1)}, bf16[2,4,16,1024]{3,2,1,0:T(8,128)(2,1)S(1)}, u32[]{:S(2)}, u32[]{:S(2)}) collective-permute-start(bf16[2,4,16,1024]{3,2,1,0:T(8,128)(2,1)S(1)} %slice.46), channel_id=1, source_target_pairs={{0,1},{1,2},{2,3},{3,0},{4,5},{5,6},{6,7},{7,4},{8,9},{9,10},{10,1... | collective-permute-start | bytes 786440 | tf_op jit(solution)/shard_map/ppermute | solution.py:185
  45.2 7.5 %collective-permute-start.10 = (bf16[2,4,16,1024]{3,2,1,0:T(8,128)(2,1)S(1)}, bf16[2,4,16,1024]{3,2,1,0:T(8,128)(2,1)S(1)}, u32[]{:S(2)}, u32[]{:S(2)}) collective-permute-start(bf16[2,4,16,1024]{3,2,1,0:T(8,128)(2,1)S(1)} %slice.47), channel_id=1, source_target_pairs={{0,3},{1,0},{2,1},{3,2},{4,7},{5,4},{6,5},{7,6},{8,11},{9,8},{10,9... | collective-permute-start | bytes 786440 | tf_op jit(solution)/shard_map/ppermute | solution.py:185
  53.1 9.9 %copy-start = (bf16[4,4,4,16,1024]{4,3,2,1,0:T(8,128)(2,1)}, bf16[4,4,4,16,1024]{4,3,2,1,0:T(8,128)(2,1)S(1)}, u32[]{:S(2)}) copy-start(bf16[4,4,4,16,1024]{4,3,2,1,0:T(8,128)(2,1)S(1)} %pad_maximum_fusion.1.here_b) | copy-start | bytes 6291460
  53.1 9.9 %copy-start.1 = (s32[16,4]{0,1:T(4,128)S(1)}, s32[16,4]{0,1:T(4,128)}, u32[]{:S(2)}) copy-start(s32[16,4]{0,1:T(4,128)} %param.6) | copy-start | bytes 772
  53.1 11.3 %copy-start.2 = (s32[16]{0:T(128)S(1)}, s32[16]{0:T(128)}, u32[]{:S(2)}) copy-start(s32[16]{0:T(128)} %counts.3) | copy-start | bytes 196
  62.5 13.5 %collective-permute-start.19 = (bf16[4,4,2,4,128,128]{5,4,3,2,1,0:T(8,128)(2,1)}, bf16[4,4,2,4,128,128]{5,4,3,2,1,0:T(8,128)(2,1)}, u32[]{:S(2)}, u32[]{:S(2)}) collective-permute-start(bf16[4,4,2,4,128,128]{5,4,3,2,1,0:T(8,128)(2,1)} %all-to-all-done.own_hbm), channel_id=1, source_target_pairs={{0,16},{16,0},{1,17},{17,1},{2,18},{18,2},{3,19},{19,3},{4,20},{20... | collective-permute-start | bytes 12582920 | tf_op jit(solution)/shard_map/ppermute | solution.py:189
  62.5 13.5 %collective-permute-start.20 = (bf16[4,4,4,16,1024]{4,3,2,1,0:T(8,128)(2,1)}, bf16[4,4,4,16,1024]{4,3,2,1,0:T(8,128)(2,1)}, u32[]{:S(2)}, u32[]{:S(2)}) collective-permute-start(bf16[4,4,4,16,1024]{4,3,2,1,0:T(8,128)(2,1)} %pad_maximum_fusion.here_a), channel_id=1, source_target_pairs={{0,16},{16,0},{1,17},{17,1},{2,18},{18,2},{3,19},{19,3},{4,20},{20... | collective-permute-start | bytes 6291464 | tf_op jit(solution)/shard_map/ppermute | solution.py:189
  63.0 13.0 %collective-permute-start.21 = (bf16[4,4,4,16,1024]{4,3,2,1,0:T(8,128)(2,1)S(1)}, bf16[4,4,4,16,1024]{4,3,2,1,0:T(8,128)(2,1)}, u32[]{:S(2)}, u32[]{:S(2)}) collective-permute-start(bf16[4,4,4,16,1024]{4,3,2,1,0:T(8,128)(2,1)S(1)} %pad_maximum_fusion.1.here_b), channel_id=1, source_target_pairs={{0,16},{16,0},{1,17},{17,1},{2,18},{18,2},{3,19},{19,3},{4,20},{20... | collective-permute-start | bytes 6291464 | tf_op jit(solution)/shard_map/ppermute | solution.py:189

commit v8 on v7

--- a/solution.py
+++ b/solution.py
@@ -22,8 +22,9 @@
     )
 
 
-def exchange_kernel(place, pairs, starts, shifts, counts, own_hbm, other_hbm, here_a, there_a,
-                    here_b, there_b, out_ref, own, other, density, halfway, total, sems):
+def exchange_kernel(place, pairs, starts, shifts, counts, own_hbm, other_hbm, here_a, here_b, *refs):
+    there_a, there_b = refs[:SIDE], refs[SIDE : 2 * SIDE]
+    out_ref, own, other, density, halfway, total, sems = refs[2 * SIDE :]
     sources, aux, per_source, neigh, size, _ = own.shape
     piece, width = density.shape[-2:]
     blocks, rows, _ = halfway.shape
@@ -33,15 +34,15 @@
         return pltpu.make_async_copy(source, target, sems.at[index])
 
     own_copies = [copy(own_hbm.at[s], own.at[s], s) for s in range(sources)]
-    first_copies = [
-        copy(here_a, density.at[0, 0], sources),
-        copy(there_a, density.at[0, 1], sources + 1),
-    ]
-    next_copies = [
-        copy(here_b, density.at[1, 0], sources + 2),
-        copy(there_b, density.at[1, 1], sources + 3),
-    ]
-    last_copy = copy(other_hbm, other, sources + 4)
+    def density_copies(half, here, there, index):
+        copies = [copy(here, density.at[half, 0], index)]
+        for back in range(SIDE):
+            copies.append(copy(there[back], density.at[half, 1, back], index + 1 + back))
+        return copies
+
+    first_copies = density_copies(0, here_a, there_a, sources)
+    next_copies = density_copies(1, here_b, there_b, sources + SIDE + 1)
+    last_copy = copy(other_hbm, other, sources + 2 * SIDE + 2)
     for one in own_copies[:1] + first_copies:
         one.start()
     for one in first_copies:
@@ -122,7 +123,7 @@
         out_ref[:, at] += moved_columns
 
 
-def exchange_rows(place, pairs, starts, shifts, counts, own, other, here_a, there_a, here_b, there_b):
+def exchange_rows(place, pairs, starts, shifts, counts, own, other, here_a, here_b, there_a, there_b):
     sources, aux, per_source, neigh, size, _ = own.shape
     width = here_a.shape[-1]
     blocks = 2 * width // size
@@ -131,7 +132,7 @@
     return pl.pallas_call(
         exchange_kernel,
         out_shape=jax.ShapeDtypeStruct((rows, LIVE), jnp.bfloat16),
-        in_specs=[scalar] * 5 + [pl.BlockSpec(memory_space=pl.ANY)] * 6,
+        in_specs=[scalar] * 5 + [pl.BlockSpec(memory_space=pl.ANY)] * (4 + 2 * SIDE),
         out_specs=vector,
         scratch_shapes=[
             pltpu.VMEM(own.shape, jnp.bfloat16),
@@ -139,7 +140,7 @@
             pltpu.VMEM((2, CORES) + here_a.shape, jnp.bfloat16),
             pltpu.VMEM((blocks, rows, aux * size), jnp.bfloat16),
             pltpu.VMEM((blocks, rows, size), jnp.float32),
-            pltpu.SemaphoreType.DMA((sources + 5,)),
+            pltpu.SemaphoreType.DMA((sources + 2 * SIDE + 3,)),
         ],
         compiler_params=pltpu.CompilerParams(vmem_limit_bytes=56 << 20),
         cost_estimate=pl.CostEstimate(
@@ -147,7 +148,7 @@
             bytes_accessed=4 * own.size + 8 * here_a.size + 2 * rows * LIVE,
             transcendentals=0,
         ),
-    )(place, pairs, starts, shifts, counts, own, other, here_a, there_a, here_b, there_b)
+    )(place, pairs, starts, shifts, counts, own, other, here_a, here_b, *there_a, *there_b)
 
 
 def finish_kernel(rows_live, starts, shifts, counts, pieces, out_ref, summed):
@@ -196,6 +197,13 @@
     return jnp.stack([value, up, jnp.concatenate(far), down])
 
 
+def last_ring(value, axis):
+    up, down = moved(value, axis, 1), moved(value, axis, SIDE - 1)
+    cut = value.shape[0] // 2
+    far = jnp.concatenate([moved(up[:cut], axis, 1), moved(down[cut:], axis, SIDE - 1)])
+    return jnp.stack([value, up, far, down]), far, (swapped(value), swapped(up), swapped(down))
+
+
 def per_device(three_index, density, pair_blocks, basis_counts):
     aux_here, own_blocks, neigh, size, _ = three_index.shape
     rows_here, basis = density.shape
@@ -217,18 +225,22 @@
     lines = jnp.stack([density] + [moved(density, "x", s) for s in range(1, SIDE)])
     lines = jnp.where(live, lines, 0)
     lines, three_index = lax.optimization_barrier((lines, three_index))
-    here_a = ring(ring(lines[..., : basis // 2], "z"), "y")
-    here_b = ring(ring(lines[..., basis // 2 :], "y"), "z")
+    here_a, far_a, near_a = last_ring(ring(lines[..., : basis // 2], "z"), "y")
+    here_b, far_b, near_b = last_ring(ring(lines[..., basis // 2 :], "y"), "z")
 
     parted = three_index.reshape(SIDE, aux_here // SIDE, own_blocks, neigh, size, size)
     own = lax.all_to_all(parted, "x", 0, 0, tiled=True)
-    own, here_a, here_b = lax.optimization_barrier((own, here_a, here_b))
-    there_a, there_b, other = swapped(here_a), swapped(here_b), swapped(own)
+    own, here_a, here_b, far_a, far_b, near_a, near_b = lax.optimization_barrier(
+        (own, here_a, here_b, far_a, far_b, near_a, near_b)
+    )
+    there_a = (near_a[0], near_a[1], swapped(far_a), near_a[2])
+    there_b = (near_b[0], near_b[1], swapped(far_b), near_b[2])
+    other = swapped(own)
 
     place = jnp.stack([x, core, z, y]).astype(jnp.int32)
     pairs = pair_blocks.reshape(-1)
     partial = exchange_rows(
-        place, pairs, starts, shifts, basis_counts, own, other, here_a, there_a, here_b, there_b
+        place, pairs, starts, shifts, basis_counts, own, other, here_a, here_b, there_a, there_b
     )
     partial = partial.reshape(-1, rows_here, LIVE)
     pieces = lax.all_to_all(partial, ("x", "z", "y"), 0, 0, tiled=True)

time: 160 us -> 155 us (0.969)
  waiting for transfers between devices: 30.4 us -> 24 us
    ppermute x3 -> x9, waiting for transfers between devices: 10.9 us -> 6.5 us  [swapped(): return lax.ppermute(value, 'core', [(0, 1), (1, 0)])]
    another operation x0 -> x4, other arithmetic: none -> 3.42 us  [last_ring(): jnp.stack([value, up, far, down])]
    another operation x8 -> x2, other arithmetic: 2.53 us -> 0.03 us  [ring(): return jnp.stack([value, up, jnp.concatenate(far), down])]
    all_to_all x1, waiting for transfers between devices: 7.43 us -> 4.93 us  [per_device(): own = lax.all_to_all(parted, 'x', 0, 0, tiled=True)]
  transfers between devices with their start and end apart: 23 -> 29, of which waited for: 6 -> 10; matrix products, arithmetic and copies ran while one was open for 4% -> 5% of each run, Pallas kernels for 0% -> 0%
where the time goes in v8:
time: 155 us
  blocking collectives  51.2 us (33%)
  starting transfers between devices  38 us (25%)
  Pallas kernels  32.2 us (21%)
  waiting for transfers between devices  24 us (15%)
  other arithmetic  7.41 us (5%)
  local copies, waits for them, and re-layouts  1.78 us (1%)
    all_to_all x1, blocking collectives, per_device(): pieces = lax.all_to_all(partial, ('x', 'z', 'y'), 0, 0, tiled=True)  51.2 us
    ppermute x19, starting transfers between devices, moved(): lax.ppermute(value, axis, [(k, (k + shift) % SIDE) for k in range(SIDE)])  32 us
    pallas_call x1, Pallas kernels, exchange_rows(): pl.pallas_call(exchange_kernel, out_shape=jax.ShapeDtypeStruct((rows, LIV...  28.4 us
    ppermute x19, waiting for transfers between devices, moved(): lax.ppermute(value, axis, [(k, (k + shift) % SIDE) for k in range(SIDE)])  12.6 us
    ppermute x9, waiting for transfers between devices, swapped(): return lax.ppermute(value, 'core', [(0, 1), (1, 0)])  6.5 us
    all_to_all x1, waiting for transfers between devices, per_device(): own = lax.all_to_all(parted, 'x', 0, 0, tiled=True)  4.93 us
    all_to_all x1, starting transfers between devices, per_device(): own = lax.all_to_all(parted, 'x', 0, 0, tiled=True)  4.85 us
    pallas_call x1, Pallas kernels, finish(): pl.pallas_call(finish_kernel, out_shape=jax.ShapeDtypeStruct((rows, basis...  3.74 us
  transfers between devices with their start and end apart: 29, of which 10 were waited for; matrix products, arithmetic and copies ran while one was open for 5% of the time, Pallas kernels for 0%

profile of v8, /device:TPU:0, one launch (start us, length us, event | category | flops | bytes accessed | tf_op | source)
XLA Modules:
  0.0 154.9 jit_solution(17470436481118376202)
XLA Ops:
  0.0 1.6 %collective-permute-start = (bf16[16,2048]{1,0:T(8,128)(2,1)}, bf16[16,2048]{1,0:T(8,128)(2,1)S(1)}, u32[]{:S(2)}, u32[]{:S(2)}) collective-permute-start(bf16[16,2048]{1,0:T(8,128)(2,1)} %param.5), channel_id=1, source_target_pairs={{0,32},{32,64},{64,96},{96,0},{1,33},{33,65},{65,97},{97,1},{2,34}... | collective-permute-start | bytes 196616 | tf_op jit(solution)/shard_map/ppermute | solution.py:186
  1.6 1.7 %collective-permute-start.2 = (bf16[16,2048]{1,0:T(8,128)(2,1)}, bf16[16,2048]{1,0:T(8,128)(2,1)S(1)}, u32[]{:S(2)}, u32[]{:S(2)}) collective-permute-start(bf16[16,2048]{1,0:T(8,128)(2,1)} %param.5), channel_id=1, source_target_pairs={{0,96},{32,0},{64,32},{96,64},{1,97},{33,1},{65,33},{97,65},{2,98}... | collective-permute-start | bytes 196616 | tf_op jit(solution)/shard_map/ppermute | solution.py:186
  3.2 1.9 %collective-permute-start.1 = (bf16[16,2048]{1,0:T(8,128)(2,1)}, bf16[16,2048]{1,0:T(8,128)(2,1)S(1)}, u32[]{:S(2)}, u32[]{:S(2)}) collective-permute-start(bf16[16,2048]{1,0:T(8,128)(2,1)} %param.5), channel_id=1, source_target_pairs={{0,64},{32,96},{64,0},{96,32},{1,65},{33,97},{65,1},{97,33},{2,66}... | collective-permute-start | bytes 196616 | tf_op jit(solution)/shard_map/ppermute | solution.py:186
  5.1 0.7 fusion
  5.9 0.8 select_reduce_fusion.1
  6.8 2.4 %collective-permute-done.1 = bf16[16,2048]{1,0:T(8,128)(2,1)S(1)} collective-permute-done((bf16[16,2048]{1,0:T(8,128)(2,1)}, bf16[16,2048]{1,0:T(8,128)(2,1)S(1)}, u32[]{:S(2)}, u32[]{:S(2)}) %collective-permute-start.1) | collective-permute-done | bytes 65568 | tf_op jit(solution)/shard_map/ppermute | solution.py:186
  9.2 1.0 and_select_fusion
  10.2 4.9 %all-to-all-start = ((bf16[4,4,2,4,128,128]{5,4,3,2,1,0:T(8,128)(2,1)}), bf16[4,4,2,4,128,128]{5,4,3,2,1,0:T(8,128)(2,1)}, u32[]{:S(2)}, u32[]{:S(2)}) async-start(bf16[4,4,2,4,128,128]{5,4,3,2,1,0:T(8,128)(2,1)} %bitcast.35), calls=%async_computation | async-start | bytes 8388608 | tf_op jit(solution)/shard_map/all_to_all | solution.py:232
  15.1 1.7 %collective-permute-start.11 = (bf16[4,16,1024]{2,1,0:T(8,128)(2,1)S(1)}, bf16[4,16,1024]{2,1,0:T(8,128)(2,1)S(1)}, u32[]{:S(2)}, u32[]{:S(2)}) collective-permute-start(bf16[4,16,1024]{2,1,0:T(8,128)(2,1)S(1)} %get-tuple-element.39), channel_id=1, source_target_pairs={{0,1},{1,2},{2,3},{3,0},{4,5},{5,6},{6,7},{7,4},{8,9},{9,10},{10,1... | collective-permute-start | bytes 393224 | tf_op jit(solution)/shard_map/ppermute | solution.py:186
  16.9 1.6 %collective-permute-start.13 = (bf16[4,16,1024]{2,1,0:T(8,128)(2,1)S(1)}, bf16[4,16,1024]{2,1,0:T(8,128)(2,1)S(1)}, u32[]{:S(2)}, u32[]{:S(2)}) collective-permute-start(bf16[4,16,1024]{2,1,0:T(8,128)(2,1)S(1)} %get-tuple-element.39), channel_id=1, source_target_pairs={{0,3},{1,0},{2,1},{3,2},{4,7},{5,4},{6,5},{7,6},{8,11},{9,8},{10,9... | collective-permute-start | bytes 393224 | tf_op jit(solution)/shard_map/ppermute | solution.py:186
  18.4 2.0 %collective-permute-start.3 = (bf16[4,16,1024]{2,1,0:T(8,128)(2,1)S(1)}, bf16[4,16,1024]{2,1,0:T(8,128)(2,1)S(1)}, u32[]{:S(2)}, u32[]{:S(2)}) collective-permute-start(bf16[4,16,1024]{2,1,0:T(8,128)(2,1)S(1)} %get-tuple-element.40), channel_id=1, source_target_pairs={{0,4},{4,8},{8,12},{12,0},{1,5},{5,9},{9,13},{13,1},{2,6},{6,10},{... | collective-permute-start | bytes 393224 | tf_op jit(solution)/shard_map/ppermute | solution.py:186
  20.4 2.1 %collective-permute-start.5 = (bf16[4,16,1024]{2,1,0:T(8,128)(2,1)S(1)}, bf16[4,16,1024]{2,1,0:T(8,128)(2,1)S(1)}, u32[]{:S(2)}, u32[]{:S(2)}) collective-permute-start(bf16[4,16,1024]{2,1,0:T(8,128)(2,1)S(1)} %get-tuple-element.40), channel_id=1, source_target_pairs={{0,12},{4,0},{8,4},{12,8},{1,13},{5,1},{9,5},{13,9},{2,14},{6,2},{... | collective-permute-start | bytes 393224 | tf_op jit(solution)/shard_map/ppermute | solution.py:186
  22.6 0.4 collective-permute-start.12
  23.0 2.9 %collective-permute-start.14 = (bf16[2,16,1024]{2,1,0:T(8,128)(2,1)S(1)}, bf16[2,16,1024]{2,1,0:T(8,128)(2,1)S(1)}, u32[]{:S(2)}, u32[]{:S(2)}) collective-permute-start(bf16[2,16,1024]{2,1,0:T(8,128)(2,1)S(1)} %slice.49), channel_id=1, source_target_pairs={{0,3},{1,0},{2,1},{3,2},{4,7},{5,4},{6,5},{7,6},{8,11},{9,8},{10,9... | collective-permute-start | bytes 196616 | tf_op jit(solution)/shard_map/ppermute | solution.py:186
  26.0 0.8 collective-permute-start.4
  26.8 2.6 %collective-permute-start.6 = (bf16[2,16,1024]{2,1,0:T(8,128)(2,1)S(1)}, bf16[2,16,1024]{2,1,0:T(8,128)(2,1)S(1)}, u32[]{:S(2)}, u32[]{:S(2)}) collective-permute-start(bf16[2,16,1024]{2,1,0:T(8,128)(2,1)S(1)} %slice.45), channel_id=1, source_target_pairs={{0,12},{4,0},{8,4},{12,8},{1,13},{5,1},{9,5},{13,9},{2,14},{6,2},{... | collective-permute-start | bytes 196616 | tf_op jit(solution)/shard_map/ppermute | solution.py:186
  29.4 0.1 fusion.8
  29.5 0.1 collective-permute-start.15
  29.6 2.7 %collective-permute-done.4 = bf16[2,16,1024]{2,1,0:T(8,128)(2,1)S(1)} collective-permute-done((bf16[2,16,1024]{2,1,0:T(8,128)(2,1)S(1)}, bf16[2,16,1024]{2,1,0:T(8,128)(2,1)S(1)}, u32[]{:S(2)}, u32[]{:S(2)}) %collective-permute-start.4) | collective-permute-done | bytes 65568 | tf_op jit(solution)/shard_map/ppermute | solution.py:186
  32.3 0.1 fusion.9
  32.4 0.1 collective-permute-start.7
  32.5 2.8 %collective-permute-start.17 = (bf16[4,4,16,1024]{3,2,1,0:T(8,128)(2,1)S(1)}, bf16[4,4,16,1024]{3,2,1,0:T(8,128)(2,1)S(1)}, u32[]{:S(2)}, u32[]{:S(2)}) collective-permute-start(bf16[4,4,16,1024]{3,2,1,0:T(8,128)(2,1)S(1)} %get-tuple-element.34), channel_id=1, source_target_pairs={{0,12},{4,0},{8,4},{12,8},{1,13},{5,1},{9,5},{13,9},{2,14},{6,2},{... | collective-permute-start | bytes 1572872 | tf_op jit(solution)/shard_map/ppermute | solution.py:186
  35.3 3.2 %collective-permute-start.9 = (bf16[4,4,16,1024]{3,2,1,0:T(8,128)(2,1)S(1)}, bf16[4,4,16,1024]{3,2,1,0:T(8,128)(2,1)S(1)}, u32[]{:S(2)}, u32[]{:S(2)}) collective-permute-start(bf16[4,4,16,1024]{3,2,1,0:T(8,128)(2,1)S(1)} %get-tuple-element.36), channel_id=1, source_target_pairs={{0,3},{1,0},{2,1},{3,2},{4,7},{5,4},{6,5},{7,6},{8,11},{9,8},{10,9... | collective-permute-start | bytes 1572872 | tf_op jit(solution)/shard_map/ppermute | solution.py:186
  38.4 3.2 %collective-permute-done.15 = bf16[4,4,16,1024]{3,2,1,0:T(8,128)(2,1)S(1)} collective-permute-done((bf16[4,4,16,1024]{3,2,1,0:T(8,128)(2,1)S(1)}, bf16[4,4,16,1024]{3,2,1,0:T(8,128)(2,1)S(1)}, u32[]{:S(2)}, u32[]{:S(2)}) %collective-permute-start.15) | collective-permute-done | bytes 524320 | tf_op jit(solution)/shard_map/ppermute | solution.py:186
  41.6 0.1 collective-permute-start.16
  41.7 1.2 collective-permute-done.7
  43.0 3.2 %collective-permute-start.18 = (bf16[2,4,16,1024]{3,2,1,0:T(8,128)(2,1)S(1)}, bf16[2,4,16,1024]{3,2,1,0:T(8,128)(2,1)S(1)}, u32[]{:S(2)}, u32[]{:S(2)}) collective-permute-start(bf16[2,4,16,1024]{3,2,1,0:T(8,128)(2,1)S(1)} %slice.51), channel_id=1, source_target_pairs={{0,12},{4,0},{8,4},{12,8},{1,13},{5,1},{9,5},{13,9},{2,14},{6,2},{... | collective-permute-start | bytes 786440 | tf_op jit(solution)/shard_map/ppermute | solution.py:186
  46.2 3.2 %collective-permute-start.10 = (bf16[2,4,16,1024]{3,2,1,0:T(8,128)(2,1)S(1)}, bf16[2,4,16,1024]{3,2,1,0:T(8,128)(2,1)S(1)}, u32[]{:S(2)}, u32[]{:S(2)}) collective-permute-start(bf16[2,4,16,1024]{3,2,1,0:T(8,128)(2,1)S(1)} %slice.47), channel_id=1, source_target_pairs={{0,3},{1,0},{2,1},{3,2},{4,7},{5,4},{6,5},{7,6},{8,11},{9,8},{10,9... | collective-permute-start | bytes 786440 | tf_op jit(solution)/shard_map/ppermute | solution.py:186
  49.5 1.1 collective-permute-done.8
  50.6 0.6 collective-permute-start.23
  51.2 0.1 collective-permute-start.21
  51.3 2.0 %collective-permute-done.10 = bf16[2,4,16,1024]{3,2,1,0:T(8,128)(2,1)S(1)} collective-permute-done((bf16[2,4,16,1024]{3,2,1,0:T(8,128)(2,1)S(1)}, bf16[2,4,16,1024]{3,2,1,0:T(8,128)(2,1)S(1)}, u32[]{:S(2)}, u32[]{:S(2)}) %collective-permute-start.10) | collective-permute-done | bytes 262176 | tf_op jit(solution)/shard_map/ppermute | solution.py:186
  53.4 1.7 %pad_maximum_fusion.here_a = bf16[4,4,4,16,1024]{4,3,2,1,0:T(8,128)(2,1)} fusion(bf16[1,4,4,16,1024]{4,3,2,1,0:T(8,128)(2,1)S(1)} %bitcast.39, bf16[1,4,4,16,1024]{4,3,2,1,0:T(8,128)(2,1)S(1)} %bitcast.42, bf16[1,4,4,16,1024]{4,3,2,1,0:T(8,128)(2,1)S(1)} %bitcast.38, bf16[1,4,4,16,1024]{4,3,2,1,0:T(8,128)(2,1)S(1)} %get-tuple-element.35), kind=kLoop, calls=%fused_computation | loop fusion | flops 3145728 | bytes 4194304 | tf_op jit(solution)/shard_map/stack | solution.py:204
  55.0 1.6 %pad_maximum_fusion.1.here_b = bf16[4,4,4,16,1024]{4,3,2,1,0:T(8,128)(2,1)} fusion(bf16[1,4,4,16,1024]{4,3,2,1,0:T(8,128)(2,1)S(1)} %bitcast.40, bf16[1,4,4,16,1024]{4,3,2,1,0:T(8,128)(2,1)S(1)} %bitcast.41, bf16[1,4,4,16,1024]{4,3,2,1,0:T(8,128)(2,1)S(1)} %bitcast.37, bf16[1,4,4,16,1024]{4,3,2,1,0:T(8,128)(2,1)S(1)} %get-tuple-element.33), kind=kLoop, calls=%fused_computation.1 | loop fusion | flops 3145728 | bytes 4194304 | tf_op jit(solution)/shard_map/stack | solution.py:204
  56.7 0.8 copy-done.7
  57.5 4.9 %all-to-all-done.own_hbm = bf16[4,4,2,4,128,128]{5,4,3,2,1,0:T(8,128)(2,1)} async-done(((bf16[4,4,2,4,128,128]{5,4,3,2,1,0:T(8,128)(2,1)}), bf16[4,4,2,4,128,128]{5,4,3,2,1,0:T(8,128)(2,1)}, u32[]{:S(2)}, u32[]{:S(2)}) %all-to-all-start) | async-done | bytes 4194336 | tf_op jit(solution)/shard_map/all_to_all | solution.py:232
  62.4 0.5 collective-permute-start.26
  63.0 0.1 copy.7
  63.0 0.6 reshape.91.pairs
  63.7 0.6 pad_add_fusion.place
  64.3 0.1 select_reduce_fusion
  64.4 0.5 multiply_subtract_fusion
  65.0 5.6 %collective-permute-done.26.refs_2_ = bf16[4,4,16,1024]{3,2,1,0:T(8,128)(2,1)S(1)} collective-permute-done((bf16[4,4,16,1024]{3,2,1,0:T(8,128)(2,1)S(1)}, bf16[4,4,16,1024]{3,2,1,0:T(8,128)(2,1)S(1)}, u32[]{:S(2)}, u32[]{:S(2)}) %collective-permute-start.26) | collective-permute-done | bytes 524320 | tf_op jit(solution)/shard_map/ppermute | solution.py:190
  70.5 0.2 collective-permute-done.27.refs_6_
  70.7 0.7 collective-permute-done.25.other_hbm
  71.5 28.4 %shard_map.46 = bf16[1024,1536]{1,0:T(8,128)(2,1)} custom-call(s32[4]{0:T(128)} %pad_add_fusion.place, s32[64]{0:T(128)} %reshape.91.pairs, s32[16]{0:T(128)} %get-tuple-element.32.starts, s32[16]{0:T(128)} %get-tuple-element.31.shifts, s32[16]{0:T(128)} %counts.3, bf16[4,4,2,4,128,128]{5,4,3,2,1,0:T(8,128)(2,1)} %all-to-all-done.own_hbm, ...), custom_call_target="tpu_custom_call" | custom-call | flops 17179869184 | bytes 19922944 | tf_op jit(solution)/shard_map/pallas_call | solution.py:132
  99.9 51.2 %all_to_all.10.pieces = bf16[64,16,1536]{2,1,0:T(8,128)(2,1)} all-to-all(bf16[64,16,1536]{2,1,0:T(8,128)(2,1)} %bitcast.36), channel_id=1, replica_groups=mesh['x'=4,'core'=2,'z'=4,'y'=4] {'x','z','y'}, dimensions={0} | all-to-all | bytes 6291456 | tf_op jit(solution)/shard_map/all_to_all | solution.py:246
  151.1 3.7 %shard_map.47 = f32[16,2048]{1,0:T(8,128)} custom-call(s32[1]{0:T(128)} %bitcast.51, s32[16]{0:T(128)} %get-tuple-element.32.starts, s32[16]{0:T(128)} %get-tuple-element.31.shifts, s32[16]{0:T(128)} %counts.3, bf16[64,16,1536]{2,1,0:T(8,128)(2,1)} %all_to_all.10.pieces), custom_call_target="tpu_custom_call" | custom-call | tf_op jit(solution)/shard_map/pallas_call | solution.py:176
  (61 shorter events, 0.5 us)
Async XLA Ops:
  0.0 6.8 %collective-permute-start = (bf16[16,2048]{1,0:T(8,128)(2,1)}, bf16[16,2048]{1,0:T(8,128)(2,1)S(1)}, u32[]{:S(2)}, u32[]{:S(2)}) collective-permute-start(bf16[16,2048]{1,0:T(8,128)(2,1)} %param.5), channel_id=1, source_target_pairs={{0,32},{32,64},{64,96},{96,0},{1,33},{33,65},{65,97},{97,1},{2,34}... | collective-permute-start | bytes 196616 | tf_op jit(solution)/shard_map/ppermute | solution.py:186
  1.6 5.3 %collective-permute-start.2 = (bf16[16,2048]{1,0:T(8,128)(2,1)}, bf16[16,2048]{1,0:T(8,128)(2,1)S(1)}, u32[]{:S(2)}, u32[]{:S(2)}) collective-permute-start(bf16[16,2048]{1,0:T(8,128)(2,1)} %param.5), channel_id=1, source_target_pairs={{0,96},{32,0},{64,32},{96,64},{1,97},{33,1},{65,33},{97,65},{2,98}... | collective-permute-start | bytes 196616 | tf_op jit(solution)/shard_map/ppermute | solution.py:186
  3.2 6.0 %collective-permute-start.1 = (bf16[16,2048]{1,0:T(8,128)(2,1)}, bf16[16,2048]{1,0:T(8,128)(2,1)S(1)}, u32[]{:S(2)}, u32[]{:S(2)}) collective-permute-start(bf16[16,2048]{1,0:T(8,128)(2,1)} %param.5), channel_id=1, source_target_pairs={{0,64},{32,96},{64,0},{96,32},{1,65},{33,97},{65,1},{97,33},{2,66}... | collective-permute-start | bytes 196616 | tf_op jit(solution)/shard_map/ppermute | solution.py:186
  6.7 3.5 %copy-start.2 = (s32[4]{0:T(128)}, s32[4]{0:T(128)S(1)}, u32[]{:S(2)}) copy-start(s32[4]{0:T(128)S(1)} %fusion.1) | copy-start | bytes 52
  10.2 52.2 %all-to-all-start = ((bf16[4,4,2,4,128,128]{5,4,3,2,1,0:T(8,128)(2,1)}), bf16[4,4,2,4,128,128]{5,4,3,2,1,0:T(8,128)(2,1)}, u32[]{:S(2)}, u32[]{:S(2)}) async-start(bf16[4,4,2,4,128,128]{5,4,3,2,1,0:T(8,128)(2,1)} %bitcast.35), calls=%async_computation | async-start | bytes 8388608 | tf_op jit(solution)/shard_map/all_to_all | solution.py:232
  15.1 7.4 %collective-permute-start.11 = (bf16[4,16,1024]{2,1,0:T(8,128)(2,1)S(1)}, bf16[4,16,1024]{2,1,0:T(8,128)(2,1)S(1)}, u32[]{:S(2)}, u32[]{:S(2)}) collective-permute-start(bf16[4,16,1024]{2,1,0:T(8,128)(2,1)S(1)} %get-tuple-element.39), channel_id=1, source_target_pairs={{0,1},{1,2},{2,3},{3,0},{4,5},{5,6},{6,7},{7,4},{8,9},{9,10},{10,1... | collective-permute-start | bytes 393224 | tf_op jit(solution)/shard_map/ppermute | solution.py:186
  16.9 6.2 %collective-permute-start.13 = (bf16[4,16,1024]{2,1,0:T(8,128)(2,1)S(1)}, bf16[4,16,1024]{2,1,0:T(8,128)(2,1)S(1)}, u32[]{:S(2)}, u32[]{:S(2)}) collective-permute-start(bf16[4,16,1024]{2,1,0:T(8,128)(2,1)S(1)} %get-tuple-element.39), channel_id=1, source_target_pairs={{0,3},{1,0},{2,1},{3,2},{4,7},{5,4},{6,5},{7,6},{8,11},{9,8},{10,9... | collective-permute-start | bytes 393224 | tf_op jit(solution)/shard_map/ppermute | solution.py:186
  18.4 7.5 %collective-permute-start.3 = (bf16[4,16,1024]{2,1,0:T(8,128)(2,1)S(1)}, bf16[4,16,1024]{2,1,0:T(8,128)(2,1)S(1)}, u32[]{:S(2)}, u32[]{:S(2)}) collective-permute-start(bf16[4,16,1024]{2,1,0:T(8,128)(2,1)S(1)} %get-tuple-element.40), channel_id=1, source_target_pairs={{0,4},{4,8},{8,12},{12,0},{1,5},{5,9},{9,13},{13,1},{2,6},{6,10},{... | collective-permute-start | bytes 393224 | tf_op jit(solution)/shard_map/ppermute | solution.py:186
  20.4 6.3 %collective-permute-start.5 = (bf16[4,16,1024]{2,1,0:T(8,128)(2,1)S(1)}, bf16[4,16,1024]{2,1,0:T(8,128)(2,1)S(1)}, u32[]{:S(2)}, u32[]{:S(2)}) collective-permute-start(bf16[4,16,1024]{2,1,0:T(8,128)(2,1)S(1)} %get-tuple-element.40), channel_id=1, source_target_pairs={{0,12},{4,0},{8,4},{12,8},{1,13},{5,1},{9,5},{13,9},{2,14},{6,2},{... | collective-permute-start | bytes 393224 | tf_op jit(solution)/shard_map/ppermute | solution.py:186
  22.6 6.8 %collective-permute-start.12 = (bf16[2,16,1024]{2,1,0:T(8,128)(2,1)S(1)}, bf16[2,16,1024]{2,1,0:T(8,128)(2,1)S(1)}, u32[]{:S(2)}, u32[]{:S(2)}) collective-permute-start(bf16[2,16,1024]{2,1,0:T(8,128)(2,1)S(1)} %slice.48), channel_id=1, source_target_pairs={{0,1},{1,2},{2,3},{3,0},{4,5},{5,6},{6,7},{7,4},{8,9},{9,10},{10,1... | collective-permute-start | bytes 196616 | tf_op jit(solution)/shard_map/ppermute | solution.py:186
  23.0 6.3 %collective-permute-start.14 = (bf16[2,16,1024]{2,1,0:T(8,128)(2,1)S(1)}, bf16[2,16,1024]{2,1,0:T(8,128)(2,1)S(1)}, u32[]{:S(2)}, u32[]{:S(2)}) collective-permute-start(bf16[2,16,1024]{2,1,0:T(8,128)(2,1)S(1)} %slice.49), channel_id=1, source_target_pairs={{0,3},{1,0},{2,1},{3,2},{4,7},{5,4},{6,5},{7,6},{8,11},{9,8},{10,9... | collective-permute-start | bytes 196616 | tf_op jit(solution)/shard_map/ppermute | solution.py:186
  26.0 6.3 %collective-permute-start.4 = (bf16[2,16,1024]{2,1,0:T(8,128)(2,1)S(1)}, bf16[2,16,1024]{2,1,0:T(8,128)(2,1)S(1)}, u32[]{:S(2)}, u32[]{:S(2)}) collective-permute-start(bf16[2,16,1024]{2,1,0:T(8,128)(2,1)S(1)} %slice.44), channel_id=1, source_target_pairs={{0,4},{4,8},{8,12},{12,0},{1,5},{5,9},{9,13},{13,1},{2,6},{6,10},{... | collective-permute-start | bytes 196616 | tf_op jit(solution)/shard_map/ppermute | solution.py:186
  26.8 5.4 %collective-permute-start.6 = (bf16[2,16,1024]{2,1,0:T(8,128)(2,1)S(1)}, bf16[2,16,1024]{2,1,0:T(8,128)(2,1)S(1)}, u32[]{:S(2)}, u32[]{:S(2)}) collective-permute-start(bf16[2,16,1024]{2,1,0:T(8,128)(2,1)S(1)} %slice.45), channel_id=1, source_target_pairs={{0,12},{4,0},{8,4},{12,8},{1,13},{5,1},{9,5},{13,9},{2,14},{6,2},{... | collective-permute-start | bytes 196616 | tf_op jit(solution)/shard_map/ppermute | solution.py:186
  29.5 12.1 %collective-permute-start.15 = (bf16[4,4,16,1024]{3,2,1,0:T(8,128)(2,1)S(1)}, bf16[4,4,16,1024]{3,2,1,0:T(8,128)(2,1)S(1)}, u32[]{:S(2)}, u32[]{:S(2)}) collective-permute-start(bf16[4,4,16,1024]{3,2,1,0:T(8,128)(2,1)S(1)} %get-tuple-element.34), channel_id=1, source_target_pairs={{0,4},{4,8},{8,12},{12,0},{1,5},{5,9},{9,13},{13,1},{2,6},{6,10},{... | collective-permute-start | bytes 1572872 | tf_op jit(solution)/shard_map/ppermute | solution.py:186
  32.4 10.5 %collective-permute-start.7 = (bf16[4,4,16,1024]{3,2,1,0:T(8,128)(2,1)S(1)}, bf16[4,4,16,1024]{3,2,1,0:T(8,128)(2,1)S(1)}, u32[]{:S(2)}, u32[]{:S(2)}) collective-permute-start(bf16[4,4,16,1024]{3,2,1,0:T(8,128)(2,1)S(1)} %get-tuple-element.36), channel_id=1, source_target_pairs={{0,1},{1,2},{2,3},{3,0},{4,5},{5,6},{6,7},{7,4},{8,9},{9,10},{10,1... | collective-permute-start | bytes 1572872 | tf_op jit(solution)/shard_map/ppermute | solution.py:186
  32.5 10.5 %collective-permute-start.17 = (bf16[4,4,16,1024]{3,2,1,0:T(8,128)(2,1)S(1)}, bf16[4,4,16,1024]{3,2,1,0:T(8,128)(2,1)S(1)}, u32[]{:S(2)}, u32[]{:S(2)}) collective-permute-start(bf16[4,4,16,1024]{3,2,1,0:T(8,128)(2,1)S(1)} %get-tuple-element.34), channel_id=1, source_target_pairs={{0,12},{4,0},{8,4},{12,8},{1,13},{5,1},{9,5},{13,9},{2,14},{6,2},{... | collective-permute-start | bytes 1572872 | tf_op jit(solution)/shard_map/ppermute | solution.py:186
  35.3 10.9 %collective-permute-start.9 = (bf16[4,4,16,1024]{3,2,1,0:T(8,128)(2,1)S(1)}, bf16[4,4,16,1024]{3,2,1,0:T(8,128)(2,1)S(1)}, u32[]{:S(2)}, u32[]{:S(2)}) collective-permute-start(bf16[4,4,16,1024]{3,2,1,0:T(8,128)(2,1)S(1)} %get-tuple-element.36), channel_id=1, source_target_pairs={{0,3},{1,0},{2,1},{3,2},{4,7},{5,4},{6,5},{7,6},{8,11},{9,8},{10,9... | collective-permute-start | bytes 1572872 | tf_op jit(solution)/shard_map/ppermute | solution.py:186
  38.4 12.2 %collective-permute-start.22 = (bf16[4,4,16,1024]{3,2,1,0:T(8,128)(2,1)S(1)}, bf16[4,4,16,1024]{3,2,1,0:T(8,128)(2,1)S(1)}, u32[]{:S(2)}, u32[]{:S(2)}) collective-permute-start(bf16[4,4,16,1024]{3,2,1,0:T(8,128)(2,1)S(1)} %get-tuple-element.34), channel_id=1, source_target_pairs={{0,16},{16,0},{1,17},{17,1},{2,18},{18,2},{3,19},{19,3},{4,20},{20... | collective-permute-start | bytes 1572872 | tf_op jit(solution)/shard_map/ppermute | solution.py:190
  41.6 7.8 %collective-permute-start.16 = (bf16[2,4,16,1024]{3,2,1,0:T(8,128)(2,1)S(1)}, bf16[2,4,16,1024]{3,2,1,0:T(8,128)(2,1)S(1)}, u32[]{:S(2)}, u32[]{:S(2)}) collective-permute-start(bf16[2,4,16,1024]{3,2,1,0:T(8,128)(2,1)S(1)} %slice.50), channel_id=1, source_target_pairs={{0,4},{4,8},{8,12},{12,0},{1,5},{5,9},{9,13},{13,1},{2,6},{6,10},{... | collective-permute-start | bytes 786440 | tf_op jit(solution)/shard_map/ppermute | solution.py:186
  42.9 7.7 %collective-permute-start.8 = (bf16[2,4,16,1024]{3,2,1,0:T(8,128)(2,1)S(1)}, bf16[2,4,16,1024]{3,2,1,0:T(8,128)(2,1)S(1)}, u32[]{:S(2)}, u32[]{:S(2)}) collective-permute-start(bf16[2,4,16,1024]{3,2,1,0:T(8,128)(2,1)S(1)} %slice.46), channel_id=1, source_target_pairs={{0,1},{1,2},{2,3},{3,0},{4,5},{5,6},{6,7},{7,4},{8,9},{9,10},{10,1... | collective-permute-start | bytes 786440 | tf_op jit(solution)/shard_map/ppermute | solution.py:186
  43.0 8.2 %collective-permute-start.18 = (bf16[2,4,16,1024]{3,2,1,0:T(8,128)(2,1)S(1)}, bf16[2,4,16,1024]{3,2,1,0:T(8,128)(2,1)S(1)}, u32[]{:S(2)}, u32[]{:S(2)}) collective-permute-start(bf16[2,4,16,1024]{3,2,1,0:T(8,128)(2,1)S(1)} %slice.51), channel_id=1, source_target_pairs={{0,12},{4,0},{8,4},{12,8},{1,13},{5,1},{9,5},{13,9},{2,14},{6,2},{... | collective-permute-start | bytes 786440 | tf_op jit(solution)/shard_map/ppermute | solution.py:186
  46.2 7.1 %collective-permute-start.10 = (bf16[2,4,16,1024]{3,2,1,0:T(8,128)(2,1)S(1)}, bf16[2,4,16,1024]{3,2,1,0:T(8,128)(2,1)S(1)}, u32[]{:S(2)}, u32[]{:S(2)}) collective-permute-start(bf16[2,4,16,1024]{3,2,1,0:T(8,128)(2,1)S(1)} %slice.47), channel_id=1, source_target_pairs={{0,3},{1,0},{2,1},{3,2},{4,7},{5,4},{6,5},{7,6},{8,11},{9,8},{10,9... | collective-permute-start | bytes 786440 | tf_op jit(solution)/shard_map/ppermute | solution.py:186
  49.4 7.2 %collective-permute-start.19 = (bf16[4,4,16,1024]{3,2,1,0:T(8,128)(2,1)S(1)}, bf16[4,4,16,1024]{3,2,1,0:T(8,128)(2,1)S(1)}, u32[]{:S(2)}, u32[]{:S(2)}) collective-permute-start(bf16[4,4,16,1024]{3,2,1,0:T(8,128)(2,1)S(1)} %get-tuple-element.36), channel_id=1, source_target_pairs={{0,16},{16,0},{1,17},{17,1},{2,18},{18,2},{3,19},{19,3},{4,20},{20... | collective-permute-start | bytes 1572872 | tf_op jit(solution)/shard_map/ppermute | solution.py:190
  50.5 6.1 %collective-permute-start.24 = (bf16[4,4,16,1024]{3,2,1,0:T(8,128)(2,1)S(1)}, bf16[4,4,16,1024]{3,2,1,0:T(8,128)(2,1)S(1)}, u32[]{:S(2)}, u32[]{:S(2)}) collective-permute-start(bf16[4,4,16,1024]{3,2,1,0:T(8,128)(2,1)S(1)} %collective-permute-done.17), channel_id=1, source_target_pairs={{0,16},{16,0},{1,17},{17,1},{2,18},{18,2},{3,19},{19,3},{4,20},{20... | collective-permute-start | bytes 1572872 | tf_op jit(solution)/shard_map/ppermute | solution.py:190
  50.6 4.4 %copy-start.3 = (bf16[4,4,16,1024]{3,2,1,0:T(8,128)(2,1)}, bf16[4,4,16,1024]{3,2,1,0:T(8,128)(2,1)S(1)}, u32[]{:S(2)}) copy-start(bf16[4,4,16,1024]{3,2,1,0:T(8,128)(2,1)S(1)} %collective-permute-done.22.refs_4_) | copy-start | bytes 1572868
  50.6 6.0 %collective-permute-start.23 = (bf16[4,4,16,1024]{3,2,1,0:T(8,128)(2,1)S(1)}, bf16[4,4,16,1024]{3,2,1,0:T(8,128)(2,1)S(1)}, u32[]{:S(2)}, u32[]{:S(2)}) collective-permute-start(bf16[4,4,16,1024]{3,2,1,0:T(8,128)(2,1)S(1)} %collective-permute-done.15), channel_id=1, source_target_pairs={{0,16},{16,0},{1,17},{17,1},{2,18},{18,2},{3,19},{19,3},{4,20},{20... | collective-permute-start | bytes 1572872 | tf_op jit(solution)/shard_map/ppermute | solution.py:190
  51.2 5.5 %collective-permute-start.21 = (bf16[4,4,16,1024]{3,2,1,0:T(8,128)(2,1)S(1)}, bf16[4,4,16,1024]{3,2,1,0:T(8,128)(2,1)S(1)}, u32[]{:S(2)}, u32[]{:S(2)}) collective-permute-start(bf16[4,4,16,1024]{3,2,1,0:T(8,128)(2,1)S(1)} %collective-permute-done.9), channel_id=1, source_target_pairs={{0,16},{16,0},{1,17},{17,1},{2,18},{18,2},{3,19},{19,3},{4,20},{20... | collective-permute-start | bytes 1572872 | tf_op jit(solution)/shard_map/ppermute | solution.py:190
  53.3 4.2 %collective-permute-start.20 = (bf16[4,4,16,1024]{3,2,1,0:T(8,128)(2,1)S(1)}, bf16[4,4,16,1024]{3,2,1,0:T(8,128)(2,1)}, u32[]{:S(2)}, u32[]{:S(2)}) collective-permute-start(bf16[4,4,16,1024]{3,2,1,0:T(8,128)(2,1)S(1)} %collective-permute-done.7), channel_id=1, source_target_pairs={{0,16},{16,0},{1,17},{17,1},{2,18},{18,2},{3,19},{19,3},{4,20},{20... | collective-permute-start | bytes 1572872 | tf_op jit(solution)/shard_map/ppermute | solution.py:190
  55.0 7.9 %copy-start = (s32[16,4]{0,1:T(4,128)S(1)}, s32[16,4]{0,1:T(4,128)}, u32[]{:S(2)}) copy-start(s32[16,4]{0,1:T(4,128)} %param.6) | copy-start | bytes 772
  55.0 9.3 %copy-start.1 = (s32[16]{0:T(128)S(1)}, s32[16]{0:T(128)}, u32[]{:S(2)}) copy-start(s32[16]{0:T(128)} %counts.3) | copy-start | bytes 196
  56.6 14.8 %copy-start.4 = (bf16[4,4,16,1024]{3,2,1,0:T(8,128)(2,1)}, bf16[4,4,16,1024]{3,2,1,0:T(8,128)(2,1)S(1)}, u32[]{:S(2)}) copy-start(bf16[4,4,16,1024]{3,2,1,0:T(8,128)(2,1)S(1)} %collective-permute-done.19.refs_0_) | copy-start | bytes 1572868
  56.6 14.8 %copy-start.5 = (bf16[4,4,16,1024]{3,2,1,0:T(8,128)(2,1)}, bf16[4,4,16,1024]{3,2,1,0:T(8,128)(2,1)S(1)}, u32[]{:S(2)}) copy-start(bf16[4,4,16,1024]{3,2,1,0:T(8,128)(2,1)S(1)} %collective-permute-done.24.refs_7_) | copy-start | bytes 1572868
  56.6 14.8 %copy-start.6 = (bf16[4,4,16,1024]{3,2,1,0:T(8,128)(2,1)}, bf16[4,4,16,1024]{3,2,1,0:T(8,128)(2,1)S(1)}, u32[]{:S(2)}) copy-start(bf16[4,4,16,1024]{3,2,1,0:T(8,128)(2,1)S(1)} %collective-permute-done.23.refs_5_) | copy-start | bytes 1572868
  56.7 0.8 copy-start.7
  62.4 9.0 %collective-permute-start.25 = (bf16[4,4,2,4,128,128]{5,4,3,2,1,0:T(8,128)(2,1)}, bf16[4,4,2,4,128,128]{5,4,3,2,1,0:T(8,128)(2,1)}, u32[]{:S(2)}, u32[]{:S(2)}) collective-permute-start(bf16[4,4,2,4,128,128]{5,4,3,2,1,0:T(8,128)(2,1)} %all-to-all-done.own_hbm), channel_id=1, source_target_pairs={{0,16},{16,0},{1,17},{17,1},{2,18},{18,2},{3,19},{19,3},{4,20},{20... | collective-permute-start | bytes 12582920 | tf_op jit(solution)/shard_map/ppermute | solution.py:190
  62.4 8.1 %collective-permute-start.26 = (bf16[4,4,16,1024]{3,2,1,0:T(8,128)(2,1)S(1)}, bf16[4,4,16,1024]{3,2,1,0:T(8,128)(2,1)S(1)}, u32[]{:S(2)}, u32[]{:S(2)}) collective-permute-start(bf16[4,4,16,1024]{3,2,1,0:T(8,128)(2,1)S(1)} %constant_dynamic-update-slice_fusion), channel_id=1, source_target_pairs={{0,16},{16,0},{1,17},{17,1},{2,18},{18,2},{3,19},{19,3},{4,20},{20... | collective-permute-start | bytes 1572872 | tf_op jit(solution)/shard_map/ppermute | solution.py:190
  63.0 7.8 %collective-permute-start.27 = (bf16[4,4,16,1024]{3,2,1,0:T(8,128)(2,1)S(1)}, bf16[4,4,16,1024]{3,2,1,0:T(8,128)(2,1)}, u32[]{:S(2)}, u32[]{:S(2)}) collective-permute-start(bf16[4,4,16,1024]{3,2,1,0:T(8,128)(2,1)S(1)} %constant_dynamic-update-slice_fusion.2), channel_id=1, source_target_pairs={{0,16},{16,0},{1,17},{17,1},{2,18},{18,2},{3,19},{19,3},{4,20},{20... | collective-permute-start | bytes 1572872 | tf_op jit(solution)/shard_map/ppermute | solution.py:190
  70.5 0.9 copy-start.8

commit v9 on v8

--- a/solution.py
+++ b/solution.py
@@ -22,9 +22,10 @@
     )
 
 
-def exchange_kernel(place, pairs, starts, shifts, counts, own_hbm, other_hbm, here_a, here_b, *refs):
-    there_a, there_b = refs[:SIDE], refs[SIDE : 2 * SIDE]
-    out_ref, own, other, density, halfway, total, sems = refs[2 * SIDE :]
+def exchange_kernel(place, pairs, starts, shifts, counts, own_hbm, other_hbm, *refs):
+    here_a, here_b = refs[:SIDE], refs[SIDE : 2 * SIDE]
+    there_a, there_b = refs[2 * SIDE : 3 * SIDE], refs[3 * SIDE : 4 * SIDE]
+    out_ref, own, other, density, halfway, total, sems = refs[4 * SIDE :]
     sources, aux, per_source, neigh, size, _ = own.shape
     piece, width = density.shape[-2:]
     blocks, rows, _ = halfway.shape
@@ -35,14 +36,15 @@
 
     own_copies = [copy(own_hbm.at[s], own.at[s], s) for s in range(sources)]
     def density_copies(half, here, there, index):
-        copies = [copy(here, density.at[half, 0], index)]
+        copies = []
         for back in range(SIDE):
-            copies.append(copy(there[back], density.at[half, 1, back], index + 1 + back))
+            copies.append(copy(here[back], density.at[half, 0, back], index + back))
+            copies.append(copy(there[back], density.at[half, 1, back], index + SIDE + back))
         return copies
 
     first_copies = density_copies(0, here_a, there_a, sources)
-    next_copies = density_copies(1, here_b, there_b, sources + SIDE + 1)
-    last_copy = copy(other_hbm, other, sources + 2 * SIDE + 2)
+    next_copies = density_copies(1, here_b, there_b, sources + 2 * SIDE)
+    last_copy = copy(other_hbm, other, sources + 4 * SIDE)
     for one in own_copies[:1] + first_copies:
         one.start()
     for one in first_copies:
@@ -125,59 +127,65 @@
 
 def exchange_rows(place, pairs, starts, shifts, counts, own, other, here_a, here_b, there_a, there_b):
     sources, aux, per_source, neigh, size, _ = own.shape
-    width = here_a.shape[-1]
+    width = here_a[0].shape[-1]
     blocks = 2 * width // size
     rows = sources * per_source * size
     scalar, vector = pl.BlockSpec(memory_space=pltpu.SMEM), pl.BlockSpec(memory_space=pltpu.VMEM)
     return pl.pallas_call(
         exchange_kernel,
         out_shape=jax.ShapeDtypeStruct((rows, LIVE), jnp.bfloat16),
-        in_specs=[scalar] * 5 + [pl.BlockSpec(memory_space=pl.ANY)] * (4 + 2 * SIDE),
+        in_specs=[scalar] * 5 + [pl.BlockSpec(memory_space=pl.ANY)] * (2 + 4 * SIDE),
         out_specs=vector,
         scratch_shapes=[
             pltpu.VMEM(own.shape, jnp.bfloat16),
             pltpu.VMEM(own.shape, jnp.bfloat16),
-            pltpu.VMEM((2, CORES) + here_a.shape, jnp.bfloat16),
+            pltpu.VMEM((2, CORES, SIDE) + here_a[0].shape, jnp.bfloat16),
             pltpu.VMEM((blocks, rows, aux * size), jnp.bfloat16),
             pltpu.VMEM((blocks, rows, size), jnp.float32),
-            pltpu.SemaphoreType.DMA((sources + 2 * SIDE + 3,)),
+            pltpu.SemaphoreType.DMA((sources + 4 * SIDE + 1,)),
         ],
         compiler_params=pltpu.CompilerParams(vmem_limit_bytes=56 << 20),
         cost_estimate=pl.CostEstimate(
             flops=4 * rows * aux * neigh * size * blocks * size,
-            bytes_accessed=4 * own.size + 8 * here_a.size + 2 * rows * LIVE,
+            bytes_accessed=4 * own.size + 8 * SIDE * here_a[0].size + 2 * rows * LIVE,
             transcendentals=0,
         ),
-    )(place, pairs, starts, shifts, counts, own, other, here_a, here_b, *there_a, *there_b)
+    )(place, pairs, starts, shifts, counts, own, other, *here_a, *here_b, *there_a, *there_b)
 
 
 def finish_kernel(rows_live, starts, shifts, counts, pieces, out_ref, summed):
+    _, rows, _ = pieces.shape
+    step = pl.program_id(0)
+    part = jnp.sum(pieces[...].astype(jnp.float32), axis=0)
+
+    @pl.when(step == 0)
+    def _():
+        summed[...] = part
+
+    @pl.when(step > 0)
+    def _():
+        summed[...] += part
+
+    @pl.when(step == pl.num_programs(0) - 1)
+    def _():
+        row = lax.broadcasted_iota(jnp.int32, (rows, LANES), 0)
+        lane = lax.broadcasted_iota(jnp.int32, (rows, LANES), 1)
+        for n in range(out_ref.shape[1] // LANES):
+            window = summed[:, pl.ds(pl.multiple_of(starts[n] * LANES, LANES), 2 * LANES)]
+            turned = pltpu.roll(window, lax.rem(2 * LANES - shifts[n], 2 * LANES), axis=1)
+            live = (lane < counts[n]) & (row < rows_live[0])
+            out_ref[:, n * LANES : (n + 1) * LANES] = jnp.where(live, turned[:, :LANES], 0.0)
+
+
+def finish(rows_live, starts, shifts, counts, pieces, basis, steps=8):
     amount, rows, _ = pieces.shape
-    summed[...] = jnp.zeros_like(summed)
-
-    def add(i, carry):
-        part = pieces[pl.ds(i * 8, 8)].astype(jnp.float32)
-        summed[...] += jnp.sum(part, axis=0)
-        return carry
-
-    lax.fori_loop(0, amount // 8, add, 0)
-    row = lax.broadcasted_iota(jnp.int32, (rows, LANES), 0)
-    lane = lax.broadcasted_iota(jnp.int32, (rows, LANES), 1)
-    for n in range(out_ref.shape[1] // LANES):
-        window = summed[:, pl.ds(pl.multiple_of(starts[n] * LANES, LANES), 2 * LANES)]
-        turned = pltpu.roll(window, lax.rem(2 * LANES - shifts[n], 2 * LANES), axis=1)
-        live = (lane < counts[n]) & (row < rows_live[0])
-        out_ref[:, n * LANES : (n + 1) * LANES] = jnp.where(live, turned[:, :LANES], 0.0)
-
-
-def finish(rows_live, starts, shifts, counts, pieces, basis):
-    rows = pieces.shape[1]
-    scalar, vector = pl.BlockSpec(memory_space=pltpu.SMEM), pl.BlockSpec(memory_space=pltpu.VMEM)
     return pl.pallas_call(
         finish_kernel,
         out_shape=jax.ShapeDtypeStruct((rows, basis), jnp.float32),
-        in_specs=[scalar] * 4 + [vector],
-        out_specs=vector,
+        grid=(steps,),
+        in_specs=[pl.BlockSpec(memory_space=pltpu.SMEM)] * 4
+        + [pl.BlockSpec((amount // steps, rows, LIVE), lambda i: (i, 0, 0))],
+        out_specs=pl.BlockSpec((rows, basis), lambda i: (0, 0)),
         scratch_shapes=[pltpu.VMEM((rows, LIVE), jnp.float32)],
     )(rows_live, starts, shifts, counts, pieces)
 
@@ -201,7 +209,8 @@
     up, down = moved(value, axis, 1), moved(value, axis, SIDE - 1)
     cut = value.shape[0] // 2
     far = jnp.concatenate([moved(up[:cut], axis, 1), moved(down[cut:], axis, SIDE - 1)])
-    return jnp.stack([value, up, far, down]), far, (swapped(value), swapped(up), swapped(down))
+    here = (value, up, far, down)
+    return here, tuple(swapped(block) for block in here)
 
 
 def per_device(three_index, density, pair_blocks, basis_counts):
@@ -225,16 +234,12 @@
     lines = jnp.stack([density] + [moved(density, "x", s) for s in range(1, SIDE)])
     lines = jnp.where(live, lines, 0)
     lines, three_index = lax.optimization_barrier((lines, three_index))
-    here_a, far_a, near_a = last_ring(ring(lines[..., : basis // 2], "z"), "y")
-    here_b, far_b, near_b = last_ring(ring(lines[..., basis // 2 :], "y"), "z")
+    here_a, there_a = last_ring(ring(lines[..., : basis // 2], "z"), "y")
+    here_b, there_b = last_ring(ring(lines[..., basis // 2 :], "y"), "z")
 
     parted = three_index.reshape(SIDE, aux_here // SIDE, own_blocks, neigh, size, size)
     own = lax.all_to_all(parted, "x", 0, 0, tiled=True)
-    own, here_a, here_b, far_a, far_b, near_a, near_b = lax.optimization_barrier(
-        (own, here_a, here_b, far_a, far_b, near_a, near_b)
-    )
-    there_a = (near_a[0], near_a[1], swapped(far_a), near_a[2])
-    there_b = (near_b[0], near_b[1], swapped(far_b), near_b[2])
+    own, there_a, there_b = lax.optimization_barrier((own, there_a, there_b))
     other = swapped(own)
 
     place = jnp.stack([x, core, z, y]).astype(jnp.int32)

time: 155 us -> 157 us (1.013)
  waiting for transfers between devices: 24 us -> 30.8 us
  starting transfers between devices: 38 us -> 33.5 us
  other arithmetic: 7.41 us -> 4.15 us
  Pallas kernels: 32.2 us -> 34.6 us
    ppermute x19, waiting for transfers between devices: 12.6 us -> 22.5 us  [moved(): lax.ppermute(value, axis, [(k, (k + shift) % SIDE) for k in range(SIDE)])]
    ppermute x19, starting transfers between devices: 32 us -> 26.9 us  [moved(): lax.ppermute(value, axis, [(k, (k + shift) % SIDE) for k in range(SIDE)])]
    all_to_all x1, waiting for transfers between devices: 4.93 us -> 0.01 us  [per_device(): own = lax.all_to_all(parted, 'x', 0, 0, tiled=True)]
    another operation x4 -> x0, other arithmetic: 3.42 us -> none  [last_ring(): jnp.stack([value, up, far, down])]
    pallas_call x1, Pallas kernels: 3.74 us -> 6.05 us  [finish(): pl.pallas_call(finish_kernel, out_shape=jax.ShapeDtypeStruct((rows, basis...]
    ppermute x9, waiting for transfers between devices: 6.5 us -> 8.34 us  [swapped(): return lax.ppermute(value, 'core', [(0, 1), (1, 0)])]
  transfers between devices with their start and end apart: 29 -> 29, of which waited for: 10 -> 13; matrix products, arithmetic and copies ran while one was open for 5% -> 3% of each run, Pallas kernels for 0% -> 0%
where the time goes in v9:
time: 157 us
  blocking collectives  51.5 us (33%)
  Pallas kernels  34.6 us (22%)
  starting transfers between devices  33.5 us (21%)
  waiting for transfers between devices  30.8 us (20%)
  other arithmetic  4.15 us (3%)
  local copies, waits for them, and re-layouts  1.79 us (1%)
    all_to_all x1, blocking collectives, per_device(): pieces = lax.all_to_all(partial, ('x', 'z', 'y'), 0, 0, tiled=True)  51.5 us
    pallas_call x1, Pallas kernels, exchange_rows(): pl.pallas_call(exchange_kernel, out_shape=jax.ShapeDtypeStruct((rows, LIV...  28.5 us
    ppermute x19, starting transfers between devices, moved(): lax.ppermute(value, axis, [(k, (k + shift) % SIDE) for k in range(SIDE)])  26.9 us
    ppermute x19, waiting for transfers between devices, moved(): lax.ppermute(value, axis, [(k, (k + shift) % SIDE) for k in range(SIDE)])  22.5 us
    ppermute x9, waiting for transfers between devices, swapped(): return lax.ppermute(value, 'core', [(0, 1), (1, 0)])  8.34 us
    pallas_call x1, Pallas kernels, finish(): pl.pallas_call(finish_kernel, out_shape=jax.ShapeDtypeStruct((rows, basis...  6.05 us
    all_to_all x1, starting transfers between devices, per_device(): own = lax.all_to_all(parted, 'x', 0, 0, tiled=True)  4.87 us
  transfers between devices with their start and end apart: 29, of which 13 were waited for; matrix products, arithmetic and copies ran while one was open for 3% of the time, Pallas kernels for 0%

profile of v9, /device:TPU:0, one launch (start us, length us, event | category | flops | bytes accessed | tf_op | source)
XLA Modules:
  0.0 156.7 jit_solution(15497782698230870259)
XLA Ops:
  0.0 1.6 %collective-permute-start = (bf16[16,2048]{1,0:T(8,128)(2,1)}, bf16[16,2048]{1,0:T(8,128)(2,1)S(1)}, u32[]{:S(2)}, u32[]{:S(2)}) collective-permute-start(bf16[16,2048]{1,0:T(8,128)(2,1)} %param.5), channel_id=1, source_target_pairs={{0,32},{32,64},{64,96},{96,0},{1,33},{33,65},{65,97},{97,1},{2,34}... | collective-permute-start | bytes 196616 | tf_op jit(solution)/shard_map/ppermute | solution.py:194
  1.6 1.7 %collective-permute-start.2 = (bf16[16,2048]{1,0:T(8,128)(2,1)}, bf16[16,2048]{1,0:T(8,128)(2,1)S(1)}, u32[]{:S(2)}, u32[]{:S(2)}) collective-permute-start(bf16[16,2048]{1,0:T(8,128)(2,1)} %param.5), channel_id=1, source_target_pairs={{0,96},{32,0},{64,32},{96,64},{1,97},{33,1},{65,33},{97,65},{2,98}... | collective-permute-start | bytes 196616 | tf_op jit(solution)/shard_map/ppermute | solution.py:194
  3.2 1.9 %collective-permute-start.1 = (bf16[16,2048]{1,0:T(8,128)(2,1)}, bf16[16,2048]{1,0:T(8,128)(2,1)S(1)}, u32[]{:S(2)}, u32[]{:S(2)}) collective-permute-start(bf16[16,2048]{1,0:T(8,128)(2,1)} %param.5), channel_id=1, source_target_pairs={{0,64},{32,96},{64,0},{96,32},{1,65},{33,97},{65,1},{97,33},{2,66}... | collective-permute-start | bytes 196616 | tf_op jit(solution)/shard_map/ppermute | solution.py:194
  5.1 0.7 fusion
  5.9 0.8 select_reduce_fusion.1
  6.8 2.4 %collective-permute-done.1 = bf16[16,2048]{1,0:T(8,128)(2,1)S(1)} collective-permute-done((bf16[16,2048]{1,0:T(8,128)(2,1)}, bf16[16,2048]{1,0:T(8,128)(2,1)S(1)}, u32[]{:S(2)}, u32[]{:S(2)}) %collective-permute-start.1) | collective-permute-done | bytes 65568 | tf_op jit(solution)/shard_map/ppermute | solution.py:194
  9.2 1.0 and_select_fusion
  10.2 4.9 %all-to-all-start = ((bf16[4,4,2,4,128,128]{5,4,3,2,1,0:T(8,128)(2,1)}), bf16[4,4,2,4,128,128]{5,4,3,2,1,0:T(8,128)(2,1)}, u32[]{:S(2)}, u32[]{:S(2)}) async-start(bf16[4,4,2,4,128,128]{5,4,3,2,1,0:T(8,128)(2,1)} %bitcast.25), calls=%async_computation | async-start | bytes 8388608 | tf_op jit(solution)/shard_map/all_to_all | solution.py:241
  15.2 2.1 %collective-permute-start.3 = (bf16[4,16,1024]{2,1,0:T(8,128)(2,1)S(1)}, bf16[4,16,1024]{2,1,0:T(8,128)(2,1)S(1)}, u32[]{:S(2)}, u32[]{:S(2)}) collective-permute-start(bf16[4,16,1024]{2,1,0:T(8,128)(2,1)S(1)} %get-tuple-element.32), channel_id=1, source_target_pairs={{0,4},{4,8},{8,12},{12,0},{1,5},{5,9},{9,13},{13,1},{2,6},{6,10},{... | collective-permute-start | bytes 393224 | tf_op jit(solution)/shard_map/ppermute | solution.py:194
  17.3 2.2 %collective-permute-start.5 = (bf16[4,16,1024]{2,1,0:T(8,128)(2,1)S(1)}, bf16[4,16,1024]{2,1,0:T(8,128)(2,1)S(1)}, u32[]{:S(2)}, u32[]{:S(2)}) collective-permute-start(bf16[4,16,1024]{2,1,0:T(8,128)(2,1)S(1)} %get-tuple-element.32), channel_id=1, source_target_pairs={{0,12},{4,0},{8,4},{12,8},{1,13},{5,1},{9,5},{13,9},{2,14},{6,2},{... | collective-permute-start | bytes 393224 | tf_op jit(solution)/shard_map/ppermute | solution.py:194
  19.5 1.6 %collective-permute-start.15 = (bf16[4,16,1024]{2,1,0:T(8,128)(2,1)S(1)}, bf16[4,16,1024]{2,1,0:T(8,128)(2,1)S(1)}, u32[]{:S(2)}, u32[]{:S(2)}) collective-permute-start(bf16[4,16,1024]{2,1,0:T(8,128)(2,1)S(1)} %get-tuple-element.31), channel_id=1, source_target_pairs={{0,1},{1,2},{2,3},{3,0},{4,5},{5,6},{6,7},{7,4},{8,9},{9,10},{10,1... | collective-permute-start | bytes 393224 | tf_op jit(solution)/shard_map/ppermute | solution.py:194
  21.0 1.7 %collective-permute-start.17 = (bf16[4,16,1024]{2,1,0:T(8,128)(2,1)S(1)}, bf16[4,16,1024]{2,1,0:T(8,128)(2,1)S(1)}, u32[]{:S(2)}, u32[]{:S(2)}) collective-permute-start(bf16[4,16,1024]{2,1,0:T(8,128)(2,1)S(1)} %get-tuple-element.31), channel_id=1, source_target_pairs={{0,3},{1,0},{2,1},{3,2},{4,7},{5,4},{6,5},{7,6},{8,11},{9,8},{10,9... | collective-permute-start | bytes 393224 | tf_op jit(solution)/shard_map/ppermute | solution.py:194
  22.7 0.1 collective-permute-start.4
  22.8 3.3 %collective-permute-start.6 = (bf16[2,16,1024]{2,1,0:T(8,128)(2,1)S(1)}, bf16[2,16,1024]{2,1,0:T(8,128)(2,1)S(1)}, u32[]{:S(2)}, u32[]{:S(2)}) collective-permute-start(bf16[2,16,1024]{2,1,0:T(8,128)(2,1)S(1)} %slice.45), channel_id=1, source_target_pairs={{0,12},{4,0},{8,4},{12,8},{1,13},{5,1},{9,5},{13,9},{2,14},{6,2},{... | collective-permute-start | bytes 196616 | tf_op jit(solution)/shard_map/ppermute | solution.py:194
  26.1 1.2 collective-permute-start.16
  27.3 2.2 %collective-permute-start.18 = (bf16[2,16,1024]{2,1,0:T(8,128)(2,1)S(1)}, bf16[2,16,1024]{2,1,0:T(8,128)(2,1)S(1)}, u32[]{:S(2)}, u32[]{:S(2)}) collective-permute-start(bf16[2,16,1024]{2,1,0:T(8,128)(2,1)S(1)} %slice.49), channel_id=1, source_target_pairs={{0,3},{1,0},{2,1},{3,2},{4,7},{5,4},{6,5},{7,6},{8,11},{9,8},{10,9... | collective-permute-start | bytes 196616 | tf_op jit(solution)/shard_map/ppermute | solution.py:194
  29.7 2.7 %collective-permute-done.16 = bf16[2,16,1024]{2,1,0:T(8,128)(2,1)S(1)} collective-permute-done((bf16[2,16,1024]{2,1,0:T(8,128)(2,1)S(1)}, bf16[2,16,1024]{2,1,0:T(8,128)(2,1)S(1)}, u32[]{:S(2)}, u32[]{:S(2)}) %collective-permute-start.16) | collective-permute-done | bytes 65568 | tf_op jit(solution)/shard_map/ppermute | solution.py:194
  32.6 2.9 %collective-permute-start.11 = (bf16[4,4,16,1024]{3,2,1,0:T(8,128)(2,1)S(1)}, bf16[4,4,16,1024]{3,2,1,0:T(8,128)(2,1)S(1)}, u32[]{:S(2)}, u32[]{:S(2)}) collective-permute-start(bf16[4,4,16,1024]{3,2,1,0:T(8,128)(2,1)S(1)} %pad_maximum_fusion.refs_0_), channel_id=1, source_target_pairs={{0,3},{1,0},{2,1},{3,2},{4,7},{5,4},{6,5},{7,6},{8,11},{9,8},{10,9... | collective-permute-start | bytes 1572872 | tf_op jit(solution)/shard_map/ppermute | solution.py:194
  35.5 3.2 %collective-permute-start.23 = (bf16[4,4,16,1024]{3,2,1,0:T(8,128)(2,1)S(1)}, bf16[4,4,16,1024]{3,2,1,0:T(8,128)(2,1)S(1)}, u32[]{:S(2)}, u32[]{:S(2)}) collective-permute-start(bf16[4,4,16,1024]{3,2,1,0:T(8,128)(2,1)S(1)} %pad_maximum_fusion.1.refs_4_), channel_id=1, source_target_pairs={{0,12},{4,0},{8,4},{12,8},{1,13},{5,1},{9,5},{13,9},{2,14},{6,2},{... | collective-permute-start | bytes 1572872 | tf_op jit(solution)/shard_map/ppermute | solution.py:194
  38.6 3.0 %collective-permute-done.8.refs_1_ = bf16[4,4,16,1024]{3,2,1,0:T(8,128)(2,1)S(1)} collective-permute-done((bf16[4,4,16,1024]{3,2,1,0:T(8,128)(2,1)S(1)}, bf16[4,4,16,1024]{3,2,1,0:T(8,128)(2,1)S(1)}, u32[]{:S(2)}, u32[]{:S(2)}) %collective-permute-start.8) | collective-permute-done | bytes 524320 | tf_op jit(solution)/shard_map/ppermute | solution.py:194
  41.7 2.3 %collective-permute-done.20.refs_5_ = bf16[4,4,16,1024]{3,2,1,0:T(8,128)(2,1)S(1)} collective-permute-done((bf16[4,4,16,1024]{3,2,1,0:T(8,128)(2,1)S(1)}, bf16[4,4,16,1024]{3,2,1,0:T(8,128)(2,1)S(1)}, u32[]{:S(2)}, u32[]{:S(2)}) %collective-permute-start.20) | collective-permute-done | bytes 524320 | tf_op jit(solution)/shard_map/ppermute | solution.py:194
  44.1 0.1 collective-permute-start.22
  44.2 0.1 collective-permute-start.7
  44.3 0.5 collective-permute-start.19
  44.8 0.6 collective-permute-done.23.refs_7_
  45.4 4.0 %collective-permute-done.10 = bf16[2,4,16,1024]{3,2,1,0:T(8,128)(2,1)S(1)} collective-permute-done((bf16[2,4,16,1024]{3,2,1,0:T(8,128)(2,1)S(1)}, bf16[2,4,16,1024]{3,2,1,0:T(8,128)(2,1)S(1)}, u32[]{:S(2)}, u32[]{:S(2)}) %collective-permute-start.10) | collective-permute-done | bytes 262176 | tf_op jit(solution)/shard_map/ppermute | solution.py:194
  49.3 0.1 collective-permute-start.12
  49.4 2.3 %collective-permute-done.22 = bf16[2,4,16,1024]{3,2,1,0:T(8,128)(2,1)S(1)} collective-permute-done((bf16[2,4,16,1024]{3,2,1,0:T(8,128)(2,1)S(1)}, bf16[2,4,16,1024]{3,2,1,0:T(8,128)(2,1)S(1)}, u32[]{:S(2)}, u32[]{:S(2)}) %collective-permute-start.22) | collective-permute-done | bytes 262176 | tf_op jit(solution)/shard_map/ppermute | solution.py:194
  51.7 1.1 collective-permute-start.24
  52.8 2.9 %collective-permute-done.12 = bf16[2,4,16,1024]{3,2,1,0:T(8,128)(2,1)S(1)} collective-permute-done((bf16[2,4,16,1024]{3,2,1,0:T(8,128)(2,1)S(1)}, bf16[2,4,16,1024]{3,2,1,0:T(8,128)(2,1)S(1)}, u32[]{:S(2)}, u32[]{:S(2)}) %collective-permute-start.12) | collective-permute-done | bytes 262176 | tf_op jit(solution)/shard_map/ppermute | solution.py:194
  55.7 2.4 %collective-permute-done.24 = bf16[2,4,16,1024]{3,2,1,0:T(8,128)(2,1)S(1)} collective-permute-done((bf16[2,4,16,1024]{3,2,1,0:T(8,128)(2,1)S(1)}, bf16[2,4,16,1024]{3,2,1,0:T(8,128)(2,1)S(1)}, u32[]{:S(2)}, u32[]{:S(2)}) %collective-permute-start.24) | collective-permute-done | bytes 262176 | tf_op jit(solution)/shard_map/ppermute | solution.py:194
  58.2 0.6 collective-permute-start.21
  58.7 0.1 collective-permute-start.13
  58.9 0.4 collective-permute-start.25
  59.3 0.7 collective-permute-done.26.refs_15_
  60.0 0.7 collective-permute-done.21.refs_13_
  60.8 1.5 collective-permute-done.13.refs_10_
  62.3 0.8 copy-done.17
  63.1 0.1 collective-permute-start.27
  63.2 0.1 copy.7
  63.3 0.6 reshape.91.pairs
  64.0 0.6 pad_add_fusion.place
  64.6 0.1 select_reduce_fusion
  64.7 0.6 multiply_subtract_fusion
  65.3 5.3 %collective-permute-done.27.other_hbm = bf16[4,4,2,4,128,128]{5,4,3,2,1,0:T(8,128)(2,1)} collective-permute-done((bf16[4,4,2,4,128,128]{5,4,3,2,1,0:T(8,128)(2,1)}, bf16[4,4,2,4,128,128]{5,4,3,2,1,0:T(8,128)(2,1)}, u32[]{:S(2)}, u32[]{:S(2)}) %collective-permute-start.27) | collective-permute-done | bytes 4194336 | tf_op jit(solution)/shard_map/ppermute | solution.py:198
  70.7 28.5 %shard_map.46 = bf16[1024,1536]{1,0:T(8,128)(2,1)} custom-call(s32[4]{0:T(128)} %pad_add_fusion.place, s32[64]{0:T(128)} %reshape.91.pairs, s32[16]{0:T(128)} %get-tuple-element.28.starts, s32[16]{0:T(128)} %get-tuple-element.27.shifts, s32[16]{0:T(128)} %counts.3, bf16[4,4,2,4,128,128]{5,4,3,2,1,0:T(8,128)(2,1)} %all-to-all-done.own_hbm, ...), custom_call_target="tpu_custom_call" | custom-call | flops 17179869184 | bytes 19922944 | tf_op jit(solution)/shard_map/pallas_call | solution.py:134
  99.2 51.5 %all_to_all.10.pieces = bf16[64,16,1536]{2,1,0:T(8,128)(2,1)} all-to-all(bf16[64,16,1536]{2,1,0:T(8,128)(2,1)} %bitcast.26), channel_id=1, replica_groups=mesh['x'=4,'core'=2,'z'=4,'y'=4] {'x','z','y'}, dimensions={0} | all-to-all | bytes 6291456 | tf_op jit(solution)/shard_map/all_to_all | solution.py:251
  150.7 6.1 %shard_map.47 = f32[16,2048]{1,0:T(8,128)} custom-call(s32[1]{0:T(128)} %bitcast.35, s32[16]{0:T(128)} %get-tuple-element.28.starts, s32[16]{0:T(128)} %get-tuple-element.27.shifts, s32[16]{0:T(128)} %counts.3, bf16[64,16,1536]{2,1,0:T(8,128)(2,1)} %all_to_all.10.pieces), custom_call_target="tpu_custom_call" | custom-call | tf_op jit(solution)/shard_map/pallas_call | solution.py:182
  (77 shorter events, 0.9 us)
Async XLA Ops:
  0.0 6.8 %collective-permute-start = (bf16[16,2048]{1,0:T(8,128)(2,1)}, bf16[16,2048]{1,0:T(8,128)(2,1)S(1)}, u32[]{:S(2)}, u32[]{:S(2)}) collective-permute-start(bf16[16,2048]{1,0:T(8,128)(2,1)} %param.5), channel_id=1, source_target_pairs={{0,32},{32,64},{64,96},{96,0},{1,33},{33,65},{65,97},{97,1},{2,34}... | collective-permute-start | bytes 196616 | tf_op jit(solution)/shard_map/ppermute | solution.py:194
  1.6 5.3 %collective-permute-start.2 = (bf16[16,2048]{1,0:T(8,128)(2,1)}, bf16[16,2048]{1,0:T(8,128)(2,1)S(1)}, u32[]{:S(2)}, u32[]{:S(2)}) collective-permute-start(bf16[16,2048]{1,0:T(8,128)(2,1)} %param.5), channel_id=1, source_target_pairs={{0,96},{32,0},{64,32},{96,64},{1,97},{33,1},{65,33},{97,65},{2,98}... | collective-permute-start | bytes 196616 | tf_op jit(solution)/shard_map/ppermute | solution.py:194
  3.2 6.0 %collective-permute-start.1 = (bf16[16,2048]{1,0:T(8,128)(2,1)}, bf16[16,2048]{1,0:T(8,128)(2,1)S(1)}, u32[]{:S(2)}, u32[]{:S(2)}) collective-permute-start(bf16[16,2048]{1,0:T(8,128)(2,1)} %param.5), channel_id=1, source_target_pairs={{0,64},{32,96},{64,0},{96,32},{1,65},{33,97},{65,1},{97,33},{2,66}... | collective-permute-start | bytes 196616 | tf_op jit(solution)/shard_map/ppermute | solution.py:194
  6.7 3.5 %copy-start.10 = (s32[4]{0:T(128)}, s32[4]{0:T(128)S(1)}, u32[]{:S(2)}) copy-start(s32[4]{0:T(128)S(1)} %fusion.1) | copy-start | bytes 52
  10.2 52.9 %all-to-all-start = ((bf16[4,4,2,4,128,128]{5,4,3,2,1,0:T(8,128)(2,1)}), bf16[4,4,2,4,128,128]{5,4,3,2,1,0:T(8,128)(2,1)}, u32[]{:S(2)}, u32[]{:S(2)}) async-start(bf16[4,4,2,4,128,128]{5,4,3,2,1,0:T(8,128)(2,1)} %bitcast.25), calls=%async_computation | async-start | bytes 8388608 | tf_op jit(solution)/shard_map/all_to_all | solution.py:241
  15.1 48.2 %copy-start.8 = (s32[16,4]{0,1:T(4,128)S(1)}, s32[16,4]{0,1:T(4,128)}, u32[]{:S(2)}) copy-start(s32[16,4]{0,1:T(4,128)} %param.6) | copy-start | bytes 772
  15.1 49.5 %copy-start.9 = (s32[16]{0:T(128)S(1)}, s32[16]{0:T(128)}, u32[]{:S(2)}) copy-start(s32[16]{0:T(128)} %counts.3) | copy-start | bytes 196
  15.2 7.5 %collective-permute-start.3 = (bf16[4,16,1024]{2,1,0:T(8,128)(2,1)S(1)}, bf16[4,16,1024]{2,1,0:T(8,128)(2,1)S(1)}, u32[]{:S(2)}, u32[]{:S(2)}) collective-permute-start(bf16[4,16,1024]{2,1,0:T(8,128)(2,1)S(1)} %get-tuple-element.32), channel_id=1, source_target_pairs={{0,4},{4,8},{8,12},{12,0},{1,5},{5,9},{9,13},{13,1},{2,6},{6,10},{... | collective-permute-start | bytes 393224 | tf_op jit(solution)/shard_map/ppermute | solution.py:194
  17.3 5.5 %collective-permute-start.5 = (bf16[4,16,1024]{2,1,0:T(8,128)(2,1)S(1)}, bf16[4,16,1024]{2,1,0:T(8,128)(2,1)S(1)}, u32[]{:S(2)}, u32[]{:S(2)}) collective-permute-start(bf16[4,16,1024]{2,1,0:T(8,128)(2,1)S(1)} %get-tuple-element.32), channel_id=1, source_target_pairs={{0,12},{4,0},{8,4},{12,8},{1,13},{5,1},{9,5},{13,9},{2,14},{6,2},{... | collective-permute-start | bytes 393224 | tf_op jit(solution)/shard_map/ppermute | solution.py:194
  19.5 6.6 %collective-permute-start.15 = (bf16[4,16,1024]{2,1,0:T(8,128)(2,1)S(1)}, bf16[4,16,1024]{2,1,0:T(8,128)(2,1)S(1)}, u32[]{:S(2)}, u32[]{:S(2)}) collective-permute-start(bf16[4,16,1024]{2,1,0:T(8,128)(2,1)S(1)} %get-tuple-element.31), channel_id=1, source_target_pairs={{0,1},{1,2},{2,3},{3,0},{4,5},{5,6},{6,7},{7,4},{8,9},{9,10},{10,1... | collective-permute-start | bytes 393224 | tf_op jit(solution)/shard_map/ppermute | solution.py:194
  21.0 6.3 %collective-permute-start.17 = (bf16[4,16,1024]{2,1,0:T(8,128)(2,1)S(1)}, bf16[4,16,1024]{2,1,0:T(8,128)(2,1)S(1)}, u32[]{:S(2)}, u32[]{:S(2)}) collective-permute-start(bf16[4,16,1024]{2,1,0:T(8,128)(2,1)S(1)} %get-tuple-element.31), channel_id=1, source_target_pairs={{0,3},{1,0},{2,1},{3,2},{4,7},{5,4},{6,5},{7,6},{8,11},{9,8},{10,9... | collective-permute-start | bytes 393224 | tf_op jit(solution)/shard_map/ppermute | solution.py:194
  22.7 6.8 %collective-permute-start.4 = (bf16[2,16,1024]{2,1,0:T(8,128)(2,1)S(1)}, bf16[2,16,1024]{2,1,0:T(8,128)(2,1)S(1)}, u32[]{:S(2)}, u32[]{:S(2)}) collective-permute-start(bf16[2,16,1024]{2,1,0:T(8,128)(2,1)S(1)} %slice.44), channel_id=1, source_target_pairs={{0,4},{4,8},{8,12},{12,0},{1,5},{5,9},{9,13},{13,1},{2,6},{6,10},{... | collective-permute-start | bytes 196616 | tf_op jit(solution)/shard_map/ppermute | solution.py:194
  22.8 6.7 %collective-permute-start.6 = (bf16[2,16,1024]{2,1,0:T(8,128)(2,1)S(1)}, bf16[2,16,1024]{2,1,0:T(8,128)(2,1)S(1)}, u32[]{:S(2)}, u32[]{:S(2)}) collective-permute-start(bf16[2,16,1024]{2,1,0:T(8,128)(2,1)S(1)} %slice.45), channel_id=1, source_target_pairs={{0,12},{4,0},{8,4},{12,8},{1,13},{5,1},{9,5},{13,9},{2,14},{6,2},{... | collective-permute-start | bytes 196616 | tf_op jit(solution)/shard_map/ppermute | solution.py:194
  26.1 6.3 %collective-permute-start.16 = (bf16[2,16,1024]{2,1,0:T(8,128)(2,1)S(1)}, bf16[2,16,1024]{2,1,0:T(8,128)(2,1)S(1)}, u32[]{:S(2)}, u32[]{:S(2)}) collective-permute-start(bf16[2,16,1024]{2,1,0:T(8,128)(2,1)S(1)} %slice.48), channel_id=1, source_target_pairs={{0,1},{1,2},{2,3},{3,0},{4,5},{5,6},{6,7},{7,4},{8,9},{9,10},{10,1... | collective-permute-start | bytes 196616 | tf_op jit(solution)/shard_map/ppermute | solution.py:194
  27.3 5.1 %collective-permute-start.18 = (bf16[2,16,1024]{2,1,0:T(8,128)(2,1)S(1)}, bf16[2,16,1024]{2,1,0:T(8,128)(2,1)S(1)}, u32[]{:S(2)}, u32[]{:S(2)}) collective-permute-start(bf16[2,16,1024]{2,1,0:T(8,128)(2,1)S(1)} %slice.49), channel_id=1, source_target_pairs={{0,3},{1,0},{2,1},{3,2},{4,7},{5,4},{6,5},{7,6},{8,11},{9,8},{10,9... | collective-permute-start | bytes 196616 | tf_op jit(solution)/shard_map/ppermute | solution.py:194
  29.6 41.0 %copy-start = (bf16[4,4,16,1024]{3,2,1,0:T(8,128)(2,1)}, bf16[4,4,16,1024]{3,2,1,0:T(8,128)(2,1)S(1)}, u32[]{:S(2)}) copy-start(bf16[4,4,16,1024]{3,2,1,0:T(8,128)(2,1)S(1)} %pad_maximum_fusion.refs_0_) | copy-start | bytes 1572868
  29.6 12.0 %collective-permute-start.8 = (bf16[4,4,16,1024]{3,2,1,0:T(8,128)(2,1)S(1)}, bf16[4,4,16,1024]{3,2,1,0:T(8,128)(2,1)S(1)}, u32[]{:S(2)}, u32[]{:S(2)}) collective-permute-start(bf16[4,4,16,1024]{3,2,1,0:T(8,128)(2,1)S(1)} %pad_maximum_fusion.refs_0_), channel_id=1, source_target_pairs={{0,1},{1,2},{2,3},{3,0},{4,5},{5,6},{6,7},{7,4},{8,9},{9,10},{10,1... | collective-permute-start | bytes 1572872 | tf_op jit(solution)/shard_map/ppermute | solution.py:194
  32.5 38.1 %copy-start.1 = (bf16[4,4,16,1024]{3,2,1,0:T(8,128)(2,1)}, bf16[4,4,16,1024]{3,2,1,0:T(8,128)(2,1)S(1)}, u32[]{:S(2)}) copy-start(bf16[4,4,16,1024]{3,2,1,0:T(8,128)(2,1)S(1)} %pad_maximum_fusion.1.refs_4_) | copy-start | bytes 1572868
  32.5 11.6 %collective-permute-start.20 = (bf16[4,4,16,1024]{3,2,1,0:T(8,128)(2,1)S(1)}, bf16[4,4,16,1024]{3,2,1,0:T(8,128)(2,1)S(1)}, u32[]{:S(2)}, u32[]{:S(2)}) collective-permute-start(bf16[4,4,16,1024]{3,2,1,0:T(8,128)(2,1)S(1)} %pad_maximum_fusion.1.refs_4_), channel_id=1, source_target_pairs={{0,4},{4,8},{8,12},{12,0},{1,5},{5,9},{9,13},{13,1},{2,6},{6,10},{... | collective-permute-start | bytes 1572872 | tf_op jit(solution)/shard_map/ppermute | solution.py:194
  32.6 11.7 %collective-permute-start.11 = (bf16[4,4,16,1024]{3,2,1,0:T(8,128)(2,1)S(1)}, bf16[4,4,16,1024]{3,2,1,0:T(8,128)(2,1)S(1)}, u32[]{:S(2)}, u32[]{:S(2)}) collective-permute-start(bf16[4,4,16,1024]{3,2,1,0:T(8,128)(2,1)S(1)} %pad_maximum_fusion.refs_0_), channel_id=1, source_target_pairs={{0,3},{1,0},{2,1},{3,2},{4,7},{5,4},{6,5},{7,6},{8,11},{9,8},{10,9... | collective-permute-start | bytes 1572872 | tf_op jit(solution)/shard_map/ppermute | solution.py:194
  35.5 9.9 %collective-permute-start.23 = (bf16[4,4,16,1024]{3,2,1,0:T(8,128)(2,1)S(1)}, bf16[4,4,16,1024]{3,2,1,0:T(8,128)(2,1)S(1)}, u32[]{:S(2)}, u32[]{:S(2)}) collective-permute-start(bf16[4,4,16,1024]{3,2,1,0:T(8,128)(2,1)S(1)} %pad_maximum_fusion.1.refs_4_), channel_id=1, source_target_pairs={{0,12},{4,0},{8,4},{12,8},{1,13},{5,1},{9,5},{13,9},{2,14},{6,2},{... | collective-permute-start | bytes 1572872 | tf_op jit(solution)/shard_map/ppermute | solution.py:194
  41.6 29.0 %copy-start.2 = (bf16[4,4,16,1024]{3,2,1,0:T(8,128)(2,1)}, bf16[4,4,16,1024]{3,2,1,0:T(8,128)(2,1)S(1)}, u32[]{:S(2)}) copy-start(bf16[4,4,16,1024]{3,2,1,0:T(8,128)(2,1)S(1)} %collective-permute-done.8.refs_1_) | copy-start | bytes 1572868
  41.7 7.7 %collective-permute-start.10 = (bf16[2,4,16,1024]{3,2,1,0:T(8,128)(2,1)S(1)}, bf16[2,4,16,1024]{3,2,1,0:T(8,128)(2,1)S(1)}, u32[]{:S(2)}, u32[]{:S(2)}) collective-permute-start(bf16[2,4,16,1024]{3,2,1,0:T(8,128)(2,1)S(1)} %slice.46), channel_id=1, source_target_pairs={{0,1},{1,2},{2,3},{3,0},{4,5},{5,6},{6,7},{7,4},{8,9},{9,10},{10,1... | collective-permute-start | bytes 786440 | tf_op jit(solution)/shard_map/ppermute | solution.py:194
  44.0 26.6 %copy-start.3 = (bf16[4,4,16,1024]{3,2,1,0:T(8,128)(2,1)}, bf16[4,4,16,1024]{3,2,1,0:T(8,128)(2,1)S(1)}, u32[]{:S(2)}) copy-start(bf16[4,4,16,1024]{3,2,1,0:T(8,128)(2,1)S(1)} %collective-permute-done.20.refs_5_) | copy-start | bytes 1572868
  44.1 7.7 %collective-permute-start.22 = (bf16[2,4,16,1024]{3,2,1,0:T(8,128)(2,1)S(1)}, bf16[2,4,16,1024]{3,2,1,0:T(8,128)(2,1)S(1)}, u32[]{:S(2)}, u32[]{:S(2)}) collective-permute-start(bf16[2,4,16,1024]{3,2,1,0:T(8,128)(2,1)S(1)} %slice.50), channel_id=1, source_target_pairs={{0,4},{4,8},{8,12},{12,0},{1,5},{5,9},{9,13},{13,1},{2,6},{6,10},{... | collective-permute-start | bytes 786440 | tf_op jit(solution)/shard_map/ppermute | solution.py:194
  44.2 14.0 %collective-permute-start.7 = (bf16[4,4,16,1024]{3,2,1,0:T(8,128)(2,1)S(1)}, bf16[4,4,16,1024]{3,2,1,0:T(8,128)(2,1)S(1)}, u32[]{:S(2)}, u32[]{:S(2)}) collective-permute-start(bf16[4,4,16,1024]{3,2,1,0:T(8,128)(2,1)S(1)} %pad_maximum_fusion.refs_0_), channel_id=1, source_target_pairs={{0,16},{16,0},{1,17},{17,1},{2,18},{18,2},{3,19},{19,3},{4,20},{20... | collective-permute-start | bytes 1572872 | tf_op jit(solution)/shard_map/ppermute | solution.py:198
  44.3 26.4 %copy-start.4 = (bf16[4,4,16,1024]{3,2,1,0:T(8,128)(2,1)}, bf16[4,4,16,1024]{3,2,1,0:T(8,128)(2,1)S(1)}, u32[]{:S(2)}) copy-start(bf16[4,4,16,1024]{3,2,1,0:T(8,128)(2,1)S(1)} %collective-permute-done.11.refs_3_) | copy-start | bytes 1572868
  44.3 14.5 %collective-permute-start.19 = (bf16[4,4,16,1024]{3,2,1,0:T(8,128)(2,1)S(1)}, bf16[4,4,16,1024]{3,2,1,0:T(8,128)(2,1)S(1)}, u32[]{:S(2)}, u32[]{:S(2)}) collective-permute-start(bf16[4,4,16,1024]{3,2,1,0:T(8,128)(2,1)S(1)} %pad_maximum_fusion.1.refs_4_), channel_id=1, source_target_pairs={{0,16},{16,0},{1,17},{17,1},{2,18},{18,2},{3,19},{19,3},{4,20},{20... | collective-permute-start | bytes 1572872 | tf_op jit(solution)/shard_map/ppermute | solution.py:198
  45.3 25.3 %copy-start.5 = (bf16[4,4,16,1024]{3,2,1,0:T(8,128)(2,1)}, bf16[4,4,16,1024]{3,2,1,0:T(8,128)(2,1)S(1)}, u32[]{:S(2)}) copy-start(bf16[4,4,16,1024]{3,2,1,0:T(8,128)(2,1)S(1)} %collective-permute-done.23.refs_7_) | copy-start | bytes 1572868
  45.3 13.5 %collective-permute-start.14 = (bf16[4,4,16,1024]{3,2,1,0:T(8,128)(2,1)S(1)}, bf16[4,4,16,1024]{3,2,1,0:T(8,128)(2,1)S(1)}, u32[]{:S(2)}, u32[]{:S(2)}) collective-permute-start(bf16[4,4,16,1024]{3,2,1,0:T(8,128)(2,1)S(1)} %collective-permute-done.11.refs_3_), channel_id=1, source_target_pairs={{0,16},{16,0},{1,17},{17,1},{2,18},{18,2},{3,19},{19,3},{4,20},{20... | collective-permute-start | bytes 1572872 | tf_op jit(solution)/shard_map/ppermute | solution.py:198
  49.3 6.4 %collective-permute-start.12 = (bf16[2,4,16,1024]{3,2,1,0:T(8,128)(2,1)S(1)}, bf16[2,4,16,1024]{3,2,1,0:T(8,128)(2,1)S(1)}, u32[]{:S(2)}, u32[]{:S(2)}) collective-permute-start(bf16[2,4,16,1024]{3,2,1,0:T(8,128)(2,1)S(1)} %slice.47), channel_id=1, source_target_pairs={{0,3},{1,0},{2,1},{3,2},{4,7},{5,4},{6,5},{7,6},{8,11},{9,8},{10,9... | collective-permute-start | bytes 786440 | tf_op jit(solution)/shard_map/ppermute | solution.py:194
  51.7 6.4 %collective-permute-start.24 = (bf16[2,4,16,1024]{3,2,1,0:T(8,128)(2,1)S(1)}, bf16[2,4,16,1024]{3,2,1,0:T(8,128)(2,1)S(1)}, u32[]{:S(2)}, u32[]{:S(2)}) collective-permute-start(bf16[2,4,16,1024]{3,2,1,0:T(8,128)(2,1)S(1)} %slice.51), channel_id=1, source_target_pairs={{0,12},{4,0},{8,4},{12,8},{1,13},{5,1},{9,5},{13,9},{2,14},{6,2},{... | collective-permute-start | bytes 786440 | tf_op jit(solution)/shard_map/ppermute | solution.py:194
  55.7 3.6 %collective-permute-start.9 = (bf16[4,4,16,1024]{3,2,1,0:T(8,128)(2,1)S(1)}, bf16[4,4,16,1024]{3,2,1,0:T(8,128)(2,1)S(1)}, u32[]{:S(2)}, u32[]{:S(2)}) collective-permute-start(bf16[4,4,16,1024]{3,2,1,0:T(8,128)(2,1)S(1)} %collective-permute-done.8.refs_1_), channel_id=1, source_target_pairs={{0,16},{16,0},{1,17},{17,1},{2,18},{18,2},{3,19},{19,3},{4,20},{20... | collective-permute-start | bytes 1572872 | tf_op jit(solution)/shard_map/ppermute | solution.py:198
  55.7 6.5 %copy-start.7 = (bf16[4,4,16,1024]{3,2,1,0:T(8,128)(2,1)}, bf16[4,4,16,1024]{3,2,1,0:T(8,128)(2,1)S(1)}, u32[]{:S(2)}) copy-start(bf16[4,4,16,1024]{3,2,1,0:T(8,128)(2,1)S(1)} %constant_dynamic-update-slice_fusion.refs_2_) | copy-start | bytes 1572868
  58.1 1.9 %collective-permute-start.26 = (bf16[4,4,16,1024]{3,2,1,0:T(8,128)(2,1)S(1)}, bf16[4,4,16,1024]{3,2,1,0:T(8,128)(2,1)S(1)}, u32[]{:S(2)}, u32[]{:S(2)}) collective-permute-start(bf16[4,4,16,1024]{3,2,1,0:T(8,128)(2,1)S(1)} %collective-permute-done.23.refs_7_), channel_id=1, source_target_pairs={{0,16},{16,0},{1,17},{17,1},{2,18},{18,2},{3,19},{19,3},{4,20},{20... | collective-permute-start | bytes 1572872 | tf_op jit(solution)/shard_map/ppermute | solution.py:198
  58.1 2.6 %copy-start.6 = (bf16[4,4,16,1024]{3,2,1,0:T(8,128)(2,1)}, bf16[4,4,16,1024]{3,2,1,0:T(8,128)(2,1)S(1)}, u32[]{:S(2)}) copy-start(bf16[4,4,16,1024]{3,2,1,0:T(8,128)(2,1)S(1)} %constant_dynamic-update-slice_fusion.2.refs_6_) | copy-start | bytes 1572868
  58.1 4.1 %copy-start.11 = (bf16[4,4,16,1024]{3,2,1,0:T(8,128)(2,1)}, bf16[4,4,16,1024]{3,2,1,0:T(8,128)(2,1)S(1)}, u32[]{:S(2)}) copy-start(bf16[4,4,16,1024]{3,2,1,0:T(8,128)(2,1)S(1)} %collective-permute-done.7.refs_8_) | copy-start | bytes 1572868
  58.2 2.6 %collective-permute-start.21 = (bf16[4,4,16,1024]{3,2,1,0:T(8,128)(2,1)S(1)}, bf16[4,4,16,1024]{3,2,1,0:T(8,128)(2,1)S(1)}, u32[]{:S(2)}, u32[]{:S(2)}) collective-permute-start(bf16[4,4,16,1024]{3,2,1,0:T(8,128)(2,1)S(1)} %collective-permute-done.20.refs_5_), channel_id=1, source_target_pairs={{0,16},{16,0},{1,17},{17,1},{2,18},{18,2},{3,19},{19,3},{4,20},{20... | collective-permute-start | bytes 1572872 | tf_op jit(solution)/shard_map/ppermute | solution.py:198
  58.7 3.5 %copy-start.12 = (bf16[4,4,16,1024]{3,2,1,0:T(8,128)(2,1)}, bf16[4,4,16,1024]{3,2,1,0:T(8,128)(2,1)S(1)}, u32[]{:S(2)}) copy-start(bf16[4,4,16,1024]{3,2,1,0:T(8,128)(2,1)S(1)} %collective-permute-done.19.refs_12_) | copy-start | bytes 1572868
  58.7 3.5 %collective-permute-start.13 = (bf16[4,4,16,1024]{3,2,1,0:T(8,128)(2,1)S(1)}, bf16[4,4,16,1024]{3,2,1,0:T(8,128)(2,1)S(1)}, u32[]{:S(2)}, u32[]{:S(2)}) collective-permute-start(bf16[4,4,16,1024]{3,2,1,0:T(8,128)(2,1)S(1)} %constant_dynamic-update-slice_fusion.refs_2_), channel_id=1, source_target_pairs={{0,16},{16,0},{1,17},{17,1},{2,18},{18,2},{3,19},{19,3},{4,20},{20... | collective-permute-start | bytes 1572872 | tf_op jit(solution)/shard_map/ppermute | solution.py:198
  58.9 3.4 %copy-start.13 = (bf16[4,4,16,1024]{3,2,1,0:T(8,128)(2,1)}, bf16[4,4,16,1024]{3,2,1,0:T(8,128)(2,1)S(1)}, u32[]{:S(2)}) copy-start(bf16[4,4,16,1024]{3,2,1,0:T(8,128)(2,1)S(1)} %collective-permute-done.14.refs_11_) | copy-start | bytes 1572868
  58.9 4.2 %collective-permute-start.25 = (bf16[4,4,16,1024]{3,2,1,0:T(8,128)(2,1)S(1)}, bf16[4,4,16,1024]{3,2,1,0:T(8,128)(2,1)}, u32[]{:S(2)}, u32[]{:S(2)}) collective-permute-start(bf16[4,4,16,1024]{3,2,1,0:T(8,128)(2,1)S(1)} %constant_dynamic-update-slice_fusion.2.refs_6_), channel_id=1, source_target_pairs={{0,16},{16,0},{1,17},{17,1},{2,18},{18,2},{3,19},{19,3},{4,20},{20... | collective-permute-start | bytes 1572872 | tf_op jit(solution)/shard_map/ppermute | solution.py:198
  59.3 3.0 %copy-start.14 = (bf16[4,4,16,1024]{3,2,1,0:T(8,128)(2,1)}, bf16[4,4,16,1024]{3,2,1,0:T(8,128)(2,1)S(1)}, u32[]{:S(2)}) copy-start(bf16[4,4,16,1024]{3,2,1,0:T(8,128)(2,1)S(1)} %collective-permute-done.9.refs_9_) | copy-start | bytes 1572868
  60.0 2.3 %copy-start.15 = (bf16[4,4,16,1024]{3,2,1,0:T(8,128)(2,1)}, bf16[4,4,16,1024]{3,2,1,0:T(8,128)(2,1)S(1)}, u32[]{:S(2)}) copy-start(bf16[4,4,16,1024]{3,2,1,0:T(8,128)(2,1)S(1)} %collective-permute-done.26.refs_15_) | copy-start | bytes 1572868
  60.8 1.5 copy-start.16
  62.3 0.8 copy-start.17
  63.1 7.5 %collective-permute-start.27 = (bf16[4,4,2,4,128,128]{5,4,3,2,1,0:T(8,128)(2,1)}, bf16[4,4,2,4,128,128]{5,4,3,2,1,0:T(8,128)(2,1)}, u32[]{:S(2)}, u32[]{:S(2)}) collective-permute-start(bf16[4,4,2,4,128,128]{5,4,3,2,1,0:T(8,128)(2,1)} %all-to-all-done.own_hbm), channel_id=1, source_target_pairs={{0,16},{16,0},{1,17},{17,1},{2,18},{18,2},{3,19},{19,3},{4,20},{20... | collective-permute-start | bytes 12582920 | tf_op jit(solution)/shard_map/ppermute | solution.py:198
